TPU v7x, 512 devices: a whole 4x4x16 slice. The times are simulated.
512 devices in a mesh: depth: 16 (over z), rows: 32 (over y, x, core).
Axes of the slice: x: 4, y: 4, z: 16, core: 2. Of those that a mesh axis runs over, the one named last changes fastest.
Arguments:
- node_feat: bfloat16 [512, 32768], P('depth', 'rows'), may hold values from -6 to 6
- grad_out: bfloat16 [512, 32768], P('depth', 'rows'), may hold values from -0.25 to 0.25
- adjacency: bfloat16 [512, 256, 256], P('rows'), may hold values from -0.1875 to 0.1875
- tile_count: int32 [32], replicated, may hold values from 4 to 16, as said below
- tile_row: int32 [32, 16], replicated, may hold values from 0 to 3, as said below
- tile_col: int32 [32, 16], replicated, may hold values from 0 to 127, as said below
Outputs:
- weight_grad: float32 [32, 16, 256, 256], P('rows', 'depth')
Inputs may be any that keep to these rules, and one draw needn't show every extreme that they name: `tile_count`: the number of live slots of each owner; one owner has exactly 16 in every draw. `tile_row`: 0 in dead slots. `tile_col`: 0 in dead slots. An owner's live slots name distinct column tiles; at most 2 of them lie among the node tiles of any one owner (column tile // 4), and every owner has exactly 2 from some owner.
All inputs are finite; a program needn't handle non-finite values.
Results may differ from a plain program's by a relative error of at most 0.0029.
Values may be sent and summed in bfloat16 or wider, within the bound.
No kernel may reach another device: no remote copies, remote signals or barrier semaphores. Data moves between devices by JAX's collectives and lax.ppermute only.
A program may use at most 64 MiB of HBM per device.

v0:
```python
import jax
import jax.numpy as jnp
from jax import lax
from jax.sharding import PartitionSpec as P

PAIR_MOST = 2


top_precision = lax.Precision.HIGHEST


def slot_tables(tile_row, tile_col, tile_count, row_tiles, pair_most, own_index):
    slot_count = tile_col.shape[1]
    slot_ids = jnp.arange(slot_count, dtype=jnp.int32)
    is_live = slot_ids[None, :] < tile_count[:, None]
    owners = tile_col // row_tiles
    earlier = slot_ids[:, None] > slot_ids[None, :]
    same_owner = (
        (owners[:, :, None] == owners[:, None, :]) & is_live[:, None, :] & earlier[None, :, :]
    )
    rank_of = jnp.sum(same_owner.astype(jnp.int32), axis=2)
    buffer_pos = owners * pair_most + rank_of
    wanted = is_live & (owners == own_index)
    rank_ids = jnp.arange(pair_most, dtype=jnp.int32)
    matched = wanted[:, :, None] & (rank_of[:, :, None] == rank_ids[None, None, :])
    local_tile = jnp.sum(jnp.where(matched, (tile_col % row_tiles)[:, :, None], 0), axis=1).reshape(
        -1
    )
    send_valid = jnp.any(matched, axis=1).reshape(-1)
    my_pos = jnp.take(buffer_pos, own_index, axis=0)
    my_live = jnp.take(is_live, own_index, axis=0)
    my_row = jnp.take(tile_row, own_index, axis=0)
    return (my_pos, my_live, my_row, local_tile, send_valid)


def pick_tiles(source, indices, keep):
    picked = jnp.take(source, indices, axis=1)
    return jnp.where(keep[None, :, None], picked, jnp.zeros((), source.dtype))


def body(node_feat, grad_out, adjacency, tile_count, tile_row, tile_col):
    tile_width = adjacency.shape[1]
    feat_part = node_feat.shape[0]
    row_tiles = node_feat.shape[1] // tile_width
    pair_most = PAIR_MOST
    peer_count = lax.axis_size("rows")
    own_index = lax.axis_index("rows")
    my_pos, my_live, my_row, local_tile, send_valid = slot_tables(
        tile_row, tile_col, tile_count, row_tiles, pair_most, own_index
    )
    buffer_len = peer_count * pair_most
    feat_tiles = node_feat.reshape(feat_part, row_tiles, tile_width)
    grad_tiles = grad_out.reshape(feat_part, row_tiles, tile_width)
    outgoing = pick_tiles(feat_tiles, local_tile, send_valid)
    incoming = lax.all_to_all(outgoing, "rows", split_axis=1, concat_axis=1, tiled=True)
    x_cols = pick_tiles(incoming, my_pos, my_live)
    dy_rows = jnp.take(grad_tiles, my_row, axis=1)
    g_terms = jnp.einsum("fsa,sab->fsb", dy_rows, adjacency, preferred_element_type=jnp.float32)
    placing = (
        (my_pos[:, None] == jnp.arange(buffer_len, dtype=jnp.int32)[None, :]) & my_live[:, None]
    ).astype(jnp.float32)
    g_outgoing = jnp.einsum("fsb,sp->fpb", g_terms, placing, precision=top_precision)
    g_incoming = lax.all_to_all(g_outgoing, "rows", split_axis=1, concat_axis=1, tiled=True)
    tile_ids = jnp.arange(row_tiles, dtype=jnp.int32)
    col_onehot = ((local_tile[:, None] == tile_ids[None, :]) & send_valid[:, None]).astype(
        jnp.float32
    )
    summed_g = jnp.einsum("fpb,pr->frb", g_incoming, col_onehot, precision=top_precision).astype(
        jnp.bfloat16
    )
    h_terms = jnp.einsum("fsb,sab->fsa", x_cols, adjacency, preferred_element_type=jnp.float32)
    row_onehot = ((my_row[:, None] == tile_ids[None, :]) & my_live[:, None]).astype(jnp.float32)
    summed_h = jnp.einsum("fsa,sr->fra", h_terms, row_onehot, precision=top_precision).astype(
        jnp.bfloat16
    )
    h_outgoing = pick_tiles(summed_h, local_tile, send_valid)
    h_incoming = lax.all_to_all(h_outgoing, "rows", split_axis=1, concat_axis=1, tiled=True)
    h_cols = pick_tiles(h_incoming, my_pos, my_live)
    g_rows = jnp.take(summed_g, my_row, axis=1)
    partial_value = jnp.einsum("fsa,fsb->sab", dy_rows, h_cols, preferred_element_type=jnp.float32)
    partial_value = partial_value + jnp.einsum(
        "fsa,fsb->sab", g_rows, x_cols, preferred_element_type=jnp.float32
    )
    result = lax.psum_scatter(partial_value, "depth", scatter_dimension=0, tiled=True)
    return result[None]


def solution(mesh):
    in_specs = (P("depth", "rows"), P("depth", "rows"), P("rows", None, None), P(), P(), P())
    out_specs = P("rows", "depth", None, None)
    return jax.shard_map(body, mesh=mesh, in_specs=in_specs, out_specs=out_specs, check_vma=False)
```

profile of v0, /device:TPU:6, one launch (start us, length us, event | category | flops | bytes accessed | tf_op | source)
XLA Modules:
  0.0 185.6 jit_solution(8449262532852980766)
XLA Ops:
  6.5 0.9 add_select_fusion
  7.4 0.7 compare_and_fusion
  8.8 0.8 copy.81
  9.6 0.6 gather_fusion.1
  10.2 1.2 bitcast_select_fusion.1
  11.5 9.5 %all-to-all-start = ((bf16[32,64,256]{2,0,1:T(8,128)(2,1)}), bf16[32,64,256]{2,0,1:T(8,128)(2,1)S(1)}, u32[]{:S(2)}, u32[]{:S(2)}) async-start(bf16[32,64,256]{2,0,1:T(8,128)(2,1)} %bitcast_select_fusion.1), calls=%async_computation | async-start | bytes 2097152 | tf_op jit(solution)/shard_map/all_to_all | solution.py:55
  22.5 1.2 convolution_bitcast_fusion
  23.6 2.6 %copy.64 = f32[32,64,256]{2,0,1:T(8,128)} copy(f32[32,64,256]{2,1,0:T(8,128)S(1)} %convolution_bitcast_fusion) | data formatting | bytes 4194304 | tf_op jit(solution)/shard_map/fsb,sp->fpb/transpose | solution.py:62
  26.2 9.4 %all-to-all-done = bf16[32,64,256]{2,0,1:T(8,128)(2,1)S(1)} async-done(((bf16[32,64,256]{2,0,1:T(8,128)(2,1)}), bf16[32,64,256]{2,0,1:T(8,128)(2,1)S(1)}, u32[]{:S(2)}, u32[]{:S(2)}) %all-to-all-start) | async-done | bytes 1048608 | tf_op jit(solution)/shard_map/all_to_all | solution.py:55
  35.6 7.3 %all-to-all-start.2 = ((f32[32,64,256]{2,0,1:T(8,128)}), f32[32,64,256]{2,0,1:T(8,128)}, u32[]{:S(2)}, u32[]{:S(2)}) async-start(f32[32,64,256]{2,0,1:T(8,128)} %copy.64), calls=%async_computation.2 | async-start | bytes 4194304 | tf_op jit(solution)/shard_map/all_to_all | solution.py:63
  43.0 1.8 gather_fusion.2
  44.8 0.7 convolution_bitcast_fusion.2
  45.5 0.6 fusion.8
  46.2 0.6 gather_fusion.3
  46.8 1.2 bitcast_select_fusion
  48.0 20.6 %all-to-all-done.2 = f32[32,64,256]{2,0,1:T(8,128)} async-done(((f32[32,64,256]{2,0,1:T(8,128)}), f32[32,64,256]{2,0,1:T(8,128)}, u32[]{:S(2)}, u32[]{:S(2)}) %all-to-all-start.2) | async-done | bytes 2097184 | tf_op jit(solution)/shard_map/all_to_all | solution.py:63
  68.6 8.3 %all-to-all-start.1 = ((bf16[32,64,256]{2,0,1:T(8,128)(2,1)}), bf16[32,64,256]{2,0,1:T(8,128)(2,1)S(1)}, u32[]{:S(2)}, u32[]{:S(2)}) async-start(bf16[32,64,256]{2,0,1:T(8,128)(2,1)} %bitcast_select_fusion), calls=%async_computation.1 | async-start | bytes 2097152 | tf_op jit(solution)/shard_map/all_to_all | solution.py:77
  77.0 3.4 %fusion.5 = bf16[32,4,256]{2,1,0:T(4,128)(2,1)S(1)} fusion(f32[32,64,256]{2,0,1:T(8,128)} %all-to-all-done.2, s32[64]{0:T(128)S(1)} %reshape.72, pred[64]{0:T(512)(128)(4,1)S(1)} %broadcast_in_dim.114), kind=kOutput, calls=%fused_computation.14 | convolution fusion | flops 25199104 | bytes 2163008 | tf_op jit(solution)/shard_map/fpb,pr->frb/dot_general | solution.py:68
  80.4 1.3 gather_fusion.5
  81.7 9.9 %all-to-all-done.1 = bf16[32,64,256]{2,0,1:T(8,128)(2,1)S(1)} async-done(((bf16[32,64,256]{2,0,1:T(8,128)(2,1)}), bf16[32,64,256]{2,0,1:T(8,128)(2,1)S(1)}, u32[]{:S(2)}, u32[]{:S(2)}) %all-to-all-start.1) | async-done | bytes 1048608 | tf_op jit(solution)/shard_map/all_to_all | solution.py:77
  91.6 1.3 gather_fusion.4
  92.9 1.9 %fusion.12 = f32[16,256,256]{2,1,0:T(8,128)S(1)} fusion(bf16[16,32,256]{2,1,0:T(8,128)(2,1)} %gather_fusion.4, pred[16]{0:T(512)(128)(4,1)S(1)} %compare_and_fusion.1, pred[16]{0:T(512)(128)(4,1)S(1)} %select_reduce_fusion.2, bf16[16,32,256]{2,1,0:T(8,128)(2,1)S(1)} %gather_fusion, pred[16]{0:T(512)(128)(4,1)S(1)} %compare_and_fusion.3), kind=kOutput, calls=%fused_computation.22 | convolution fusion | flops 67502080 | bytes 4718640 | tf_op jit(solution)/shard_map/fsa,fsb->sab/dot_general | solution.py:80
  94.8 2.8 %convolution_add_fusion = f32[16,256,256]{2,1,0:T(8,128)} fusion(f32[16,256,256]{2,1,0:T(8,128)S(1)} %fusion.12, bf16[16,32,256]{2,1,0:T(8,128)(2,1)S(1)} %copy-done.4, pred[16]{0:T(512)(128)(4,1)S(1)} %compare_and_fusion.3, bf16[16,32,256]{2,1,0:T(8,128)(2,1)S(1)} %copy-done.2, pred[16]{0:T(512)(128)(4,1)S(1)} %compare_and_fusion.1, ...), kind=kOutput, calls=%fused_computation.6 | convolution fusion | flops 68550656 | bytes 8912944 | tf_op jit(solution)/shard_map/fsa,fsb->sab/dot_general | solution.py:81
  97.6 81.2 %reduce-scatter.2.cloned.1.call-done = f32[1,256,256]{2,1,0:T(8,128)} async-done(((f32[16,256,256]{2,1,0:T(8,128)}), f32[1,256,256]{2,1,0:T(8,128)}) %reduce-scatter.2.cloned.1.call-update) | async-done | bytes 262160 | tf_op jit(solution)/shard_map/reduce_scatter | solution.py:84
  (40 shorter events, 2.2 us)
Async XLA Ops:
  6.5 15.4 %copy-start = (bf16[16,256,256]{2,1,0:T(8,128)(2,1)S(1)}, bf16[16,256,256]{2,1,0:T(8,128)(2,1)}, u32[]{:S(2)}) copy-start(bf16[16,256,256]{2,1,0:T(8,128)(2,1)} %param.16) | copy-start | bytes 6291460
  10.2 10.7 %copy-start.6 = (s32[32,16]{0,1:T(8,128)S(1)}, s32[32,16]{0,1:T(8,128)}, u32[]{:S(2)}) copy-start(s32[32,16]{0,1:T(8,128)} %param.18) | copy-start | bytes 6148
  10.2 10.9 %copy-start.5 = (bf16[32,1024]{1,0:T(8,128)(2,1)S(1)}, bf16[32,1024]{1,0:T(8,128)(2,1)}, u32[]{:S(2)}) copy-start(bf16[32,1024]{1,0:T(8,128)(2,1)} %param.15) | copy-start | bytes 196612
  11.5 24.2 %all-to-all-start = ((bf16[32,64,256]{2,0,1:T(8,128)(2,1)}), bf16[32,64,256]{2,0,1:T(8,128)(2,1)S(1)}, u32[]{:S(2)}, u32[]{:S(2)}) async-start(bf16[32,64,256]{2,0,1:T(8,128)(2,1)} %bitcast_select_fusion.1), calls=%async_computation | async-start | bytes 2097152 | tf_op jit(solution)/shard_map/all_to_all | solution.py:55
  35.6 7.3 %copy-start.3 = (bf16[32,64,256]{2,0,1:T(8,128)(2,1)}, bf16[32,64,256]{2,0,1:T(8,128)(2,1)S(1)}, u32[]{:S(2)}) copy-start(bf16[32,64,256]{2,0,1:T(8,128)(2,1)S(1)} %all-to-all-done) | copy-start | bytes 3145732
  35.6 33.0 %all-to-all-start.2 = ((f32[32,64,256]{2,0,1:T(8,128)}), f32[32,64,256]{2,0,1:T(8,128)}, u32[]{:S(2)}, u32[]{:S(2)}) async-start(f32[32,64,256]{2,0,1:T(8,128)} %copy.64), calls=%async_computation.2 | async-start | bytes 4194304 | tf_op jit(solution)/shard_map/all_to_all | solution.py:63
  44.8 1.3 copy-start.1
  68.6 23.0 %all-to-all-start.1 = ((bf16[32,64,256]{2,0,1:T(8,128)(2,1)}), bf16[32,64,256]{2,0,1:T(8,128)(2,1)S(1)}, u32[]{:S(2)}, u32[]{:S(2)}) async-start(bf16[32,64,256]{2,0,1:T(8,128)(2,1)} %bitcast_select_fusion), calls=%async_computation.1 | async-start | bytes 2097152 | tf_op jit(solution)/shard_map/all_to_all | solution.py:77
  76.9 101.9 %reduce-scatter.2.cloned.1.call-start = ((), (), s32[]{:S(2)}) async-start(), calls=%async_computation.4 | async-start | bytes 4456448 | tf_op jit(solution)/shard_map/reduce_scatter | solution.py:84
  92.9 1.9 %copy-start.2 = (bf16[16,32,256]{2,1,0:T(8,128)(2,1)S(1)}, bf16[16,32,256]{2,1,0:T(8,128)(2,1)}, u32[]{:S(2)}) copy-start(bf16[16,32,256]{2,1,0:T(8,128)(2,1)} %copy-done.1) | copy-start | bytes 786436
  92.9 1.9 %copy-start.4 = (bf16[16,32,256]{2,1,0:T(8,128)(2,1)S(1)}, bf16[16,32,256]{2,1,0:T(8,128)(2,1)}, u32[]{:S(2)}) copy-start(bf16[16,32,256]{2,1,0:T(8,128)(2,1)} %gather_fusion.5) | copy-start | bytes 786436
Sparse Core Ops, SparseCore 0:
  97.7 81.0 reduce-scatter.1
where the time goes:
time: 186 us
  waiting for transfers between devices  121 us (65%)
  starting transfers between devices  25.1 us (13%)
  between operations  13.7 us (7%)
  matrix products  11.1 us (6%)
  local copies, waits for them, and re-layouts  9.98 us (5%)
  other arithmetic  4.59 us (2%)
    reduce_scatter x1, waiting for transfers between devices, body(): lax.psum_scatter(partial_value, 'depth', scatter_dimension=0, tiled=True)  81.2 us
    all_to_all x1, waiting for transfers between devices, body(): lax.all_to_all(g_outgoing, 'rows', split_axis=1, concat_axis=1, tiled=True)  20.6 us
    all_to_all x1, waiting for transfers between devices, body(): lax.all_to_all(h_outgoing, 'rows', split_axis=1, concat_axis=1, tiled=True)  9.94 us
    all_to_all x1, starting transfers between devices, body(): lax.all_to_all(outgoing, 'rows', split_axis=1, concat_axis=1, tiled=True)  9.46 us
    all_to_all x1, waiting for transfers between devices, body(): lax.all_to_all(outgoing, 'rows', split_axis=1, concat_axis=1, tiled=True)  9.43 us
    all_to_all x1, starting transfers between devices, body(): lax.all_to_all(h_outgoing, 'rows', split_axis=1, concat_axis=1, tiled=True)  8.28 us
    all_to_all x1, starting transfers between devices, body(): lax.all_to_all(g_outgoing, 'rows', split_axis=1, concat_axis=1, tiled=True)  7.31 us
    gather x4, local copies, waits for them, and re-layouts, pick_tiles(): picked = jnp.take(source, indices, axis=1)  4.28 us
  transfers between devices with their start and end apart: 4, of which 4 were waited for; matrix products, arithmetic and copies ran while one was open for 8% of the time, Pallas kernels for 0%

commit v1 on v0

v1 whole, which is shorter than its diff:
```python
import jax
import jax.numpy as jnp
from jax import lax
from jax.experimental import pallas as pl
from jax.experimental.pallas import tpu as pltpu
from jax.sharding import PartitionSpec as P

PAIR_MOST = 2
SMEM = pltpu.SMEM
VMEM = pltpu.VMEM


def spec_of(space):
    return pl.BlockSpec(memory_space=space)


def request_tables(tile_row, tile_col, tile_count, row_tiles, own_index):
    slot_count = tile_col.shape[1]
    slot_ids = jnp.arange(slot_count, dtype=jnp.int32)
    is_live = slot_ids[None, :] < tile_count[:, None]
    owners = tile_col // row_tiles
    wanted = is_live & (owners == own_index)
    code = tile_col % row_tiles + 1
    first = jnp.max(jnp.where(wanted, (slot_count - 1 - slot_ids)[None, :] * 8 + code, 0), axis=1)
    last = jnp.max(jnp.where(wanted, slot_ids[None, :] * 8 + code, 0), axis=1)
    two = (last // 8 + first // 8) != slot_count - 1
    asked = jnp.stack([first % 8, jnp.where(two, last % 8, 0)], axis=1).reshape(-1)
    my_owner = lax.dynamic_index_in_dim(owners, own_index, 0, keepdims=False)
    my_live = lax.dynamic_index_in_dim(is_live, own_index, 0, keepdims=False)
    my_row = lax.dynamic_index_in_dim(tile_row, own_index, 0, keepdims=False)
    earlier = (slot_ids[:, None] > slot_ids[None, :]) & (my_owner[:, None] == my_owner[None, :])
    rank = jnp.sum(earlier.astype(jnp.int32), axis=1)
    place = jnp.where(my_live, my_owner * PAIR_MOST + rank, -1)
    return asked, jnp.concatenate([place, my_row])


def tile_cols(index, width):
    return pl.ds(pl.multiple_of(index * width, width), width)


def pack_x_kernel(asked_ref, x_ref, out_ref):
    width = out_ref.shape[2]
    for p in range(out_ref.shape[0]):
        t = jnp.maximum(asked_ref[p] - 1, 0)
        out_ref[p] = x_ref[:, tile_cols(t, width)]


def g_terms_kernel(mine_ref, dy_ref, a_ref, g_ref, dyz_ref):
    slots, width = a_ref.shape[0], a_ref.shape[1]
    g_ref[...] = jnp.zeros(g_ref.shape, g_ref.dtype)
    for s in range(slots):
        place = mine_ref[s]
        dy = dy_ref[:, tile_cols(mine_ref[slots + s], width)]
        dyz_ref[s] = dy
        term = jnp.dot(dy, a_ref[s], preferred_element_type=jnp.float32).astype(g_ref.dtype)

        @pl.when(place >= 0)
        def _():
            g_ref[jnp.maximum(place, 0)] = term


def h_kernel(mine_ref, asked_ref, xin_ref, a_ref, h_ref, xz_ref, acc_ref):
    slots = a_ref.shape[0]
    acc_ref[...] = jnp.zeros(acc_ref.shape, acc_ref.dtype)
    for s in range(slots):
        place = mine_ref[s]
        row = mine_ref[slots + s]
        x = xin_ref[jnp.maximum(place, 0)]
        xz_ref[s] = x
        term = lax.dot_general(x, a_ref[s], (((1,), (1,)), ((), ())), preferred_element_type=jnp.float32)

        @pl.when(place >= 0)
        def _():
            acc_ref[row] += term

    for p in range(h_ref.shape[0]):
        t = jnp.maximum(asked_ref[p] - 1, 0)
        h_ref[p] = acc_ref[t].astype(h_ref.dtype)


def g_sum_kernel(mine_ref, asked_ref, gin_ref, gz_ref, acc_ref):
    acc_ref[...] = jnp.zeros(acc_ref.shape, acc_ref.dtype)
    for p in range(gin_ref.shape[0]):
        t = asked_ref[p]

        @pl.when(t > 0)
        def _():
            acc_ref[jnp.maximum(t - 1, 0)] += gin_ref[p].astype(jnp.float32)

    slots = gz_ref.shape[0]
    for s in range(slots):
        gz_ref[s] = acc_ref[mine_ref[slots + s]].astype(gz_ref.dtype)


def pick_kernel(mine_ref, hin_ref, hz_ref):
    for s in range(hz_ref.shape[0]):
        hz_ref[s] = hin_ref[jnp.maximum(mine_ref[s], 0)]


def body(node_feat, grad_out, adjacency, tile_count, tile_row, tile_col):
    slots, width = adjacency.shape[0], adjacency.shape[1]
    feat_part = node_feat.shape[0]
    row_tiles = node_feat.shape[1] // width
    own_index = lax.axis_index("rows")
    places = lax.axis_size("rows") * PAIR_MOST
    bf16 = node_feat.dtype
    asked, mine = request_tables(tile_row, tile_col, tile_count, row_tiles, own_index)
    packed = jax.ShapeDtypeStruct((places, feat_part, width), bf16)
    slotted = jax.ShapeDtypeStruct((slots, feat_part, width), bf16)
    acc = VMEM((row_tiles, feat_part, width), jnp.float32)
    smem, vmem = spec_of(SMEM), spec_of(VMEM)

    x_out = pl.pallas_call(pack_x_kernel, out_shape=packed, in_specs=[smem, vmem], out_specs=vmem)(asked, node_feat)
    x_in = lax.all_to_all(x_out, "rows", 0, 0, tiled=True)
    g_out, dy_z = pl.pallas_call(
        g_terms_kernel, out_shape=(packed, slotted), in_specs=[smem, vmem, vmem], out_specs=(vmem, vmem)
    )(mine, grad_out, adjacency)
    g_in = lax.all_to_all(g_out, "rows", 0, 0, tiled=True)
    h_out, x_z = pl.pallas_call(
        h_kernel,
        out_shape=(packed, slotted),
        in_specs=[smem, smem, vmem, vmem],
        out_specs=(vmem, vmem),
        scratch_shapes=[acc],
    )(mine, asked, x_in, adjacency)
    h_in = lax.all_to_all(h_out, "rows", 0, 0, tiled=True)
    g_z = pl.pallas_call(
        g_sum_kernel, out_shape=slotted, in_specs=[smem, smem, vmem], out_specs=vmem, scratch_shapes=[acc]
    )(mine, asked, g_in)
    h_z = pl.pallas_call(pick_kernel, out_shape=slotted, in_specs=[smem, vmem], out_specs=vmem)(mine, h_in)
    left = jnp.concatenate([dy_z, g_z], axis=1)
    right = jnp.concatenate([h_z, x_z], axis=1)
    both = jnp.concatenate([left, right], axis=1)
    full = lax.all_to_all(both, "depth", 0, 0, tiled=True)
    two = 2 * feat_part
    result = jnp.einsum("qfa,qfb->ab", full[:, :two], full[:, two:], preferred_element_type=jnp.float32)
    alive = lax.axis_index("depth") < lax.dynamic_index_in_dim(tile_count, own_index, 0, keepdims=False)
    return jnp.where(alive, result, 0.0)[None, None]


def solution(mesh):
    in_specs = (P("depth", "rows"), P("depth", "rows"), P("rows", None, None), P(), P(), P())
    out_specs = P("rows", "depth", None, None)
    return jax.shard_map(body, mesh=mesh, in_specs=in_specs, out_specs=out_specs, check_vma=False)
```

time: 186 us -> 144 us (0.77)
  the two profiles are of different devices: /device:TPU:6 before, /device:TPU:32 now
where the time goes in v1:
time: 144 us; the launch traced here: 143 us
  waiting for transfers between devices  85.4 us (59%)
  starting transfers between devices  30.5 us (21%)
  Pallas kernels  17.7 us (12%)
  other arithmetic  4.41 us (3%)
  local copies, waits for them, and re-layouts  2.92 us (2%)
    all_to_all x1, waiting for transfers between devices, body(): full = lax.all_to_all(both, 'depth', 0, 0, tiled=True)  48.6 us
    all_to_all x1, starting transfers between devices, body(): full = lax.all_to_all(both, 'depth', 0, 0, tiled=True)  15.2 us
    all_to_all x1, waiting for transfers between devices, body(): h_in = lax.all_to_all(h_out, 'rows', 0, 0, tiled=True)  14.8 us
    all_to_all x1, waiting for transfers between devices, body(): g_in = lax.all_to_all(g_out, 'rows', 0, 0, tiled=True)  11.2 us
    all_to_all x1, waiting for transfers between devices, body(): x_in = lax.all_to_all(x_out, 'rows', 0, 0, tiled=True)  10.8 us
    all_to_all x1, starting transfers between devices, body(): x_in = lax.all_to_all(x_out, 'rows', 0, 0, tiled=True)  7.32 us
    pallas_call x1, Pallas kernels, body(): pl.pallas_call(h_kernel, out_shape=(packed, slotted), in_specs=[smem, sme...  6.09 us
    pallas_call x1, Pallas kernels, body(): pl.pallas_call(g_terms_kernel, out_shape=(packed, slotted), in_specs=[sme...  5.19 us
  transfers between devices with their start and end apart: 4, of which 4 were waited for; matrix products, arithmetic and copies ran while one was open for 1% of the time, Pallas kernels for 10%

profile of v1, /device:TPU:32, one launch (start us, length us, event | category | flops | bytes accessed | tf_op | source)
XLA Modules:
  0.0 142.8 jit_solution(14769213118425174968)
XLA Ops:
  0.0 0.7 compare_and_fusion
  0.7 0.8 select_reduce_fusion
  1.7 0.7 reshape.166.asked_ref
  2.4 2.0 %shard_map.66 = bf16[64,32,256]{2,1,0:T(8,128)(2,1)} custom-call(s32[64]{0:T(128)} %reshape.166.asked_ref, bf16[32,1024]{1,0:T(8,128)(2,1)} %x_ref.1), custom_call_target="tpu_custom_call" | custom-call | tf_op jit(solution)/shard_map/pallas_call | solution.py:113
  4.3 7.3 %all-to-all-start.1 = ((bf16[64,32,256]{2,1,0:T(8,128)(2,1)}), bf16[64,32,256]{2,1,0:T(8,128)(2,1)S(1)}, u32[]{:S(2)}, u32[]{:S(2)}) async-start(bf16[64,32,256]{2,1,0:T(8,128)(2,1)} %shard_map.66), calls=%async_computation.1 | async-start | bytes 2097152 | tf_op jit(solution)/shard_map/all_to_all | solution.py:114
  11.7 0.2 dynamic-slice_reduce_fusion
  12.0 0.2 dynamic-slice_reduce_fusion.2
  12.2 0.2 convert_reduce_fusion
  12.4 0.6 pad_add_fusion.1.mine_ref
  13.0 5.2 %shard_map.64 = (bf16[64,32,256]{2,1,0:T(8,128)(2,1)}, bf16[16,32,256]{2,1,0:T(8,128)(2,1)}) custom-call(s32[32]{0:T(128)} %pad_add_fusion.1.mine_ref, bf16[32,1024]{1,0:T(8,128)(2,1)} %dy_ref.1, bf16[16,256,256]{2,1,0:T(8,128)(2,1)} %a_ref.3), custom_call_target="tpu_custom_call" | custom-call | tf_op jit(solution)/shard_map/pallas_call | solution.py:115
  18.2 10.8 %all-to-all-done.1.xin_ref = bf16[64,32,256]{2,1,0:T(8,128)(2,1)S(1)} async-done(((bf16[64,32,256]{2,1,0:T(8,128)(2,1)}), bf16[64,32,256]{2,1,0:T(8,128)(2,1)S(1)}, u32[]{:S(2)}, u32[]{:S(2)}) %all-to-all-start.1) | async-done | bytes 1048608 | tf_op jit(solution)/shard_map/all_to_all | solution.py:114
  29.0 3.9 %all-to-all-start = ((bf16[64,32,256]{2,1,0:T(8,128)(2,1)}), bf16[64,32,256]{2,1,0:T(8,128)(2,1)S(1)}, u32[]{:S(2)}, u32[]{:S(2)}) async-start(bf16[64,32,256]{2,1,0:T(8,128)(2,1)} %get-tuple-element.10), calls=%async_computation | async-start | bytes 2097152 | tf_op jit(solution)/shard_map/all_to_all | solution.py:118
  32.9 6.1 %shard_map.67 = (bf16[64,32,256]{2,1,0:T(8,128)(2,1)}, bf16[16,32,256]{2,1,0:T(8,128)(2,1)}) custom-call(s32[32]{0:T(128)} %pad_add_fusion.1.mine_ref, s32[64]{0:T(128)} %reshape.166.asked_ref, bf16[64,32,256]{2,1,0:T(8,128)(2,1)} %copy-done.1, bf16[16,256,256]{2,1,0:T(8,128)(2,1)} %a_ref.3), custom_call_target="tpu_custom_call" | custom-call | tf_op jit(solution)/shard_map/pallas_call | solution.py:119
  39.0 11.2 %all-to-all-done.gin_ref = bf16[64,32,256]{2,1,0:T(8,128)(2,1)S(1)} async-done(((bf16[64,32,256]{2,1,0:T(8,128)(2,1)}), bf16[64,32,256]{2,1,0:T(8,128)(2,1)S(1)}, u32[]{:S(2)}, u32[]{:S(2)}) %all-to-all-start) | async-done | bytes 1048608 | tf_op jit(solution)/shard_map/all_to_all | solution.py:118
  50.3 4.1 %all-to-all-start.2 = ((bf16[64,32,256]{2,1,0:T(8,128)(2,1)}), bf16[64,32,256]{2,1,0:T(8,128)(2,1)S(1)}, u32[]{:S(2)}, u32[]{:S(2)}) async-start(bf16[64,32,256]{2,1,0:T(8,128)(2,1)} %get-tuple-element.11), calls=%async_computation.2 | async-start | bytes 2097152 | tf_op jit(solution)/shard_map/all_to_all | solution.py:126
  54.3 2.5 %shard_map.65 = bf16[16,32,256]{2,1,0:T(8,128)(2,1)} custom-call(s32[32]{0:T(128)} %pad_add_fusion.1.mine_ref, s32[64]{0:T(128)} %reshape.166.asked_ref, bf16[64,32,256]{2,1,0:T(8,128)(2,1)} %copy-done.2), custom_call_target="tpu_custom_call" | custom-call | tf_op jit(solution)/shard_map/pallas_call | solution.py:127
  56.9 14.8 %all-to-all-done.2.hin_ref = bf16[64,32,256]{2,1,0:T(8,128)(2,1)S(1)} async-done(((bf16[64,32,256]{2,1,0:T(8,128)(2,1)}), bf16[64,32,256]{2,1,0:T(8,128)(2,1)S(1)}, u32[]{:S(2)}, u32[]{:S(2)}) %all-to-all-start.2) | async-done | bytes 1048608 | tf_op jit(solution)/shard_map/all_to_all | solution.py:126
  71.7 1.0 copy-done.3
  72.6 2.0 %shard_map.68 = bf16[16,32,256]{2,1,0:T(8,128)(2,1)} custom-call(s32[32]{0:T(128)} %pad_add_fusion.1.mine_ref, bf16[64,32,256]{2,1,0:T(8,128)(2,1)} %copy-done.3), custom_call_target="tpu_custom_call" | custom-call | tf_op jit(solution)/shard_map/pallas_call | solution.py:130
  74.6 2.1 %pad_maximum_fusion = bf16[16,128,256]{2,1,0:T(8,128)(2,1)} fusion(bf16[16,32,256]{2,1,0:T(8,128)(2,1)S(1)} %copy-done.5, bf16[16,32,256]{2,1,0:T(8,128)(2,1)} %shard_map.68, bf16[16,32,256]{2,1,0:T(8,128)(2,1)} %shard_map.65, bf16[16,32,256]{2,1,0:T(8,128)(2,1)S(1)} %copy-done.4), kind=kLoop, calls=%fused_computation.3 | loop fusion | flops 4194304 | bytes 2097152 | tf_op jit(solution)/shard_map/concatenate | solution.py:133
  76.7 15.2 %all-to-all-start.3 = ((bf16[16,128,256]{2,1,0:T(8,128)(2,1)}), bf16[16,128,256]{2,1,0:T(8,128)(2,1)S(1)}, u32[]{:S(2)}, u32[]{:S(2)}) async-start(bf16[16,128,256]{2,1,0:T(8,128)(2,1)} %pad_maximum_fusion), calls=%async_computation.3 | async-start | bytes 2097152 | tf_op jit(solution)/shard_map/all_to_all | solution.py:134
  91.9 0.6 dynamic_slice.15
  93.1 48.6 %all-to-all-done.3 = bf16[16,128,256]{2,1,0:T(8,128)(2,1)S(1)} async-done(((bf16[16,128,256]{2,1,0:T(8,128)(2,1)}), bf16[16,128,256]{2,1,0:T(8,128)(2,1)S(1)}, u32[]{:S(2)}, u32[]{:S(2)}) %all-to-all-start.3) | async-done | bytes 1048608 | tf_op jit(solution)/shard_map/all_to_all | solution.py:134
  141.8 1.0 fusion.1
  (19 shorter events, 0.3 us)
Async XLA Ops:
  0.0 11.6 %copy-start = (s32[32,16]{0,1:T(8,128)S(1)}, s32[32,16]{0,1:T(8,128)}, u32[]{:S(2)}) copy-start(s32[32,16]{0,1:T(8,128)} %param.10) | copy-start | bytes 6148
  4.3 24.7 %all-to-all-start.1 = ((bf16[64,32,256]{2,1,0:T(8,128)(2,1)}), bf16[64,32,256]{2,1,0:T(8,128)(2,1)S(1)}, u32[]{:S(2)}, u32[]{:S(2)}) async-start(bf16[64,32,256]{2,1,0:T(8,128)(2,1)} %shard_map.66), calls=%async_computation.1 | async-start | bytes 2097152 | tf_op jit(solution)/shard_map/all_to_all | solution.py:114
  29.0 3.9 %copy-start.1 = (bf16[64,32,256]{2,1,0:T(8,128)(2,1)}, bf16[64,32,256]{2,1,0:T(8,128)(2,1)S(1)}, u32[]{:S(2)}) copy-start(bf16[64,32,256]{2,1,0:T(8,128)(2,1)S(1)} %all-to-all-done.1.xin_ref) | copy-start | bytes 3145732
  29.0 21.3 %all-to-all-start = ((bf16[64,32,256]{2,1,0:T(8,128)(2,1)}), bf16[64,32,256]{2,1,0:T(8,128)(2,1)S(1)}, u32[]{:S(2)}, u32[]{:S(2)}) async-start(bf16[64,32,256]{2,1,0:T(8,128)(2,1)} %get-tuple-element.10), calls=%async_computation | async-start | bytes 2097152 | tf_op jit(solution)/shard_map/all_to_all | solution.py:118
  50.3 4.1 %copy-start.2 = (bf16[64,32,256]{2,1,0:T(8,128)(2,1)}, bf16[64,32,256]{2,1,0:T(8,128)(2,1)S(1)}, u32[]{:S(2)}) copy-start(bf16[64,32,256]{2,1,0:T(8,128)(2,1)S(1)} %all-to-all-done.gin_ref) | copy-start | bytes 3145732
  50.3 24.3 %copy-start.4 = (bf16[16,32,256]{2,1,0:T(8,128)(2,1)S(1)}, bf16[16,32,256]{2,1,0:T(8,128)(2,1)}, u32[]{:S(2)}) copy-start(bf16[16,32,256]{2,1,0:T(8,128)(2,1)} %get-tuple-element.9) | copy-start | bytes 786436
  50.3 24.3 %copy-start.5 = (bf16[16,32,256]{2,1,0:T(8,128)(2,1)S(1)}, bf16[16,32,256]{2,1,0:T(8,128)(2,1)}, u32[]{:S(2)}) copy-start(bf16[16,32,256]{2,1,0:T(8,128)(2,1)} %get-tuple-element.12) | copy-start | bytes 786436
  50.3 21.4 %all-to-all-start.2 = ((bf16[64,32,256]{2,1,0:T(8,128)(2,1)}), bf16[64,32,256]{2,1,0:T(8,128)(2,1)S(1)}, u32[]{:S(2)}, u32[]{:S(2)}) async-start(bf16[64,32,256]{2,1,0:T(8,128)(2,1)} %get-tuple-element.11), calls=%async_computation.2 | async-start | bytes 2097152 | tf_op jit(solution)/shard_map/all_to_all | solution.py:126
  71.7 1.0 copy-start.3
  74.6 17.3 %copy-start.6 = (s32[32]{0:T(128)S(1)}, s32[32]{0:T(128)}, u32[]{:S(2)}) copy-start(s32[32]{0:T(128)} %param.9) | copy-start | bytes 388
  76.7 65.1 %all-to-all-start.3 = ((bf16[16,128,256]{2,1,0:T(8,128)(2,1)}), bf16[16,128,256]{2,1,0:T(8,128)(2,1)S(1)}, u32[]{:S(2)}, u32[]{:S(2)}) async-start(bf16[16,128,256]{2,1,0:T(8,128)(2,1)} %pad_maximum_fusion), calls=%async_computation.3 | async-start | bytes 2097152 | tf_op jit(solution)/shard_map/all_to_all | solution.py:134

commit v2 on v1

v2 whole, which is shorter than its diff:
```python
import jax
import jax.numpy as jnp
from jax import lax
from jax.experimental import pallas as pl
from jax.experimental.pallas import tpu as pltpu
from jax.sharding import PartitionSpec as P

PAIR_MOST = 2
SMEM = pl.BlockSpec(memory_space=pltpu.SMEM)
VMEM = pl.BlockSpec(memory_space=pltpu.VMEM)
ANY = pl.BlockSpec(memory_space=pl.ANY)


def request_tables(tile_row, tile_col, tile_count, row_tiles, own_index):
    slot_count = tile_col.shape[1]
    slot_ids = jnp.arange(slot_count, dtype=jnp.int32)
    is_live = slot_ids[None, :] < tile_count[:, None]
    owners = tile_col // row_tiles
    wanted = is_live & (owners == own_index)
    code = tile_col % row_tiles + 1
    first = jnp.max(jnp.where(wanted, (slot_count - 1 - slot_ids)[None, :] * 8 + code, 0), axis=1)
    last = jnp.max(jnp.where(wanted, slot_ids[None, :] * 8 + code, 0), axis=1)
    two = (last // 8 + first // 8) != slot_count - 1
    asked = jnp.stack([first % 8, jnp.where(two, last % 8, 0)])
    my_owner = lax.dynamic_index_in_dim(owners, own_index, 0, keepdims=False)
    my_live = lax.dynamic_index_in_dim(is_live, own_index, 0, keepdims=False)
    my_row = lax.dynamic_index_in_dim(tile_row, own_index, 0, keepdims=False)
    earlier = (slot_ids[:, None] > slot_ids[None, :]) & (my_owner[:, None] == my_owner[None, :])
    rank = jnp.sum(earlier.astype(jnp.int32), axis=1)
    place = jnp.where(my_live, my_owner * PAIR_MOST + rank, -1)
    return asked, jnp.concatenate([place, my_row])


def tile_cols(index, width):
    return pl.ds(pl.multiple_of(index * width, width), width)


def send_xg_kernel(mine_ref, asked_ref, x_ref, dy_ref, a_ref, out_ref):
    slots, width = a_ref.shape[0], a_ref.shape[1]
    peers, most = out_ref.shape[0], out_ref.shape[1] // 2
    for r in range(peers):
        for k in range(most):
            t = jnp.maximum(asked_ref[k, r] - 1, 0)
            out_ref[r, k] = x_ref[:, tile_cols(t, width)]
            out_ref[r, most + k] = jnp.zeros(out_ref.shape[2:], out_ref.dtype)
    terms = []
    for s in range(slots):
        dy = dy_ref[:, tile_cols(mine_ref[slots + s], width)]
        terms.append(jnp.dot(dy, a_ref[s], preferred_element_type=jnp.float32).astype(out_ref.dtype))
    for s in range(slots):
        place = mine_ref[s]

        @pl.when(place >= 0)
        def _():
            out_ref[place // most, most + place % most] = terms[s]


def h_kernel(mine_ref, asked_ref, in_ref, a_ref, out_ref, a_buf, x_buf, acc_ref, a_sem, x_sem):
    slots = a_ref.shape[0]
    peers, most = out_ref.shape[0], out_ref.shape[1]
    row_tiles = acc_ref.shape[0]
    copies = []
    for s in range(slots):
        held = jnp.maximum(mine_ref[s], 0)
        x_copy = pltpu.make_async_copy(in_ref.at[held // most, held % most], x_buf.at[s], x_sem.at[s])
        a_copy = pltpu.make_async_copy(a_ref.at[s], a_buf.at[s], a_sem.at[s])
        x_copy.start()
        a_copy.start()
        copies.append((x_copy, a_copy))
    sums = [jnp.zeros(acc_ref.shape[1:], jnp.float32) for _ in range(row_tiles)]
    for s in range(slots):
        for copy in copies[s]:
            copy.wait()
        row = mine_ref[slots + s]
        term = lax.dot_general(
            x_buf[s], a_buf[s], (((1,), (1,)), ((), ())), preferred_element_type=jnp.float32
        )
        for t in range(row_tiles):
            sums[t] = sums[t] + jnp.where((row == t) & (mine_ref[s] >= 0), term, 0.0)
    for t in range(row_tiles):
        acc_ref[t] = sums[t].astype(acc_ref.dtype)
    for r in range(peers):
        for k in range(most):
            out_ref[r, k] = acc_ref[jnp.maximum(asked_ref[k, r] - 1, 0)]


def fill_kernel(mine_ref, asked_ref, in_ref, dy_ref, z_ref, acc_ref):
    peers, most = in_ref.shape[0], in_ref.shape[1] // 2
    slots, row_tiles = z_ref.shape[0], acc_ref.shape[0]
    feat, width = acc_ref.shape[1:]
    sums = [jnp.zeros(acc_ref.shape[1:], jnp.float32) for _ in range(row_tiles)]
    for r in range(peers):
        for k in range(most):
            term = in_ref[r, most + k].astype(jnp.float32)
            code = asked_ref[k, r]
            for t in range(row_tiles):
                sums[t] = sums[t] + jnp.where(code == t + 1, term, 0.0)
    for t in range(row_tiles):
        acc_ref[t] = sums[t].astype(acc_ref.dtype)
    for s in range(slots):
        held = jnp.maximum(mine_ref[s], 0)
        row = mine_ref[slots + s]
        z_ref[s, :feat] = dy_ref[:, tile_cols(row, width)]
        z_ref[s, feat : 2 * feat] = acc_ref[row]
        z_ref[s, 2 * feat : 3 * feat] = jnp.zeros((feat, width), z_ref.dtype)
        z_ref[s, 3 * feat :] = in_ref[held // most, held % most]


def add_h_kernel(mine_ref, in_ref, z_in_ref, z_ref, sem):
    del z_in_ref
    most, feat = in_ref.shape[1], in_ref.shape[2]
    copies = []
    for s in range(z_ref.shape[0]):
        held = jnp.maximum(mine_ref[s], 0)
        target = z_ref.at[s, pl.ds(2 * feat, feat)]
        copies.append(pltpu.make_async_copy(in_ref.at[held // most, held % most], target, sem.at[s]))
        copies[-1].start()
    for copy in copies:
        copy.wait()


def exchange(value, axis):
    return lax.all_to_all(value, axis, 0, 0, tiled=True)


def body(node_feat, grad_out, adjacency, tile_count, tile_row, tile_col):
    slots, width = adjacency.shape[0], adjacency.shape[1]
    feat = node_feat.shape[0]
    row_tiles = node_feat.shape[1] // width
    own_index = lax.axis_index("rows")
    depth_index = lax.axis_index("depth")
    peers = lax.axis_size("rows")
    bf16 = node_feat.dtype
    asked, mine = request_tables(tile_row, tile_col, tile_count, row_tiles, own_index)
    xg_type = jax.ShapeDtypeStruct((peers, 2 * PAIR_MOST, feat, width), bf16)
    h_type = jax.ShapeDtypeStruct((peers, PAIR_MOST, feat, width), bf16)
    z_type = jax.ShapeDtypeStruct((slots, 4 * feat, width), bf16)
    tiles = pltpu.VMEM((row_tiles, feat, width), bf16)
    sems = pltpu.SemaphoreType.DMA((slots,))

    xg_out = pl.pallas_call(
        send_xg_kernel, out_shape=xg_type, in_specs=[SMEM, SMEM, VMEM, VMEM, VMEM], out_specs=VMEM
    )(mine, asked, node_feat, grad_out, adjacency)
    xg_in = exchange(xg_out, "rows")
    h_out = pl.pallas_call(
        h_kernel,
        out_shape=h_type,
        in_specs=[SMEM, SMEM, ANY, ANY],
        out_specs=VMEM,
        scratch_shapes=[
            pltpu.VMEM(adjacency.shape, bf16),
            pltpu.VMEM((slots, feat, width), bf16),
            tiles,
            sems,
            sems,
        ],
    )(mine, asked, xg_in, adjacency)
    h_in = exchange(h_out, "rows")
    z_part = pl.pallas_call(
        fill_kernel,
        out_shape=z_type,
        in_specs=[SMEM, SMEM, VMEM, VMEM],
        out_specs=VMEM,
        scratch_shapes=[tiles],
    )(mine, asked, xg_in, grad_out)
    z_out = pl.pallas_call(
        add_h_kernel,
        out_shape=z_type,
        in_specs=[SMEM, ANY, ANY],
        out_specs=ANY,
        input_output_aliases={2: 0},
        scratch_shapes=[sems],
    )(mine, h_in, z_part)
    z_in = exchange(z_out, "depth")
    left, right = z_in[:, : 2 * feat], z_in[:, 2 * feat :]
    result = jnp.einsum("qfa,qfb->ab", left, right, preferred_element_type=jnp.float32)
    return jnp.where(mine[depth_index] >= 0, result, 0.0)[None, None]


def solution(mesh):
    in_specs = (P("depth", "rows"), P("depth", "rows"), P("rows", None, None), P(), P(), P())
    out_specs = P("rows", "depth", None, None)
    return jax.shard_map(body, mesh=mesh, in_specs=in_specs, out_specs=out_specs, check_vma=False)
```

time: 144 us -> 149 us (1.035)
  blocking collectives: 0 us -> 36 us
  waiting for transfers between devices: 85.4 us -> 62.7 us
  starting transfers between devices: 30.5 us -> 19.2 us
  Pallas kernels: 17.7 us -> 22.9 us
  other arithmetic: 4.41 us -> 2.89 us
    all_to_all x0 -> x1, blocking collectives: none -> 36 us  [exchange(): return lax.all_to_all(value, axis, 0, 0, tiled=True)]
    all_to_all x4 -> x2, waiting for transfers between devices: 85.4 us -> 62.7 us  [exchange(): return lax.all_to_all(value, axis, 0, 0, tiled=True)]
    all_to_all x4 -> x2, starting transfers between devices: 30.5 us -> 19.2 us  [exchange(): return lax.all_to_all(value, axis, 0, 0, tiled=True)]
    pallas_call x5 -> x4, Pallas kernels: 17.7 us -> 22.9 us  [the longest x1 9.85 us: body(): pl.pallas_call(add_h_kernel, out_shape=z_type, in_specs=[SMEM, ANY, ANY],...]
    concatenate x1 -> x0, other arithmetic: 2.08 us -> none  [body(): both = jnp.concatenate([left, right], axis=1)]
  transfers between devices with their start and end apart: 4 -> 2, of which waited for: 4 -> 2; matrix products, arithmetic and copies ran while one was open for 1% -> 0% of each run, Pallas kernels for 10% -> 2%
where the time goes in v2:
time: 149 us; the launch traced here: 148 us
  waiting for transfers between devices  62.7 us (42%)
  blocking collectives  36 us (24%)
  Pallas kernels  22.9 us (15%)
  starting transfers between devices  19.2 us (13%)
  other arithmetic  2.89 us (2%)
  local copies, waits for them, and re-layouts  2.65 us (2%)
    all_to_all x2, waiting for transfers between devices, exchange(): return lax.all_to_all(value, axis, 0, 0, tiled=True)  62.7 us
    all_to_all x1, blocking collectives, exchange(): return lax.all_to_all(value, axis, 0, 0, tiled=True)  36 us
    all_to_all x2, starting transfers between devices, exchange(): return lax.all_to_all(value, axis, 0, 0, tiled=True)  19.2 us
    pallas_call x1, Pallas kernels, body(): pl.pallas_call(add_h_kernel, out_shape=z_type, in_specs=[SMEM, ANY, ANY],...  9.85 us
    pallas_call x1, Pallas kernels, body(): pl.pallas_call(h_kernel, out_shape=h_type, in_specs=[SMEM, SMEM, ANY, ANY...  6.01 us
    pallas_call x1, Pallas kernels, body(): pl.pallas_call(send_xg_kernel, out_shape=xg_type, in_specs=[SMEM, SMEM, V...  3.73 us
    pallas_call x1, Pallas kernels, body(): pl.pallas_call(fill_kernel, out_shape=z_type, in_specs=[SMEM, SMEM, VMEM,...  3.32 us
  transfers between devices with their start and end apart: 2, of which 2 were waited for; matrix products, arithmetic and copies ran while one was open for 0% of the time, Pallas kernels for 2%

profile of v2, /device:TPU:32, one launch (start us, length us, event | category | flops | bytes accessed | tf_op | source)
XLA Modules:
  0.0 148.0 jit_solution(6328034360103558376)
XLA Ops:
  0.0 0.7 compare_and_fusion
  0.7 0.2 dynamic-slice_reduce_fusion.2
  0.9 0.9 dynamic-slice_reduce_fusion
  1.8 0.2 convert_reduce_fusion
  2.0 0.8 select_reduce_fusion
  2.8 0.6 pad_add_fusion.asked_ref
  3.4 0.6 pad_add_fusion.1.mine_ref
  4.0 3.7 %shard_map.64 = bf16[32,4,32,256]{3,2,1,0:T(8,128)(2,1)} custom-call(s32[32]{0:T(128)} %pad_add_fusion.1.mine_ref, s32[2,32]{1,0:T(2,128)} %pad_add_fusion.asked_ref, bf16[32,1024]{1,0:T(8,128)(2,1)} %x_ref.1, bf16[32,1024]{1,0:T(8,128)(2,1)} %dy_ref.3, bf16[16,256,256]{2,1,0:T(8,128)(2,1)} %a_ref.3), custom_call_target="tpu_custom_call" | custom-call | tf_op jit(solution)/shard_map/pallas_call | solution.py:141
  7.7 36.0 %all_to_all.15.in_ref = bf16[32,4,32,256]{3,2,1,0:T(8,128)(2,1)} all-to-all(bf16[32,4,32,256]{3,2,1,0:T(8,128)(2,1)} %shard_map.64), channel_id=1, replica_groups=mesh['depth'=16,'rows'=32] {'rows'}, dimensions={0} | all-to-all | bytes 4194304 | tf_op jit(solution)/shard_map/all_to_all | solution.py:123
  43.7 6.0 %shard_map.65 = bf16[32,2,32,256]{3,2,1,0:T(8,128)(2,1)} custom-call(s32[32]{0:T(128)} %pad_add_fusion.1.mine_ref, s32[2,32]{1,0:T(2,128)} %pad_add_fusion.asked_ref, bf16[32,4,32,256]{3,2,1,0:T(8,128)(2,1)} %all_to_all.15.in_ref, bf16[16,256,256]{2,1,0:T(8,128)(2,1)} %a_ref.3), custom_call_target="tpu_custom_call" | custom-call | tf_op jit(solution)/shard_map/pallas_call | solution.py:145
  49.7 3.9 %all-to-all-start.1 = ((bf16[32,2,32,256]{3,2,1,0:T(8,128)(2,1)}), bf16[32,2,32,256]{3,2,1,0:T(8,128)(2,1)S(1)}, u32[]{:S(2)}, u32[]{:S(2)}) async-start(bf16[32,2,32,256]{3,2,1,0:T(8,128)(2,1)} %shard_map.65), calls=%async_computation.1 | async-start | bytes 2097152 | tf_op jit(solution)/shard_map/all_to_all | solution.py:123
  53.7 3.3 %shard_map.66.z_in_ref = bf16[16,128,256]{2,1,0:T(8,128)(2,1)} custom-call(s32[32]{0:T(128)} %pad_add_fusion.1.mine_ref, s32[2,32]{1,0:T(2,128)} %pad_add_fusion.asked_ref, bf16[32,4,32,256]{3,2,1,0:T(8,128)(2,1)} %all_to_all.15.in_ref, bf16[32,1024]{1,0:T(8,128)(2,1)} %dy_ref.3), custom_call_target="tpu_custom_call" | custom-call | tf_op jit(solution)/shard_map/pallas_call | solution.py:159
  57.0 0.0 copy-start.1
  57.0 14.0 %all-to-all-done.1.in_ref = bf16[32,2,32,256]{3,2,1,0:T(8,128)(2,1)S(1)} async-done(((bf16[32,2,32,256]{3,2,1,0:T(8,128)(2,1)}), bf16[32,2,32,256]{3,2,1,0:T(8,128)(2,1)S(1)}, u32[]{:S(2)}, u32[]{:S(2)}) %all-to-all-start.1) | async-done | bytes 1048608 | tf_op jit(solution)/shard_map/all_to_all | solution.py:123
  71.0 0.0 copy-start
  71.0 1.0 copy-done
  72.0 9.9 %shard_map.67 = bf16[16,128,256]{2,1,0:T(8,128)(2,1)} custom-call(s32[32]{0:T(128)} %pad_add_fusion.1.mine_ref, bf16[32,2,32,256]{3,2,1,0:T(8,128)(2,1)} %copy-done, bf16[16,128,256]{2,1,0:T(8,128)(2,1)} %shard_map.66.z_in_ref), custom_call_target="tpu_custom_call", output_to_operand_aliasing={{}: (2, {})} | custom-call | tf_op jit(solution)/shard_map/pallas_call | solution.py:166
  81.9 15.2 %all-to-all-start.2 = ((bf16[16,128,256]{2,1,0:T(8,128)(2,1)}), bf16[16,128,256]{2,1,0:T(8,128)(2,1)S(1)}, u32[]{:S(2)}, u32[]{:S(2)}) async-start(bf16[16,128,256]{2,1,0:T(8,128)(2,1)} %shard_map.67), calls=%async_computation.2 | async-start | bytes 2097152 | tf_op jit(solution)/shard_map/all_to_all | solution.py:123
  97.1 0.0 copy-done.1
  97.1 0.6 dynamic_slice.17
  98.3 48.6 %all-to-all-done.2 = bf16[16,128,256]{2,1,0:T(8,128)(2,1)S(1)} async-done(((bf16[16,128,256]{2,1,0:T(8,128)(2,1)}), bf16[16,128,256]{2,1,0:T(8,128)(2,1)S(1)}, u32[]{:S(2)}, u32[]{:S(2)}) %all-to-all-start.2) | async-done | bytes 1048608 | tf_op jit(solution)/shard_map/all_to_all | solution.py:123
  147.0 1.0 fusion.1
  (3 shorter events, 0.0 us)
Async XLA Ops:
  49.7 21.3 %all-to-all-start.1 = ((bf16[32,2,32,256]{3,2,1,0:T(8,128)(2,1)}), bf16[32,2,32,256]{3,2,1,0:T(8,128)(2,1)S(1)}, u32[]{:S(2)}, u32[]{:S(2)}) async-start(bf16[32,2,32,256]{3,2,1,0:T(8,128)(2,1)} %shard_map.65), calls=%async_computation.1 | async-start | bytes 2097152 | tf_op jit(solution)/shard_map/all_to_all | solution.py:123
  57.0 40.1 %copy-start.1 = (s32[32]{0:T(128)S(1)}, s32[32]{0:T(128)}, u32[]{:S(2)}) copy-start(s32[32]{0:T(128)} %pad_add_fusion.1.mine_ref) | copy-start | bytes 388
  71.0 1.0 copy-start
  81.9 65.1 %all-to-all-start.2 = ((bf16[16,128,256]{2,1,0:T(8,128)(2,1)}), bf16[16,128,256]{2,1,0:T(8,128)(2,1)S(1)}, u32[]{:S(2)}, u32[]{:S(2)}) async-start(bf16[16,128,256]{2,1,0:T(8,128)(2,1)} %shard_map.67), calls=%async_computation.2 | async-start | bytes 2097152 | tf_op jit(solution)/shard_map/all_to_all | solution.py:123

commit v3 on v2

v3 whole, which is shorter than its diff:
```python
import jax
import jax.numpy as jnp
from jax import lax
from jax.experimental import pallas as pl
from jax.experimental.pallas import tpu as pltpu
from jax.sharding import PartitionSpec as P

PAIR_MOST = 2
SMEM = pl.BlockSpec(memory_space=pltpu.SMEM)
VMEM = pl.BlockSpec(memory_space=pltpu.VMEM)
PARAMS = pltpu.CompilerParams(vmem_limit_bytes=12 * 2**20)


def tile_cols(index, width):
    return pl.ds(pl.multiple_of(index * width, width), width)


def send_xg_kernel(
    own_ref, count_ref, col_ref, row_ref, x_ref, dy_ref, a_ref, out_ref, asked_ref, mine_ref, term_ref
):
    slots, width = a_ref.shape[0], a_ref.shape[1]
    peers, most = out_ref.shape[0], out_ref.shape[1] // 2
    row_tiles = x_ref.shape[1] // width
    own = own_ref[0]
    my_count = count_ref[own]
    owners = [col_ref[s, own] // row_tiles for s in range(slots)]
    places = []
    for s in range(slots):
        row = row_ref[s, own]
        rank = jnp.int32(0)
        for earlier in range(s):
            rank = rank + jnp.where(owners[earlier] == owners[s], 1, 0)
        place = jnp.where(s < my_count, owners[s] * most + rank, -1)
        places.append(place)
        mine_ref[s] = place
        mine_ref[slots + s] = row
        dy = dy_ref[:, tile_cols(row, width)]
        term_ref[s] = jnp.dot(dy, a_ref[s], preferred_element_type=jnp.float32).astype(out_ref.dtype)
    for r in range(peers):
        first, last = jnp.int32(0), jnp.int32(0)
        for s in range(slots):
            col = col_ref[s, r]
            code = jnp.where((col // row_tiles == own) & (s < count_ref[r]), col % row_tiles + 1, 0)
            last = jnp.where((first > 0) & (code > 0), code, last)
            first = jnp.where(first > 0, first, code)
        asked_ref[0, r] = first
        asked_ref[1, r] = last
        for k, code in enumerate((first, last)):
            out_ref[r, k] = x_ref[:, tile_cols(jnp.maximum(code - 1, 0), width)]
        for k in range(most):
            out_ref[r, most + k] = jnp.zeros(out_ref.shape[2:], out_ref.dtype)
    for s in range(slots):
        place = places[s]

        @pl.when(place >= 0)
        def _():
            out_ref[place // most, most + place % most] = term_ref[s]


def h_kernel(mine_ref, asked_ref, in_ref, a_ref, out_ref, acc_ref):
    slots = a_ref.shape[0]
    peers, most = out_ref.shape[0], out_ref.shape[1]
    row_tiles = acc_ref.shape[0]
    sums = [jnp.zeros(acc_ref.shape[1:], jnp.float32) for _ in range(row_tiles)]
    for s in range(slots):
        held = jnp.maximum(mine_ref[s], 0)
        row = mine_ref[slots + s]
        x = in_ref[held // most, held % most]
        term = lax.dot_general(x, a_ref[s], (((1,), (1,)), ((), ())), preferred_element_type=jnp.float32)
        for t in range(row_tiles):
            sums[t] = sums[t] + jnp.where((row == t) & (mine_ref[s] >= 0), term, 0.0)
    for t in range(row_tiles):
        acc_ref[t] = sums[t].astype(acc_ref.dtype)
    for r in range(peers):
        for k in range(most):
            out_ref[r, k] = acc_ref[jnp.maximum(asked_ref[k, r] - 1, 0)]


def fill_kernel(mine_ref, asked_ref, in_ref, dy_ref, z_ref, acc_ref):
    peers, most = in_ref.shape[0], in_ref.shape[1] // 2
    slots, row_tiles = z_ref.shape[0], acc_ref.shape[0]
    width = acc_ref.shape[2]
    sums = [jnp.zeros(acc_ref.shape[1:], jnp.float32) for _ in range(row_tiles)]
    for r in range(peers):
        for k in range(most):
            term = in_ref[r, most + k].astype(jnp.float32)
            code = asked_ref[k, r]
            for t in range(row_tiles):
                sums[t] = sums[t] + jnp.where(code == t + 1, term, 0.0)
    for t in range(row_tiles):
        acc_ref[t] = sums[t].astype(acc_ref.dtype)
    for s in range(slots):
        held = jnp.maximum(mine_ref[s], 0)
        row = mine_ref[slots + s]
        z_ref[s, 0] = dy_ref[:, tile_cols(row, width)]
        z_ref[s, 1] = acc_ref[row]
        z_ref[s, 2] = in_ref[held // most, held % most]


def join_kernel(mine_ref, in_ref, part_ref, z_ref):
    most = in_ref.shape[1]
    ready = part_ref.shape[1]
    for s in range(z_ref.shape[0]):
        held = jnp.maximum(mine_ref[s], 0)
        z_ref[s, :ready] = part_ref[s]
        z_ref[s, ready] = in_ref[held // most, held % most]


def exchange(value, axis):
    return lax.all_to_all(value, axis, 0, 0, tiled=True)


def near(value):
    return pltpu.with_memory_space_constraint(value, pltpu.VMEM)


def body(node_feat, grad_out, adjacency, tile_count, tile_row, tile_col):
    slots, width = adjacency.shape[0], adjacency.shape[1]
    feat = node_feat.shape[0]
    row_tiles = node_feat.shape[1] // width
    own_index = lax.axis_index("rows")
    peers = lax.axis_size("rows")
    bf16 = node_feat.dtype
    xg_type = jax.ShapeDtypeStruct((peers, 2 * PAIR_MOST, feat, width), bf16)
    h_type = jax.ShapeDtypeStruct((peers, PAIR_MOST, feat, width), bf16)
    asked_type = jax.ShapeDtypeStruct((PAIR_MOST, peers), jnp.int32)
    mine_type = jax.ShapeDtypeStruct((2 * slots,), jnp.int32)
    part_type = jax.ShapeDtypeStruct((slots, 3, feat, width), bf16)
    z_type = jax.ShapeDtypeStruct((slots, 4, feat, width), bf16)
    tiles = pltpu.VMEM((row_tiles, feat, width), bf16)
    adjacency = near(adjacency)

    xg_out, asked, mine = pl.pallas_call(
        send_xg_kernel,
        out_shape=(xg_type, asked_type, mine_type),
        in_specs=[SMEM, SMEM, SMEM, SMEM, VMEM, VMEM, VMEM],
        out_specs=(VMEM, SMEM, SMEM),
        compiler_params=PARAMS,
        scratch_shapes=[pltpu.VMEM((slots, feat, width), bf16)],
    )(own_index[None], tile_count, tile_col.T, tile_row.T, node_feat, grad_out, adjacency)
    xg_in = near(exchange(xg_out, "rows"))
    h_out = pl.pallas_call(
        h_kernel,
        out_shape=h_type,
        in_specs=[SMEM, SMEM, VMEM, VMEM],
        out_specs=VMEM,
        compiler_params=PARAMS,
        scratch_shapes=[tiles],
    )(mine, asked, xg_in, adjacency)
    h_in = near(exchange(h_out, "rows"))
    z_part = pl.pallas_call(
        fill_kernel,
        out_shape=part_type,
        in_specs=[SMEM, SMEM, VMEM, VMEM],
        out_specs=VMEM,
        compiler_params=PARAMS,
        scratch_shapes=[tiles],
    )(mine, asked, xg_in, grad_out)
    z_out = pl.pallas_call(
        join_kernel,
        out_shape=z_type,
        in_specs=[SMEM, VMEM, VMEM],
        out_specs=VMEM,
        compiler_params=PARAMS,
    )(mine, h_in, near(z_part))
    z_in = exchange(z_out, "depth")
    result = jnp.einsum("qfa,qfb->ab", z_in[:, 0], z_in[:, 3], preferred_element_type=jnp.float32)
    result += jnp.einsum("qfa,qfb->ab", z_in[:, 1], z_in[:, 2], preferred_element_type=jnp.float32)
    count = lax.dynamic_index_in_dim(tile_count, own_index, 0, keepdims=False)
    return jnp.where(lax.axis_index("depth") < count, result, 0.0)[None, None]


def solution(mesh):
    in_specs = (P("depth", "rows"), P("depth", "rows"), P("rows", None, None), P(), P(), P())
    out_specs = P("rows", "depth", None, None)
    return jax.shard_map(body, mesh=mesh, in_specs=in_specs, out_specs=out_specs, check_vma=False)
```

time: 149 us -> 141 us (0.946)
  Pallas kernels: 22.9 us -> 10.5 us
  local copies, waits for them, and re-layouts: 2.65 us -> 8.94 us
  other arithmetic: 2.89 us -> 0 us
    pallas_call x4, Pallas kernels: 22.9 us -> 10.5 us  [the longest x1 6.31 us: body(): pl.pallas_call(send_xg_kernel, out_shape=(xg_type, asked_type, mine_type)...]
    unnamed x4 -> x24, local copies, waits for them, and re-layouts: 0.99 us -> 8.36 us
  transfers between devices with their start and end apart: 2 -> 2, of which waited for: 2 -> 2; matrix products, arithmetic and copies ran while one was open for 0% -> 0% of each run, Pallas kernels for 2% -> 1%
where the time goes in v3:
time: 141 us; the launch traced here: 140 us
  waiting for transfers between devices  63.7 us (45%)
  blocking collectives  35.8 us (25%)
  starting transfers between devices  19.3 us (14%)
  Pallas kernels  10.5 us (7%)
  local copies, waits for them, and re-layouts  8.94 us (6%)
    all_to_all x2, waiting for transfers between devices, exchange(): return lax.all_to_all(value, axis, 0, 0, tiled=True)  63.7 us
    all_to_all x1, blocking collectives, exchange(): return lax.all_to_all(value, axis, 0, 0, tiled=True)  35.8 us
    all_to_all x2, starting transfers between devices, exchange(): return lax.all_to_all(value, axis, 0, 0, tiled=True)  19.3 us
    unnamed x24, local copies, waits for them, and re-layouts  8.36 us
    pallas_call x1, Pallas kernels, body(): pl.pallas_call(send_xg_kernel, out_shape=(xg_type, asked_type, mine_type)...  6.31 us
  transfers between devices with their start and end apart: 2, of which 2 were waited for; matrix products, arithmetic and copies ran while one was open for 0% of the time, Pallas kernels for 1%

profile of v3, /device:TPU:32, one launch (start us, length us, event | category | flops | bytes accessed | tf_op | source)
XLA Modules:
  0.0 140.3 jit_solution(1495329162382120394)
XLA Ops:
  0.0 1.6 %copy-done = bf16[16,256,256]{2,1,0:T(8,128)(2,1)S(1)} copy-done((bf16[16,256,256]{2,1,0:T(8,128)(2,1)S(1)}, bf16[16,256,256]{2,1,0:T(8,128)(2,1)}, u32[]{:S(2)}) %copy-start) | copy-done | bytes 2097176
  1.6 0.8 copy-done.5
  2.4 0.8 copy-done.7
  3.3 0.7 copy-done.8
  4.0 0.7 copy-done.9
  4.7 0.7 copy-done.10
  5.3 6.3 %shard_map.64 = (bf16[32,4,32,256]{3,2,1,0:T(8,128)(2,1)S(1)}, s32[2,32]{1,0:T(2,128)S(1)}, s32[32]{0:T(128)S(1)}) custom-call(s32[1]{0:T(128)} %bitcast.1.own_ref, s32[32]{0:T(128)S(1)} %copy-done.10, s32[16,32]{1,0:T(8,128)S(1)} %bitcast.28, s32[16,32]{1,0:T(8,128)S(1)} %bitcast.29, bf16[32,1024]{1,0:T(8,128)(2,1)S(1)} %copy-done.7, ...), custom_call_target="tpu_custom_call" | custom-call | tf_op jit(solution)/shard_map/pallas_call | solution.py:133
  11.6 0.0 copy-start.1
  11.7 35.8 %all_to_all.15.in_ref = bf16[32,4,32,256]{3,2,1,0:T(8,128)(2,1)S(1)} all-to-all(bf16[32,4,32,256]{3,2,1,0:T(8,128)(2,1)S(1)} %get-tuple-element.10), channel_id=1, replica_groups=mesh['depth'=16,'rows'=32] {'rows'}, dimensions={0} | all-to-all | bytes 4194304 | tf_op jit(solution)/shard_map/all_to_all | solution.py:110
  47.5 0.0 copy-done.1
  47.5 1.4 shard_map.65
  48.9 0.0 copy-start.2
  48.9 1.0 copy-done.2
  49.8 4.1 %all-to-all-start.1 = ((bf16[32,2,32,256]{3,2,1,0:T(8,128)(2,1)}), bf16[32,2,32,256]{3,2,1,0:T(8,128)(2,1)S(1)}, u32[]{:S(2)}, u32[]{:S(2)}) async-start(bf16[32,2,32,256]{3,2,1,0:T(8,128)(2,1)} %copy-done.2), calls=%async_computation.1 | async-start | bytes 2097152 | tf_op jit(solution)/shard_map/all_to_all | solution.py:110
  53.9 1.3 shard_map.66.part_ref
  55.2 0.9 copy-done.3
  56.1 15.1 %all-to-all-done.1.in_ref = bf16[32,2,32,256]{3,2,1,0:T(8,128)(2,1)S(1)} async-done(((bf16[32,2,32,256]{3,2,1,0:T(8,128)(2,1)}), bf16[32,2,32,256]{3,2,1,0:T(8,128)(2,1)S(1)}, u32[]{:S(2)}, u32[]{:S(2)}) %all-to-all-start.1) | async-done | bytes 1048608 | tf_op jit(solution)/shard_map/all_to_all | solution.py:110
  71.2 1.1 copy-done.4
  72.4 1.6 %shard_map.67 = bf16[16,4,32,256]{3,2,1,0:T(8,128)(2,1)} custom-call(s32[32]{0:T(128)S(1)} %get-tuple-element.8.mine_ref, bf16[32,2,32,256]{3,2,1,0:T(8,128)(2,1)S(1)} %all-to-all-done.1.in_ref, bf16[16,3,32,256]{3,2,1,0:T(8,128)(2,1)S(1)} %copy-done.4), custom_call_target="tpu_custom_call" | custom-call | tf_op jit(solution)/shard_map/pallas_call | solution.py:159
  74.0 15.2 %all-to-all-start.2 = ((bf16[16,4,32,256]{3,2,1,0:T(8,128)(2,1)}), bf16[16,4,32,256]{3,2,1,0:T(8,128)(2,1)S(1)}, u32[]{:S(2)}, u32[]{:S(2)}) async-start(bf16[16,4,32,256]{3,2,1,0:T(8,128)(2,1)} %shard_map.67), calls=%async_computation.2 | async-start | bytes 2097152 | tf_op jit(solution)/shard_map/all_to_all | solution.py:110
  89.2 0.6 dynamic_slice.4
  90.4 48.6 %all-to-all-done.2 = bf16[16,4,32,256]{3,2,1,0:T(8,128)(2,1)S(1)} async-done(((bf16[16,4,32,256]{3,2,1,0:T(8,128)(2,1)}), bf16[16,4,32,256]{3,2,1,0:T(8,128)(2,1)S(1)}, u32[]{:S(2)}, u32[]{:S(2)}) %all-to-all-start.2) | async-done | bytes 1048608 | tf_op jit(solution)/shard_map/all_to_all | solution.py:110
  139.1 0.3 convolution_bitcast_fusion
  139.3 1.0 fusion.2
  (12 shorter events, 0.0 us)
Async XLA Ops:
  0.0 1.6 %copy-start = (bf16[16,256,256]{2,1,0:T(8,128)(2,1)S(1)}, bf16[16,256,256]{2,1,0:T(8,128)(2,1)}, u32[]{:S(2)}) copy-start(bf16[16,256,256]{2,1,0:T(8,128)(2,1)} %a_ref.3) | copy-start | bytes 6291460
  1.6 0.8 copy-start.5
  2.4 0.8 copy-start.7
  3.3 0.7 copy-start.8
  4.0 0.7 copy-start.9
  4.7 0.7 copy-start.10
  11.6 35.9 %copy-start.1 = (bf16[16,256,256]{2,1,0:T(8,128)(2,1)S(1)}, bf16[16,256,256]{2,1,0:T(8,128)(2,1)}, u32[]{:S(2)}) copy-start(bf16[16,256,256]{2,1,0:T(8,128)(2,1)} %a_ref.3) | copy-start | bytes 6291460
  48.9 1.0 copy-start.2
  49.8 4.1 %copy-start.6 = (bf16[32,1024]{1,0:T(8,128)(2,1)S(1)}, bf16[32,1024]{1,0:T(8,128)(2,1)}, u32[]{:S(2)}) copy-start(bf16[32,1024]{1,0:T(8,128)(2,1)} %dy_ref.3) | copy-start | bytes 196612
  49.8 21.4 %all-to-all-start.1 = ((bf16[32,2,32,256]{3,2,1,0:T(8,128)(2,1)}), bf16[32,2,32,256]{3,2,1,0:T(8,128)(2,1)S(1)}, u32[]{:S(2)}, u32[]{:S(2)}) async-start(bf16[32,2,32,256]{3,2,1,0:T(8,128)(2,1)} %copy-done.2), calls=%async_computation.1 | async-start | bytes 2097152 | tf_op jit(solution)/shard_map/all_to_all | solution.py:110
  55.2 0.9 copy-start.3
  71.2 1.1 copy-start.4
  72.4 16.8 %copy-start.11 = (s32[32]{0:T(128)S(1)}, s32[32]{0:T(128)}, u32[]{:S(2)}) copy-start(s32[32]{0:T(128)} %count_ref.1) | copy-start | bytes 388
  74.0 65.1 %all-to-all-start.2 = ((bf16[16,4,32,256]{3,2,1,0:T(8,128)(2,1)}), bf16[16,4,32,256]{3,2,1,0:T(8,128)(2,1)S(1)}, u32[]{:S(2)}, u32[]{:S(2)}) async-start(bf16[16,4,32,256]{3,2,1,0:T(8,128)(2,1)} %shard_map.67), calls=%async_computation.2 | async-start | bytes 2097152 | tf_op jit(solution)/shard_map/all_to_all | solution.py:110

commit v4 on v3

--- a/solution.py
+++ b/solution.py
@@ -6,8 +6,12 @@
 from jax.sharding import PartitionSpec as P
 
 PAIR_MOST = 2
+LOADS = 4
+STORES = 4
 SMEM = pl.BlockSpec(memory_space=pltpu.SMEM)
 VMEM = pl.BlockSpec(memory_space=pltpu.VMEM)
+ANY = pl.BlockSpec(memory_space=pl.ANY)
+HBM = pl.BlockSpec(memory_space=pltpu.HBM)
 PARAMS = pltpu.CompilerParams(vmem_limit_bytes=12 * 2**20)
 
 
@@ -16,13 +20,29 @@
 
 
 def send_xg_kernel(
-    own_ref, count_ref, col_ref, row_ref, x_ref, dy_ref, a_ref, out_ref, asked_ref, mine_ref, term_ref
+    own_ref, col_ref, row_ref, count_ref, cols_ref, counts_ref, x_ref, dy_ref, a_hbm,
+    out_ref, asked_ref, mine_ref, a_ref, term_ref, code_ref, a_sem, code_sem,
 ):
     slots, width = a_ref.shape[0], a_ref.shape[1]
     peers, most = out_ref.shape[0], out_ref.shape[1] // 2
     row_tiles = x_ref.shape[1] // width
+    loads = []
+    for c in range(LOADS):
+        part = pl.ds(c * (slots // LOADS), slots // LOADS)
+        loads.append(pltpu.make_async_copy(a_hbm.at[part], a_ref.at[part], a_sem.at[c]))
+        loads[c].start()
     own = own_ref[0]
-    my_count = count_ref[own]
+    cols = cols_ref[...]
+    slot_ids = lax.broadcasted_iota(jnp.int32, cols.shape, 0)
+    wanted = (slot_ids < counts_ref[...]) & (cols // row_tiles == own)
+    code = cols % row_tiles + 1
+    first = jnp.max(jnp.where(wanted, (slots - 1 - slot_ids) * 8 + code, 0), axis=0, keepdims=True)
+    last = jnp.max(jnp.where(wanted, slot_ids * 8 + code, 0), axis=0, keepdims=True)
+    two = first // 8 + last // 8 != slots - 1
+    code_ref[0:1] = first % 8
+    code_ref[1:2] = jnp.where(two, last % 8, 0)
+    to_scalars = pltpu.make_async_copy(code_ref, asked_ref, code_sem)
+    to_scalars.start()
     owners = [col_ref[s, own] // row_tiles for s in range(slots)]
     places = []
     for s in range(slots):
@@ -30,25 +50,21 @@
         rank = jnp.int32(0)
         for earlier in range(s):
             rank = rank + jnp.where(owners[earlier] == owners[s], 1, 0)
-        place = jnp.where(s < my_count, owners[s] * most + rank, -1)
+        place = jnp.where(s < count_ref[own], owners[s] * most + rank, -1)
         places.append(place)
         mine_ref[s] = place
         mine_ref[slots + s] = row
-        dy = dy_ref[:, tile_cols(row, width)]
+    to_scalars.wait()
+    for r in range(peers):
+        for k in range(most):
+            t = jnp.maximum(asked_ref[k, r] - 1, 0)
+            out_ref[r, k] = x_ref[:, tile_cols(t, width)]
+            out_ref[r, most + k] = jnp.zeros(out_ref.shape[2:], out_ref.dtype)
+    for s in range(slots):
+        if s % (slots // LOADS) == 0:
+            loads[s // (slots // LOADS)].wait()
+        dy = dy_ref[:, tile_cols(mine_ref[slots + s], width)]
         term_ref[s] = jnp.dot(dy, a_ref[s], preferred_element_type=jnp.float32).astype(out_ref.dtype)
-    for r in range(peers):
-        first, last = jnp.int32(0), jnp.int32(0)
-        for s in range(slots):
-            col = col_ref[s, r]
-            code = jnp.where((col // row_tiles == own) & (s < count_ref[r]), col % row_tiles + 1, 0)
-            last = jnp.where((first > 0) & (code > 0), code, last)
-            first = jnp.where(first > 0, first, code)
-        asked_ref[0, r] = first
-        asked_ref[1, r] = last
-        for k, code in enumerate((first, last)):
-            out_ref[r, k] = x_ref[:, tile_cols(jnp.maximum(code - 1, 0), width)]
-        for k in range(most):
-            out_ref[r, most + k] = jnp.zeros(out_ref.shape[2:], out_ref.dtype)
     for s in range(slots):
         place = places[s]
 
@@ -57,7 +73,7 @@
             out_ref[place // most, most + place % most] = term_ref[s]
 
 
-def h_kernel(mine_ref, asked_ref, in_ref, a_ref, out_ref, acc_ref):
+def h_kernel(mine_ref, asked_ref, in_ref, a_ref, out_hbm, acc_ref, out_ref, out_sem):
     slots = a_ref.shape[0]
     peers, most = out_ref.shape[0], out_ref.shape[1]
     row_tiles = acc_ref.shape[0]
@@ -71,9 +87,17 @@
             sums[t] = sums[t] + jnp.where((row == t) & (mine_ref[s] >= 0), term, 0.0)
     for t in range(row_tiles):
         acc_ref[t] = sums[t].astype(acc_ref.dtype)
+    stores = []
     for r in range(peers):
         for k in range(most):
             out_ref[r, k] = acc_ref[jnp.maximum(asked_ref[k, r] - 1, 0)]
+        if (r + 1) % (peers // STORES) == 0:
+            part = pl.ds(r + 1 - peers // STORES, peers // STORES)
+            copy = pltpu.make_async_copy(out_ref.at[part], out_hbm.at[part], out_sem.at[len(stores)])
+            copy.start()
+            stores.append(copy)
+    for copy in stores:
+        copy.wait()
 
 
 def fill_kernel(mine_ref, asked_ref, in_ref, dy_ref, z_ref, acc_ref):
@@ -97,17 +121,24 @@
         z_ref[s, 2] = in_ref[held // most, held % most]
 
 
-def join_kernel(mine_ref, in_ref, part_ref, z_ref):
+def join_kernel(mine_ref, in_ref, part_ref, z_ref, sem):
+    del part_ref
     most = in_ref.shape[1]
-    ready = part_ref.shape[1]
+    copies = []
     for s in range(z_ref.shape[0]):
         held = jnp.maximum(mine_ref[s], 0)
-        z_ref[s, :ready] = part_ref[s]
-        z_ref[s, ready] = in_ref[held // most, held % most]
+        copies.append(pltpu.make_async_copy(in_ref.at[held // most, held % most], z_ref.at[s, 3], sem.at[s]))
+        copies[s].start()
+    for copy in copies:
+        copy.wait()
 
 
 def exchange(value, axis):
     return lax.all_to_all(value, axis, 0, 0, tiled=True)
+
+
+def far(value):
+    return pltpu.with_memory_space_constraint(value, pltpu.HBM)
 
 
 def near(value):
@@ -125,32 +156,41 @@
     h_type = jax.ShapeDtypeStruct((peers, PAIR_MOST, feat, width), bf16)
     asked_type = jax.ShapeDtypeStruct((PAIR_MOST, peers), jnp.int32)
     mine_type = jax.ShapeDtypeStruct((2 * slots,), jnp.int32)
-    part_type = jax.ShapeDtypeStruct((slots, 3, feat, width), bf16)
     z_type = jax.ShapeDtypeStruct((slots, 4, feat, width), bf16)
     tiles = pltpu.VMEM((row_tiles, feat, width), bf16)
-    adjacency = near(adjacency)
+    node_feat, grad_out, adjacency = far(node_feat), far(grad_out), far(adjacency)
+    cols, counts = tile_col.T, tile_count
 
     xg_out, asked, mine = pl.pallas_call(
         send_xg_kernel,
         out_shape=(xg_type, asked_type, mine_type),
-        in_specs=[SMEM, SMEM, SMEM, SMEM, VMEM, VMEM, VMEM],
+        in_specs=[SMEM, SMEM, SMEM, SMEM, VMEM, VMEM, VMEM, VMEM, ANY],
         out_specs=(VMEM, SMEM, SMEM),
         compiler_params=PARAMS,
-        scratch_shapes=[pltpu.VMEM((slots, feat, width), bf16)],
-    )(own_index[None], tile_count, tile_col.T, tile_row.T, node_feat, grad_out, adjacency)
+        scratch_shapes=[
+            pltpu.VMEM(adjacency.shape, bf16),
+            pltpu.VMEM((slots, feat, width), bf16),
+            pltpu.VMEM(asked_type.shape, jnp.int32),
+            pltpu.SemaphoreType.DMA((LOADS,)),
+            pltpu.SemaphoreType.DMA,
+        ],
+    )(
+        own_index[None], far(cols), far(tile_row.T), far(counts), far(cols), far(counts[None]),
+        node_feat, grad_out, adjacency,
+    )
     xg_in = near(exchange(xg_out, "rows"))
     h_out = pl.pallas_call(
         h_kernel,
         out_shape=h_type,
         in_specs=[SMEM, SMEM, VMEM, VMEM],
-        out_specs=VMEM,
-        compiler_params=PARAMS,
-        scratch_shapes=[tiles],
-    )(mine, asked, xg_in, adjacency)
+        out_specs=HBM,
+        compiler_params=PARAMS,
+        scratch_shapes=[tiles, pltpu.VMEM(h_type.shape, bf16), pltpu.SemaphoreType.DMA((STORES,))],
+    )(mine, asked, xg_in, near(adjacency))
     h_in = near(exchange(h_out, "rows"))
     z_part = pl.pallas_call(
         fill_kernel,
-        out_shape=part_type,
+        out_shape=z_type,
         in_specs=[SMEM, SMEM, VMEM, VMEM],
         out_specs=VMEM,
         compiler_params=PARAMS,
@@ -159,10 +199,12 @@
     z_out = pl.pallas_call(
         join_kernel,
         out_shape=z_type,
-        in_specs=[SMEM, VMEM, VMEM],
-        out_specs=VMEM,
-        compiler_params=PARAMS,
-    )(mine, h_in, near(z_part))
+        in_specs=[SMEM, VMEM, HBM],
+        out_specs=HBM,
+        compiler_params=PARAMS,
+        input_output_aliases={2: 0},
+        scratch_shapes=[pltpu.SemaphoreType.DMA((slots,))],
+    )(mine, h_in, z_part)
     z_in = exchange(z_out, "depth")
     result = jnp.einsum("qfa,qfb->ab", z_in[:, 0], z_in[:, 3], preferred_element_type=jnp.float32)
     result += jnp.einsum("qfa,qfb->ab", z_in[:, 1], z_in[:, 2], preferred_element_type=jnp.float32)

time: 141 us -> 132 us (0.936)
  local copies, waits for them, and re-layouts: 8.94 us -> 1.62 us
    unnamed x24 -> x6, local copies, waits for them, and re-layouts: 8.36 us -> 1.03 us
    pallas_call x1, Pallas kernels: 6.31 us -> 3.73 us  [body(): pl.pallas_call(send_xg_kernel, out_shape=(xg_type, asked_type, mine_type)...]
  transfers between devices with their start and end apart: 2 -> 2, of which waited for: 2 -> 2; matrix products, arithmetic and copies ran while one was open for 0% -> 0% of each run, Pallas kernels for 1% -> 2%
where the time goes in v4:
time: 132 us; the launch traced here: 131 us
  waiting for transfers between devices  63.4 us (48%)
  blocking collectives  35.9 us (27%)
  starting transfers between devices  19.1 us (14%)
  Pallas kernels  9.2 us (7%)
  local copies, waits for them, and re-layouts  1.62 us (1%)
    all_to_all x2, waiting for transfers between devices, exchange(): return lax.all_to_all(value, axis, 0, 0, tiled=True)  63.4 us
    all_to_all x1, blocking collectives, exchange(): return lax.all_to_all(value, axis, 0, 0, tiled=True)  35.9 us
    all_to_all x2, starting transfers between devices, exchange(): return lax.all_to_all(value, axis, 0, 0, tiled=True)  19.1 us
    pallas_call x1, Pallas kernels, body(): pl.pallas_call(send_xg_kernel, out_shape=(xg_type, asked_type, mine_type)...  3.73 us
  transfers between devices with their start and end apart: 2, of which 2 were waited for; matrix products, arithmetic and copies ran while one was open for 0% of the time, Pallas kernels for 2%

profile of v4, /device:TPU:32, one launch (start us, length us, event | category | flops | bytes accessed | tf_op | source)
XLA Modules:
  0.0 131.2 jit_solution(14211496115781239810)
XLA Ops:
  0.0 3.7 %shard_map.64 = (bf16[32,4,32,256]{3,2,1,0:T(8,128)(2,1)S(1)}, s32[2,32]{1,0:T(2,128)S(1)}, s32[32]{0:T(128)S(1)}) custom-call(s32[1]{0:T(128)} %bitcast.1.own_ref, s32[16,32]{1,0:T(8,128)} %bitcast.29, s32[16,32]{1,0:T(8,128)} %bitcast.31, s32[32]{0:T(128)} %count_ref.1, s32[16,32]{1,0:T(8,128)} %bitcast.30, s32[1,32]{1,0:T(1,128)} %bitcast.32, ...), custom_call_target="tpu_custom_call" | custom-call | tf_op jit(solution)/shard_map/pallas_call | solution.py:164
  3.7 0.0 copy-start
  3.8 35.9 %all_to_all.15.in_ref = bf16[32,4,32,256]{3,2,1,0:T(8,128)(2,1)S(1)} all-to-all(bf16[32,4,32,256]{3,2,1,0:T(8,128)(2,1)S(1)} %get-tuple-element.10), channel_id=1, replica_groups=mesh['depth'=16,'rows'=32] {'rows'}, dimensions={0} | all-to-all | bytes 4194304 | tf_op jit(solution)/shard_map/all_to_all | solution.py:137
  39.6 0.0 copy-done
  39.6 1.5 %shard_map.65 = bf16[32,2,32,256]{3,2,1,0:T(8,128)(2,1)S(1)} custom-call(s32[32]{0:T(128)S(1)} %get-tuple-element.8.mine_ref, s32[2,32]{1,0:T(2,128)S(1)} %get-tuple-element.9.asked_ref, bf16[32,4,32,256]{3,2,1,0:T(8,128)(2,1)S(1)} %all_to_all.15.in_ref, bf16[16,256,256]{2,1,0:T(8,128)(2,1)S(1)} %copy-done), custom_call_target="tpu_custom_call" | custom-call | tf_op jit(solution)/shard_map/pallas_call | solution.py:182
  41.1 0.0 copy-start.1
  41.2 1.0 copy-done.1
  42.2 3.9 %all-to-all-start.1 = ((bf16[32,2,32,256]{3,2,1,0:T(8,128)(2,1)}), bf16[32,2,32,256]{3,2,1,0:T(8,128)(2,1)S(1)}, u32[]{:S(2)}, u32[]{:S(2)}) async-start(bf16[32,2,32,256]{3,2,1,0:T(8,128)(2,1)} %copy-done.1), calls=%async_computation.1 | async-start | bytes 2097152 | tf_op jit(solution)/shard_map/all_to_all | solution.py:137
  46.1 2.5 %shard_map.66.part_ref = bf16[16,4,32,256]{3,2,1,0:T(8,128)(2,1)} custom-call(s32[32]{0:T(128)S(1)} %get-tuple-element.8.mine_ref, s32[2,32]{1,0:T(2,128)S(1)} %get-tuple-element.9.asked_ref, bf16[32,4,32,256]{3,2,1,0:T(8,128)(2,1)S(1)} %all_to_all.15.in_ref, bf16[32,1024]{1,0:T(8,128)(2,1)} %dy_ref.3), custom_call_target="tpu_custom_call" | custom-call | tf_op jit(solution)/shard_map/pallas_call | solution.py:191
  48.7 0.0 copy-start.2
  48.7 14.8 %all-to-all-done.1.in_ref = bf16[32,2,32,256]{3,2,1,0:T(8,128)(2,1)S(1)} async-done(((bf16[32,2,32,256]{3,2,1,0:T(8,128)(2,1)}), bf16[32,2,32,256]{3,2,1,0:T(8,128)(2,1)S(1)}, u32[]{:S(2)}, u32[]{:S(2)}) %all-to-all-start.1) | async-done | bytes 1048608 | tf_op jit(solution)/shard_map/all_to_all | solution.py:137
  63.5 1.4 %shard_map.67 = bf16[16,4,32,256]{3,2,1,0:T(8,128)(2,1)} custom-call(s32[32]{0:T(128)S(1)} %get-tuple-element.8.mine_ref, bf16[32,2,32,256]{3,2,1,0:T(8,128)(2,1)S(1)} %all-to-all-done.1.in_ref, bf16[16,4,32,256]{3,2,1,0:T(8,128)(2,1)} %shard_map.66.part_ref), custom_call_target="tpu_custom_call", output_to_operand_aliasing={{}: (2, {})} | custom-call | tf_op jit(solution)/shard_map/pallas_call | solution.py:199
  64.9 15.2 %all-to-all-start.2 = ((bf16[16,4,32,256]{3,2,1,0:T(8,128)(2,1)}), bf16[16,4,32,256]{3,2,1,0:T(8,128)(2,1)S(1)}, u32[]{:S(2)}, u32[]{:S(2)}) async-start(bf16[16,4,32,256]{3,2,1,0:T(8,128)(2,1)} %shard_map.67), calls=%async_computation.2 | async-start | bytes 2097152 | tf_op jit(solution)/shard_map/all_to_all | solution.py:137
  80.1 0.0 copy-done.2
  80.1 0.6 dynamic_slice.4
  81.3 48.6 %all-to-all-done.2 = bf16[16,4,32,256]{3,2,1,0:T(8,128)(2,1)S(1)} async-done(((bf16[16,4,32,256]{3,2,1,0:T(8,128)(2,1)}), bf16[16,4,32,256]{3,2,1,0:T(8,128)(2,1)S(1)}, u32[]{:S(2)}, u32[]{:S(2)}) %all-to-all-start.2) | async-done | bytes 1048608 | tf_op jit(solution)/shard_map/all_to_all | solution.py:137
  130.0 0.3 convolution_bitcast_fusion
  130.2 1.0 fusion.2
Async XLA Ops:
  3.7 35.9 %copy-start = (bf16[16,256,256]{2,1,0:T(8,128)(2,1)S(1)}, bf16[16,256,256]{2,1,0:T(8,128)(2,1)}, u32[]{:S(2)}) copy-start(bf16[16,256,256]{2,1,0:T(8,128)(2,1)} %a_ref.1) | copy-start | bytes 6291460
  41.1 1.0 copy-start.1
  42.2 21.3 %all-to-all-start.1 = ((bf16[32,2,32,256]{3,2,1,0:T(8,128)(2,1)}), bf16[32,2,32,256]{3,2,1,0:T(8,128)(2,1)S(1)}, u32[]{:S(2)}, u32[]{:S(2)}) async-start(bf16[32,2,32,256]{3,2,1,0:T(8,128)(2,1)} %copy-done.1), calls=%async_computation.1 | async-start | bytes 2097152 | tf_op jit(solution)/shard_map/all_to_all | solution.py:137
  48.7 31.4 %copy-start.2 = (s32[32]{0:T(128)S(1)}, s32[32]{0:T(128)}, u32[]{:S(2)}) copy-start(s32[32]{0:T(128)} %count_ref.1) | copy-start | bytes 388
  64.9 65.1 %all-to-all-start.2 = ((bf16[16,4,32,256]{3,2,1,0:T(8,128)(2,1)}), bf16[16,4,32,256]{3,2,1,0:T(8,128)(2,1)S(1)}, u32[]{:S(2)}, u32[]{:S(2)}) async-start(bf16[16,4,32,256]{3,2,1,0:T(8,128)(2,1)} %shard_map.67), calls=%async_computation.2 | async-start | bytes 2097152 | tf_op jit(solution)/shard_map/all_to_all | solution.py:137

commit v5 on v4

v5 whole, which is shorter than its diff:
```python
import jax
import jax.numpy as jnp
from jax import lax
from jax.experimental import pallas as pl
from jax.experimental.pallas import tpu as pltpu
from jax.sharding import PartitionSpec as P

PAIR_MOST = 2
LOADS = 4
STORES = 4
LANES = 128
SMEM = pl.BlockSpec(memory_space=pltpu.SMEM)
VMEM = pl.BlockSpec(memory_space=pltpu.VMEM)
ANY = pl.BlockSpec(memory_space=pl.ANY)
HBM = pl.BlockSpec(memory_space=pltpu.HBM)
PARAMS = pltpu.CompilerParams(vmem_limit_bytes=12 * 2**20)


def tile_cols(index, width):
    return pl.ds(pl.multiple_of(index * width, width), width)


def send_xg_kernel(
    own_ref, col_ref, row_ref, count_ref, cols_ref, counts_ref, x_ref, dy_ref, a_hbm,
    out_ref, asked_ref, mine_ref, spare_ref, a_ref, term_ref, code_ref, a_sem, code_sem,
):
    del spare_ref
    slots, width = a_ref.shape[0], a_ref.shape[1]
    peers, most = out_ref.shape[0], PAIR_MOST
    feat = x_ref.shape[0]
    row_tiles = x_ref.shape[1] // width
    loads = []
    for c in range(LOADS):
        part = pl.ds(c * (slots // LOADS), slots // LOADS)
        loads.append(pltpu.make_async_copy(a_hbm.at[part], a_ref.at[part], a_sem.at[c]))
        loads[c].start()
    own = own_ref[0]
    cols = cols_ref[...]
    slot_ids = lax.broadcasted_iota(jnp.int32, cols.shape, 0)
    wanted = (slot_ids < counts_ref[...]) & (cols // row_tiles == own)
    code = cols % row_tiles + 1
    first = jnp.max(jnp.where(wanted, (slots - 1 - slot_ids) * 8 + code, 0), axis=0, keepdims=True)
    last = jnp.max(jnp.where(wanted, slot_ids * 8 + code, 0), axis=0, keepdims=True)
    two = first // 8 + last // 8 != slots - 1
    code_ref[0:1] = first % 8
    code_ref[1:2] = jnp.where(two, last % 8, 0)
    to_scalars = pltpu.make_async_copy(code_ref, asked_ref, code_sem)
    to_scalars.start()
    owners = [col_ref[s, own] // row_tiles for s in range(slots)]
    for s in range(slots):
        row = row_ref[s, own]
        rank = jnp.int32(0)
        for earlier in range(s):
            rank = rank + jnp.where(owners[earlier] == owners[s], 1, 0)
        mine_ref[s] = jnp.where(s < count_ref[own], owners[s] * most + rank, -1)
        mine_ref[slots + s] = row
    to_scalars.wait()
    for r in range(peers):
        for k in range(most):
            t = jnp.maximum(asked_ref[k, r] - 1, 0)
            out_ref[r, k * feat : (k + 1) * feat] = x_ref[:, tile_cols(t, width)]
    for s in range(slots):
        if s % (slots // LOADS) == 0:
            loads[s // (slots // LOADS)].wait()
        dy = dy_ref[:, tile_cols(mine_ref[slots + s], width)]
        term = jnp.dot(dy, a_ref[s], preferred_element_type=jnp.float32)
        for lanes, half in enumerate(term_ref):
            half[s * feat : (s + 1) * feat] = term[:, lanes * LANES : (lanes + 1) * LANES]
    for r in range(peers):
        for lanes, half in enumerate(term_ref):
            of_feature = half[pl.ds(r, slots, stride=feat)].astype(out_ref.dtype)
            out_ref[r, most * feat :, lanes * LANES : (lanes + 1) * LANES] = of_feature


def h_kernel(
    mine_ref, asked_ref, cols_ref, counts_ref, in_ref, a_ref, spare_ref,
    out_hbm, acc_ref, pick_ref, sum_ref, out_ref, out_sem,
):
    del spare_ref
    slots = a_ref.shape[0]
    peers, most = out_ref.shape[0], PAIR_MOST
    row_tiles, feat, width = acc_ref.shape
    sums = [jnp.zeros((feat, width), jnp.float32) for _ in range(row_tiles)]
    for s in range(slots):
        held = jnp.maximum(mine_ref[s], 0)
        row = mine_ref[slots + s]
        x = in_ref[held // most, pl.ds(pl.multiple_of(held % most * feat, feat), feat)]
        term = lax.dot_general(x, a_ref[s], (((1,), (1,)), ((), ())), preferred_element_type=jnp.float32)
        for t in range(row_tiles):
            sums[t] = sums[t] + jnp.where((row == t) & (mine_ref[s] >= 0), term, 0.0)
    for t in range(row_tiles):
        acc_ref[t] = sums[t].astype(acc_ref.dtype)
    cols = cols_ref[...]
    live = lax.broadcasted_iota(jnp.int32, cols.shape, 0) < counts_ref[...]
    cols = jnp.where(live, cols, -1)
    tile_ids = lax.broadcasted_iota(jnp.int32, (slots, peers * row_tiles), 1)
    for r in range(peers):
        pick_ref[r * slots : (r + 1) * slots] = (cols[:, r : r + 1] == tile_ids).astype(pick_ref.dtype)
    terms = in_ref[:, most * feat :].reshape(peers * slots, width)
    sum_ref[: peers * row_tiles] = lax.dot_general(
        pick_ref[...], terms, (((0,), (0,)), ((), ())), preferred_element_type=jnp.float32
    )
    sum_ref[peers * row_tiles :] = jnp.zeros((row_tiles, width), jnp.float32)
    stores = []
    for r in range(peers):
        for k in range(most):
            out_ref[r, k * feat : (k + 1) * feat] = acc_ref[jnp.maximum(asked_ref[k, r] - 1, 0)]
        of_tiles = sum_ref[r * row_tiles : (r + 2) * row_tiles]
        out_ref[r, most * feat :] = of_tiles.astype(out_ref.dtype)
        if (r + 1) % (peers // STORES) == 0:
            part = pl.ds(r + 1 - peers // STORES, peers // STORES)
            copy = pltpu.make_async_copy(out_ref.at[part], out_hbm.at[part], out_sem.at[len(stores)])
            copy.start()
            stores.append(copy)
    for copy in stores:
        copy.wait()


def fill_kernel(mine_ref, in_ref, dy_ref, z_ref):
    slots, _, feat, width = z_ref.shape
    for s in range(slots):
        held = jnp.maximum(mine_ref[s], 0)
        z_ref[s, 0] = dy_ref[:, tile_cols(mine_ref[slots + s], width)]
        z_ref[s, 2] = in_ref[held // PAIR_MOST, pl.ds(pl.multiple_of(held % PAIR_MOST * feat, feat), feat)]


def join_kernel(mine_ref, in_ref, part_ref, z_ref, rows_ref, g_ref, sem):
    del part_ref
    peers, most = in_ref.shape[0], PAIR_MOST
    slots = z_ref.shape[0]
    row_tiles, feat, _ = g_ref.shape
    copies = []
    for s in range(slots):
        held = jnp.maximum(mine_ref[s], 0)
        tile = in_ref.at[held // most, pl.ds(pl.multiple_of(held % most * feat, feat), feat)]
        copies.append(pltpu.make_async_copy(tile, z_ref.at[s, 3], sem.at[s]))
        copies[s].start()
    step = in_ref.shape[1] - most * feat
    for r in range(peers):
        of_tiles = in_ref[r, most * feat :].astype(jnp.float32)
        for lanes, half in enumerate(rows_ref):
            half[r * step : (r + 1) * step] = of_tiles[:, lanes * LANES : (lanes + 1) * LANES]
    for t in range(row_tiles):
        for lanes, half in enumerate(rows_ref):
            of_tile = half[pl.ds(t, feat, stride=step)].astype(g_ref.dtype)
            g_ref[t, :, lanes * LANES : (lanes + 1) * LANES] = of_tile
    for s in range(slots):
        copies.append(pltpu.make_async_copy(g_ref.at[mine_ref[slots + s]], z_ref.at[s, 1], sem.at[slots + s]))
        copies[slots + s].start()
    for copy in copies:
        copy.wait()


def exchange(value, axis):
    return lax.all_to_all(value, axis, 0, 0, tiled=True)


def far(value):
    return pltpu.with_memory_space_constraint(value, pltpu.HBM)


def near(value):
    return pltpu.with_memory_space_constraint(value, pltpu.VMEM)


def body(node_feat, grad_out, adjacency, tile_count, tile_row, tile_col):
    slots, width = adjacency.shape[0], adjacency.shape[1]
    feat = node_feat.shape[0]
    row_tiles = node_feat.shape[1] // width
    own_index = lax.axis_index("rows")
    peers = lax.axis_size("rows")
    bf16 = node_feat.dtype
    wanted_rows = PAIR_MOST * feat
    xg_type = jax.ShapeDtypeStruct((peers, wanted_rows + slots, width), bf16)
    hg_type = jax.ShapeDtypeStruct((peers, wanted_rows + 2 * row_tiles, width), bf16)
    asked_type = jax.ShapeDtypeStruct((PAIR_MOST, peers), jnp.int32)
    mine_type = jax.ShapeDtypeStruct((2 * slots,), jnp.int32)
    z_type = jax.ShapeDtypeStruct((slots, 4, feat, width), bf16)
    tiles = pltpu.VMEM((row_tiles, feat, width), bf16)
    node_feat, grad_out, adjacency = far(node_feat), far(grad_out), far(adjacency)
    cols, counts = tile_col.T, tile_count[None]

    xg_out, asked, mine, spare = pl.pallas_call(
        send_xg_kernel,
        out_shape=(xg_type, asked_type, mine_type, hg_type),
        in_specs=[SMEM, SMEM, SMEM, SMEM, VMEM, VMEM, VMEM, VMEM, ANY],
        out_specs=(VMEM, SMEM, SMEM, HBM),
        compiler_params=PARAMS,
        scratch_shapes=[
            pltpu.VMEM(adjacency.shape, bf16),
            [pltpu.VMEM((slots * feat, LANES), jnp.float32)] * (width // LANES),
            pltpu.VMEM(asked_type.shape, jnp.int32),
            pltpu.SemaphoreType.DMA((LOADS,)),
            pltpu.SemaphoreType.DMA,
        ],
    )(
        own_index[None], far(cols), far(tile_row.T), far(tile_count), far(cols), far(counts),
        node_feat, grad_out, adjacency,
    )
    xg_in = near(exchange(xg_out, "rows"))
    hg_out = pl.pallas_call(
        h_kernel,
        out_shape=hg_type,
        in_specs=[SMEM, SMEM, VMEM, VMEM, VMEM, VMEM, HBM],
        out_specs=HBM,
        input_output_aliases={6: 0},
        compiler_params=PARAMS,
        scratch_shapes=[
            tiles,
            pltpu.VMEM((peers * slots, peers * row_tiles), bf16),
            pltpu.VMEM(((peers + 1) * row_tiles, width), jnp.float32),
            pltpu.VMEM(hg_type.shape, bf16),
            pltpu.SemaphoreType.DMA((STORES,)),
        ],
    )(mine, asked, near(cols), near(counts), xg_in, near(adjacency), far(spare))
    hg_in = near(exchange(hg_out, "rows"))
    z_part = pl.pallas_call(
        fill_kernel,
        out_shape=z_type,
        in_specs=[SMEM, VMEM, VMEM],
        out_specs=VMEM,
        compiler_params=PARAMS,
    )(mine, xg_in, grad_out)
    z_out = pl.pallas_call(
        join_kernel,
        out_shape=z_type,
        in_specs=[SMEM, VMEM, HBM],
        out_specs=HBM,
        compiler_params=PARAMS,
        input_output_aliases={2: 0},
        scratch_shapes=[
            [pltpu.VMEM((peers * 2 * row_tiles, LANES), jnp.float32)] * (width // LANES),
            tiles,
            pltpu.SemaphoreType.DMA((2 * slots,)),
        ],
    )(mine, hg_in, z_part)
    z_in = exchange(z_out, "depth")
    result = jnp.einsum("qfa,qfb->ab", z_in[:, 0], z_in[:, 3], preferred_element_type=jnp.float32)
    result += jnp.einsum("qfa,qfb->ab", z_in[:, 1], z_in[:, 2], preferred_element_type=jnp.float32)
    count = lax.dynamic_index_in_dim(tile_count, own_index, 0, keepdims=False)
    return jnp.where(lax.axis_index("depth") < count, result, 0.0)[None, None]


def solution(mesh):
    in_specs = (P("depth", "rows"), P("depth", "rows"), P("rows", None, None), P(), P(), P())
    out_specs = P("rows", "depth", None, None)
    return jax.shard_map(body, mesh=mesh, in_specs=in_specs, out_specs=out_specs, check_vma=False)
```

time: 132 us -> 125 us (0.947)
  the two profiles are of different devices: /device:TPU:32 before, /device:TPU:2 now
where the time goes in v5:
time: 125 us
  waiting for transfers between devices  64.7 us (52%)
  blocking collectives  27.7 us (22%)
  starting transfers between devices  19 us (15%)
  Pallas kernels  9.58 us (8%)
  local copies, waits for them, and re-layouts  1.62 us (1%)
    all_to_all x2, waiting for transfers between devices, exchange(): return lax.all_to_all(value, axis, 0, 0, tiled=True)  64.7 us
    all_to_all x1, blocking collectives, exchange(): return lax.all_to_all(value, axis, 0, 0, tiled=True)  27.7 us
    all_to_all x2, starting transfers between devices, exchange(): return lax.all_to_all(value, axis, 0, 0, tiled=True)  19 us
    pallas_call x1, Pallas kernels, body(): pl.pallas_call(send_xg_kernel, out_shape=(xg_type, asked_type, mine_type,...  3.54 us
  transfers between devices with their start and end apart: 2, of which 2 were waited for; matrix products, arithmetic and copies ran while one was open for 0% of the time, Pallas kernels for 2%

profile of v5, /device:TPU:2, one launch (start us, length us, event | category | flops | bytes accessed | tf_op | source)
XLA Modules:
  0.0 124.6 jit_solution(4771389925410252155)
XLA Ops:
  0.0 3.5 %shard_map.64 = (bf16[32,80,256]{2,1,0:T(8,128)(2,1)S(1)}, s32[2,32]{1,0:T(2,128)S(1)}, s32[32]{0:T(128)S(1)}, bf16[32,72,256]{2,1,0:T(8,128)(2,1)S(1)}) custom-call(s32[1]{0:T(128)} %bitcast.1.own_ref, s32[16,32]{1,0:T(8,128)} %bitcast.29, s32[16,32]{1,0:T(8,128)} %bitcast.34, s32[32]{0:T(128)} %count_ref.1, s32[16,32]{1,0:T(8,128)} %bitcast.30, ...), custom_call_target="tpu_custom_call" | custom-call | tf_op jit(solution)/shard_map/pallas_call | solution.py:183
  3.6 0.0 copy-start.1
  3.6 1.0 copy-done.1
  4.6 0.0 copy-start
  4.6 0.0 copy-start.2
  4.6 0.0 copy-start.3
  4.6 27.7 %all_to_all.15.in_ref = bf16[32,80,256]{2,1,0:T(8,128)(2,1)S(1)} all-to-all(bf16[32,80,256]{2,1,0:T(8,128)(2,1)S(1)} %get-tuple-element.11), channel_id=1, replica_groups=mesh['depth'=16,'rows'=32] {'rows'}, dimensions={0} | all-to-all | bytes 2621440 | tf_op jit(solution)/shard_map/all_to_all | solution.py:155
  32.3 0.0 copy-done
  32.3 0.0 copy-done.2
  32.3 0.0 copy-done.3
  32.3 2.4 %shard_map.65 = bf16[32,72,256]{2,1,0:T(8,128)(2,1)} custom-call(s32[32]{0:T(128)S(1)} %get-tuple-element.9.mine_ref, s32[2,32]{1,0:T(2,128)S(1)} %get-tuple-element.10.asked_ref, s32[16,32]{1,0:T(8,128)S(1)} %bitcast.31, s32[1,32]{1,0:T(1,128)S(1)} %bitcast.33, bf16[32,80,256]{2,1,0:T(8,128)(2,1)S(1)} %all_to_all.15.in_ref, ...), custom_call_target="tpu_custom_call", output_to_operand_aliasing={{}: (6, {})} | custom-call | tf_op jit(solution)/shard_map/pallas_call | solution.py:201
  34.8 5.1 %all-to-all-start.1 = ((bf16[32,72,256]{2,1,0:T(8,128)(2,1)}), bf16[32,72,256]{2,1,0:T(8,128)(2,1)S(1)}, u32[]{:S(2)}, u32[]{:S(2)}) async-start(bf16[32,72,256]{2,1,0:T(8,128)(2,1)} %shard_map.65), calls=%async_computation.1 | async-start | bytes 2359296 | tf_op jit(solution)/shard_map/all_to_all | solution.py:155
  39.8 1.9 %shard_map.66.part_ref = bf16[16,4,32,256]{3,2,1,0:T(8,128)(2,1)} custom-call(s32[32]{0:T(128)S(1)} %get-tuple-element.9.mine_ref, bf16[32,80,256]{2,1,0:T(8,128)(2,1)S(1)} %all_to_all.15.in_ref, bf16[32,1024]{1,0:T(8,128)(2,1)} %dy_ref.3), custom_call_target="tpu_custom_call" | custom-call | tf_op jit(solution)/shard_map/pallas_call | solution.py:217
  41.8 15.7 %all-to-all-done.1.in_ref = bf16[32,72,256]{2,1,0:T(8,128)(2,1)S(1)} async-done(((bf16[32,72,256]{2,1,0:T(8,128)(2,1)}), bf16[32,72,256]{2,1,0:T(8,128)(2,1)S(1)}, u32[]{:S(2)}, u32[]{:S(2)}) %all-to-all-start.1) | async-done | bytes 1179680 | tf_op jit(solution)/shard_map/all_to_all | solution.py:155
  57.5 1.7 %shard_map.67 = bf16[16,4,32,256]{3,2,1,0:T(8,128)(2,1)} custom-call(s32[32]{0:T(128)S(1)} %get-tuple-element.9.mine_ref, bf16[32,72,256]{2,1,0:T(8,128)(2,1)S(1)} %all-to-all-done.1.in_ref, bf16[16,4,32,256]{3,2,1,0:T(8,128)(2,1)} %shard_map.66.part_ref), custom_call_target="tpu_custom_call", output_to_operand_aliasing={{}: (2, {})} | custom-call | tf_op jit(solution)/shard_map/pallas_call | solution.py:224
  59.1 14.0 %all-to-all-start.2 = ((bf16[16,4,32,256]{3,2,1,0:T(8,128)(2,1)}), bf16[16,4,32,256]{3,2,1,0:T(8,128)(2,1)S(1)}, u32[]{:S(2)}, u32[]{:S(2)}) async-start(bf16[16,4,32,256]{3,2,1,0:T(8,128)(2,1)} %shard_map.67), calls=%async_computation.2 | async-start | bytes 2097152 | tf_op jit(solution)/shard_map/all_to_all | solution.py:155
  73.1 0.6 dynamic_slice.4
  74.3 49.0 %all-to-all-done.2 = bf16[16,4,32,256]{3,2,1,0:T(8,128)(2,1)S(1)} async-done(((bf16[16,4,32,256]{3,2,1,0:T(8,128)(2,1)}), bf16[16,4,32,256]{3,2,1,0:T(8,128)(2,1)S(1)}, u32[]{:S(2)}, u32[]{:S(2)}) %all-to-all-start.2) | async-done | bytes 1048608 | tf_op jit(solution)/shard_map/all_to_all | solution.py:155
  123.3 0.3 convolution_bitcast_fusion
  123.6 1.0 fusion.2
Async XLA Ops:
  3.6 1.0 copy-start.1
  4.6 27.7 %copy-start = (bf16[16,256,256]{2,1,0:T(8,128)(2,1)S(1)}, bf16[16,256,256]{2,1,0:T(8,128)(2,1)}, u32[]{:S(2)}) copy-start(bf16[16,256,256]{2,1,0:T(8,128)(2,1)} %a_ref.1) | copy-start | bytes 6291460
  4.6 27.7 %copy-start.2 = (s32[32,16]{0,1:T(8,128)S(1)}, s32[32,16]{0,1:T(8,128)}, u32[]{:S(2)}) copy-start(s32[32,16]{0,1:T(8,128)} %param.11) | copy-start | bytes 6148
  4.6 27.7 %copy-start.3 = (s32[32]{0:T(128)S(1)}, s32[32]{0:T(128)}, u32[]{:S(2)}) copy-start(s32[32]{0:T(128)} %count_ref.1) | copy-start | bytes 388
  34.8 22.7 %all-to-all-start.1 = ((bf16[32,72,256]{2,1,0:T(8,128)(2,1)}), bf16[32,72,256]{2,1,0:T(8,128)(2,1)S(1)}, u32[]{:S(2)}, u32[]{:S(2)}) async-start(bf16[32,72,256]{2,1,0:T(8,128)(2,1)} %shard_map.65), calls=%async_computation.1 | async-start | bytes 2359296 | tf_op jit(solution)/shard_map/all_to_all | solution.py:155
  59.1 64.2 %all-to-all-start.2 = ((bf16[16,4,32,256]{3,2,1,0:T(8,128)(2,1)}), bf16[16,4,32,256]{3,2,1,0:T(8,128)(2,1)S(1)}, u32[]{:S(2)}, u32[]{:S(2)}) async-start(bf16[16,4,32,256]{3,2,1,0:T(8,128)(2,1)} %shard_map.67), calls=%async_computation.2 | async-start | bytes 2097152 | tf_op jit(solution)/shard_map/all_to_all | solution.py:155

commit v6 on v5

--- a/solution.py
+++ b/solution.py
@@ -9,6 +9,7 @@
 LOADS = 4
 STORES = 4
 LANES = 128
+GROUP = 4
 SMEM = pl.BlockSpec(memory_space=pltpu.SMEM)
 VMEM = pl.BlockSpec(memory_space=pltpu.VMEM)
 ANY = pl.BlockSpec(memory_space=pl.ANY)
@@ -22,9 +23,8 @@
 
 def send_xg_kernel(
     own_ref, col_ref, row_ref, count_ref, cols_ref, counts_ref, x_ref, dy_ref, a_hbm,
-    out_ref, asked_ref, mine_ref, spare_ref, a_ref, term_ref, code_ref, a_sem, code_sem,
+    out_ref, asked_ref, mine_ref, dy0_ref, dy1_ref, dy2_ref, dy3_ref, a_ref, term_ref, code_ref, a_sem, code_sem,
 ):
-    del spare_ref
     slots, width = a_ref.shape[0], a_ref.shape[1]
     peers, most = out_ref.shape[0], PAIR_MOST
     feat = x_ref.shape[0]
@@ -54,6 +54,10 @@
             rank = rank + jnp.where(owners[earlier] == owners[s], 1, 0)
         mine_ref[s] = jnp.where(s < count_ref[own], owners[s] * most + rank, -1)
         mine_ref[slots + s] = row
+    for step, part_ref in enumerate((dy0_ref, dy1_ref, dy2_ref, dy3_ref)):
+        group = own_ref[1] // GROUP ^ step
+        for e in range(GROUP):
+            part_ref[e] = dy_ref[:, tile_cols(row_ref[group * GROUP + e, own], width)]
     to_scalars.wait()
     for r in range(peers):
         for k in range(most):
@@ -73,10 +77,9 @@
 
 
 def h_kernel(
-    mine_ref, asked_ref, cols_ref, counts_ref, in_ref, a_ref, spare_ref,
+    mine_ref, asked_ref, cols_ref, counts_ref, in_ref, a_ref,
     out_hbm, acc_ref, pick_ref, sum_ref, out_ref, out_sem,
 ):
-    del spare_ref
     slots = a_ref.shape[0]
     peers, most = out_ref.shape[0], PAIR_MOST
     row_tiles, feat, width = acc_ref.shape
@@ -116,12 +119,23 @@
         copy.wait()
 
 
-def fill_kernel(mine_ref, in_ref, dy_ref, z_ref):
-    slots, _, feat, width = z_ref.shape
+def turn_kernel(own_ref, in0_ref, in1_ref, in2_ref, in3_ref, out0_ref, out1_ref, out2_ref, out3_ref):
+    for e, out_ref in enumerate((out0_ref, out1_ref, out2_ref, out3_ref)):
+        for g, in_ref in enumerate((in0_ref, in1_ref, in2_ref, in3_ref)):
+            out_ref[g] = in_ref[own_ref[1] % GROUP ^ e]
+
+
+def order_kernel(own_ref, in0_ref, in1_ref, in2_ref, in3_ref, out_ref):
+    for e, in_ref in enumerate((in0_ref, in1_ref, in2_ref, in3_ref)):
+        for g in range(GROUP):
+            out_ref[own_ref[1] ^ (g * GROUP + e)] = in_ref[g]
+
+
+def fill_kernel(mine_ref, in_ref, z_ref):
+    slots, _, feat, _ = z_ref.shape
     for s in range(slots):
         held = jnp.maximum(mine_ref[s], 0)
-        z_ref[s, 0] = dy_ref[:, tile_cols(mine_ref[slots + s], width)]
-        z_ref[s, 2] = in_ref[held // PAIR_MOST, pl.ds(pl.multiple_of(held % PAIR_MOST * feat, feat), feat)]
+        z_ref[s, 1] = in_ref[held // PAIR_MOST, pl.ds(pl.multiple_of(held % PAIR_MOST * feat, feat), feat)]
 
 
 def join_kernel(mine_ref, in_ref, part_ref, z_ref, rows_ref, g_ref, sem):
@@ -133,7 +147,7 @@
     for s in range(slots):
         held = jnp.maximum(mine_ref[s], 0)
         tile = in_ref.at[held // most, pl.ds(pl.multiple_of(held % most * feat, feat), feat)]
-        copies.append(pltpu.make_async_copy(tile, z_ref.at[s, 3], sem.at[s]))
+        copies.append(pltpu.make_async_copy(tile, z_ref.at[s, 2], sem.at[s]))
         copies[s].start()
     step = in_ref.shape[1] - most * feat
     for r in range(peers):
@@ -145,7 +159,7 @@
             of_tile = half[pl.ds(t, feat, stride=step)].astype(g_ref.dtype)
             g_ref[t, :, lanes * LANES : (lanes + 1) * LANES] = of_tile
     for s in range(slots):
-        copies.append(pltpu.make_async_copy(g_ref.at[mine_ref[slots + s]], z_ref.at[s, 1], sem.at[slots + s]))
+        copies.append(pltpu.make_async_copy(g_ref.at[mine_ref[slots + s]], z_ref.at[s, 0], sem.at[slots + s]))
         copies[slots + s].start()
     for copy in copies:
         copy.wait()
@@ -153,6 +167,17 @@
 
 def exchange(value, axis):
     return lax.all_to_all(value, axis, 0, 0, tiled=True)
+
+
+def swap(value, step):
+    if step == 0:
+        return value
+    places = range(lax.axis_size("depth"))
+    return lax.ppermute(value, "depth", [(place, place ^ step) for place in places])
+
+
+def hbm(kind):
+    return pltpu.HBM(kind.shape, kind.dtype)
 
 
 def far(value):
@@ -175,16 +200,19 @@
     hg_type = jax.ShapeDtypeStruct((peers, wanted_rows + 2 * row_tiles, width), bf16)
     asked_type = jax.ShapeDtypeStruct((PAIR_MOST, peers), jnp.int32)
     mine_type = jax.ShapeDtypeStruct((2 * slots,), jnp.int32)
-    z_type = jax.ShapeDtypeStruct((slots, 4, feat, width), bf16)
+    z_type = jax.ShapeDtypeStruct((slots, 3, feat, width), bf16)
     tiles = pltpu.VMEM((row_tiles, feat, width), bf16)
+    slot_type = jax.ShapeDtypeStruct((slots, feat, width), bf16)
     node_feat, grad_out, adjacency = far(node_feat), far(grad_out), far(adjacency)
     cols, counts = tile_col.T, tile_count[None]
 
-    xg_out, asked, mine, spare = pl.pallas_call(
+    four_type = jax.ShapeDtypeStruct((GROUP, feat, width), bf16)
+    own = jnp.stack([own_index, lax.axis_index("depth")])
+    xg_out, asked, mine, *dy_parts = pl.pallas_call(
         send_xg_kernel,
-        out_shape=(xg_type, asked_type, mine_type, hg_type),
+        out_shape=(hbm(xg_type), hbm(asked_type), hbm(mine_type)) + (hbm(four_type),) * GROUP,
         in_specs=[SMEM, SMEM, SMEM, SMEM, VMEM, VMEM, VMEM, VMEM, ANY],
-        out_specs=(VMEM, SMEM, SMEM, HBM),
+        out_specs=(VMEM, SMEM, SMEM) + (VMEM,) * GROUP,
         compiler_params=PARAMS,
         scratch_shapes=[
             pltpu.VMEM(adjacency.shape, bf16),
@@ -194,16 +222,17 @@
             pltpu.SemaphoreType.DMA,
         ],
     )(
-        own_index[None], far(cols), far(tile_row.T), far(tile_count), far(cols), far(counts),
+        own, far(cols), far(tile_row.T), far(tile_count), far(cols), far(counts),
         node_feat, grad_out, adjacency,
     )
-    xg_in = near(exchange(xg_out, "rows"))
+    xg_in = exchange(xg_out, "rows")
+    dy_parts = [swap(part, GROUP * step) for step, part in enumerate(dy_parts)]
+    xg_in, *dy_parts = lax.optimization_barrier((xg_in, *dy_parts))
     hg_out = pl.pallas_call(
         h_kernel,
-        out_shape=hg_type,
-        in_specs=[SMEM, SMEM, VMEM, VMEM, VMEM, VMEM, HBM],
+        out_shape=hbm(hg_type),
+        in_specs=[SMEM, SMEM, VMEM, VMEM, VMEM, VMEM],
         out_specs=HBM,
-        input_output_aliases={6: 0},
         compiler_params=PARAMS,
         scratch_shapes=[
             tiles,
@@ -212,15 +241,31 @@
             pltpu.VMEM(hg_type.shape, bf16),
             pltpu.SemaphoreType.DMA((STORES,)),
         ],
-    )(mine, asked, near(cols), near(counts), xg_in, near(adjacency), far(spare))
-    hg_in = near(exchange(hg_out, "rows"))
+    )(far(mine), far(asked), near(cols), near(counts), near(xg_in), near(adjacency))
+    hg_in = exchange(hg_out, "rows")
+    dy_parts = pl.pallas_call(
+        turn_kernel,
+        out_shape=(hbm(four_type),) * GROUP,
+        in_specs=[SMEM] + [VMEM] * GROUP,
+        out_specs=(VMEM,) * GROUP,
+        compiler_params=PARAMS,
+    )(own, *dy_parts)
+    dy_parts = [swap(part, step) for step, part in enumerate(dy_parts)]
+    hg_in, *dy_parts = lax.optimization_barrier((hg_in, *dy_parts))
+    dy = pl.pallas_call(
+        order_kernel,
+        out_shape=slot_type,
+        in_specs=[SMEM] + [VMEM] * GROUP,
+        out_specs=VMEM,
+        compiler_params=PARAMS,
+    )(own, *dy_parts)
     z_part = pl.pallas_call(
         fill_kernel,
         out_shape=z_type,
-        in_specs=[SMEM, VMEM, VMEM],
+        in_specs=[SMEM, VMEM],
         out_specs=VMEM,
         compiler_params=PARAMS,
-    )(mine, xg_in, grad_out)
+    )(mine, near(xg_in))
     z_out = pl.pallas_call(
         join_kernel,
         out_shape=z_type,
@@ -233,10 +278,10 @@
             tiles,
             pltpu.SemaphoreType.DMA((2 * slots,)),
         ],
-    )(mine, hg_in, z_part)
+    )(mine, near(hg_in), z_part)
     z_in = exchange(z_out, "depth")
-    result = jnp.einsum("qfa,qfb->ab", z_in[:, 0], z_in[:, 3], preferred_element_type=jnp.float32)
-    result += jnp.einsum("qfa,qfb->ab", z_in[:, 1], z_in[:, 2], preferred_element_type=jnp.float32)
+    result = jnp.einsum("qfa,qfb->ab", dy, z_in[:, 2], preferred_element_type=jnp.float32)
+    result += jnp.einsum("qfa,qfb->ab", z_in[:, 0], z_in[:, 1], preferred_element_type=jnp.float32)
     count = lax.dynamic_index_in_dim(tile_count, own_index, 0, keepdims=False)
     return jnp.where(lax.axis_index("depth") < count, result, 0.0)[None, None]
 

time: 125 us -> 126 us (level)
  the two profiles are of different devices: /device:TPU:2 before, /device:TPU:34 now
where the time goes in v6:
time: 126 us; the launch traced here: 125 us
  starting transfers between devices  56.1 us (45%)
  waiting for transfers between devices  53.7 us (43%)
  Pallas kernels  11.9 us (9%)
  local copies, waits for them, and re-layouts  1.27 us (1%)
    all_to_all x3, waiting for transfers between devices, exchange(): return lax.all_to_all(value, axis, 0, 0, tiled=True)  41 us
    ppermute x6, starting transfers between devices, swap(): lax.ppermute(value, 'depth', [(place, place ^ step) for place in places])  30.4 us
    all_to_all x3, starting transfers between devices, exchange(): return lax.all_to_all(value, axis, 0, 0, tiled=True)  25.7 us
    ppermute x6, waiting for transfers between devices, swap(): lax.ppermute(value, 'depth', [(place, place ^ step) for place in places])  12.6 us
    pallas_call x1, Pallas kernels, body(): pl.pallas_call(send_xg_kernel, out_shape=(hbm(xg_type), hbm(asked_type),...  4.33 us
    pallas_call x1, Pallas kernels, body(): pl.pallas_call(h_kernel, out_shape=hbm(hg_type), in_specs=[SMEM, SMEM, VM...  2.6 us
  transfers between devices with their start and end apart: 9, of which 5 were waited for; matrix products, arithmetic and copies ran while one was open for 0% of the time, Pallas kernels for 3%

profile of v6, /device:TPU:34, one launch (start us, length us, event | category | flops | bytes accessed | tf_op | source)
XLA Modules:
  0.0 125.1 jit_solution(9944866402391443592)
XLA Ops:
  0.1 4.3 %shard_map.64 = (bf16[32,80,256]{2,1,0:T(8,128)(2,1)}, s32[2,32]{1,0:T(2,128)}, s32[32]{0:T(128)}, bf16[4,32,256]{2,1,0:T(8,128)(2,1)}, bf16[4,32,256]{2,1,0:T(8...) custom-call(s32[2]{0:T(128)S(1)} %pad_add_fusion.own_ref, s32[16,32]{1,0:T(8,128)} %bitcast.28, ...), custom_call_target="tpu_custom_call" | custom-call | tf_op jit(solution)/shard_map/pallas_call | solution.py:211
  4.5 7.8 %all-to-all-start = ((bf16[32,80,256]{2,1,0:T(8,128)(2,1)}), bf16[32,80,256]{2,1,0:T(8,128)(2,1)S(1)}, u32[]{:S(2)}, u32[]{:S(2)}) async-start(bf16[32,80,256]{2,1,0:T(8,128)(2,1)} %get-tuple-element.28), calls=%async_computation | async-start | bytes 2621440 | tf_op jit(solution)/shard_map/all_to_all | solution.py:169
  12.2 9.1 %collective-permute-start = (bf16[4,32,256]{2,1,0:T(8,128)(2,1)}, bf16[4,32,256]{2,1,0:T(8,128)(2,1)S(1)}, u32[]{:S(2)}, u32[]{:S(2)}) collective-permute-start(bf16[4,32,256]{2,1,0:T(8,128)(2,1)} %get-tuple-element.30), channel_id=1, source_target_pairs={{0,128},{32,160},{64,192},{96,224},{128,0},{160,32},{192,64},{224,... | collective-permute-start | bytes 196616 | tf_op jit(solution)/shard_map/ppermute | solution.py:176
  21.3 10.0 %collective-permute-start.1 = (bf16[4,32,256]{2,1,0:T(8,128)(2,1)}, bf16[4,32,256]{2,1,0:T(8,128)(2,1)S(1)}, u32[]{:S(2)}, u32[]{:S(2)}) collective-permute-start(bf16[4,32,256]{2,1,0:T(8,128)(2,1)} %get-tuple-element.31), channel_id=1, source_target_pairs={{0,256},{32,288},{64,320},{96,352},{128,384},{160,416},{192,448},{... | collective-permute-start | bytes 196616 | tf_op jit(solution)/shard_map/ppermute | solution.py:176
  31.3 1.9 %collective-permute-start.2 = (bf16[4,32,256]{2,1,0:T(8,128)(2,1)}, bf16[4,32,256]{2,1,0:T(8,128)(2,1)S(1)}, u32[]{:S(2)}, u32[]{:S(2)}) collective-permute-start(bf16[4,32,256]{2,1,0:T(8,128)(2,1)} %get-tuple-element.32), channel_id=1, source_target_pairs={{0,384},{32,416},{64,448},{96,480},{128,256},{160,288},{192,320},{... | collective-permute-start | bytes 196616 | tf_op jit(solution)/shard_map/ppermute | solution.py:176
  33.3 3.3 %collective-permute-done.1.in2_ref = bf16[4,32,256]{2,1,0:T(8,128)(2,1)S(1)} collective-permute-done((bf16[4,32,256]{2,1,0:T(8,128)(2,1)}, bf16[4,32,256]{2,1,0:T(8,128)(2,1)S(1)}, u32[]{:S(2)}, u32[]{:S(2)}) %collective-permute-start.1) | collective-permute-done | bytes 65568 | tf_op jit(solution)/shard_map/ppermute | solution.py:176
  36.6 6.9 %collective-permute-done.2.in3_ref = bf16[4,32,256]{2,1,0:T(8,128)(2,1)S(1)} collective-permute-done((bf16[4,32,256]{2,1,0:T(8,128)(2,1)}, bf16[4,32,256]{2,1,0:T(8,128)(2,1)S(1)}, u32[]{:S(2)}, u32[]{:S(2)}) %collective-permute-start.2) | collective-permute-done | bytes 65568 | tf_op jit(solution)/shard_map/ppermute | solution.py:176
  43.5 0.6 copy-done.4
  44.2 2.6 %shard_map.65 = bf16[32,72,256]{2,1,0:T(8,128)(2,1)} custom-call(s32[32]{0:T(128)} %get-tuple-element.26.mine_ref, s32[2,32]{1,0:T(2,128)} %get-tuple-element.27.asked_ref, s32[16,32]{1,0:T(8,128)S(1)} %bitcast.30, s32[1,32]{1,0:T(1,128)S(1)} %bitcast.32, bf16[32,80,256]{2,1,0:T(8,128)(2,1)S(1)} %all-to-all-done.in_ref, bf16[16,256,256]{2,1,0:T(8,128)(2,1)S(1)} %copy-done), custom_call_target="tpu_custom_call" | custom-call | tf_op jit(solution)/shard_map/pallas_call | solution.py:231
  46.8 7.5 %all-to-all-start.1 = ((bf16[32,72,256]{2,1,0:T(8,128)(2,1)}), bf16[32,72,256]{2,1,0:T(8,128)(2,1)S(1)}, u32[]{:S(2)}, u32[]{:S(2)}) async-start(bf16[32,72,256]{2,1,0:T(8,128)(2,1)} %shard_map.65), calls=%async_computation.1 | async-start | bytes 2359296 | tf_op jit(solution)/shard_map/all_to_all | solution.py:169
  54.4 1.2 shard_map.66
  55.6 2.9 %collective-permute-start.3 = (bf16[4,32,256]{2,1,0:T(8,128)(2,1)}, bf16[4,32,256]{2,1,0:T(8,128)(2,1)S(1)}, u32[]{:S(2)}, u32[]{:S(2)}) collective-permute-start(bf16[4,32,256]{2,1,0:T(8,128)(2,1)} %get-tuple-element.39), channel_id=1, source_target_pairs={{0,32},{32,0},{64,96},{96,64},{128,160},{160,128},{192,224},{224,1... | collective-permute-start | bytes 196616 | tf_op jit(solution)/shard_map/ppermute | solution.py:176
  58.5 4.0 %collective-permute-start.4 = (bf16[4,32,256]{2,1,0:T(8,128)(2,1)}, bf16[4,32,256]{2,1,0:T(8,128)(2,1)S(1)}, u32[]{:S(2)}, u32[]{:S(2)}) collective-permute-start(bf16[4,32,256]{2,1,0:T(8,128)(2,1)} %get-tuple-element.40), channel_id=1, source_target_pairs={{0,64},{32,96},{64,0},{96,32},{128,192},{160,224},{192,128},{224,1... | collective-permute-start | bytes 196616 | tf_op jit(solution)/shard_map/ppermute | solution.py:176
  62.6 2.5 %collective-permute-start.5 = (bf16[4,32,256]{2,1,0:T(8,128)(2,1)}, bf16[4,32,256]{2,1,0:T(8,128)(2,1)S(1)}, u32[]{:S(2)}, u32[]{:S(2)}) collective-permute-start(bf16[4,32,256]{2,1,0:T(8,128)(2,1)} %get-tuple-element.41), channel_id=1, source_target_pairs={{0,96},{32,64},{64,32},{96,0},{128,224},{160,192},{192,160},{224,1... | collective-permute-start | bytes 196616 | tf_op jit(solution)/shard_map/ppermute | solution.py:176
  65.0 1.5 %shard_map.68.part_ref = bf16[16,3,32,256]{3,2,1,0:T(8,128)(2,1)} custom-call(s32[32]{0:T(128)S(1)} %copy-done.7, bf16[32,80,256]{2,1,0:T(8,128)(2,1)S(1)} %all-to-all-done.in_ref), custom_call_target="tpu_custom_call" | custom-call | tf_op jit(solution)/shard_map/pallas_call | solution.py:262
  66.6 2.4 %collective-permute-done.5.in3_ref = bf16[4,32,256]{2,1,0:T(8,128)(2,1)S(1)} collective-permute-done((bf16[4,32,256]{2,1,0:T(8,128)(2,1)}, bf16[4,32,256]{2,1,0:T(8,128)(2,1)S(1)}, u32[]{:S(2)}, u32[]{:S(2)}) %collective-permute-start.5) | collective-permute-done | bytes 65568 | tf_op jit(solution)/shard_map/ppermute | solution.py:176
  68.9 3.0 %all-to-all-done.1.in_ref = bf16[32,72,256]{2,1,0:T(8,128)(2,1)S(1)} async-done(((bf16[32,72,256]{2,1,0:T(8,128)(2,1)}), bf16[32,72,256]{2,1,0:T(8,128)(2,1)S(1)}, u32[]{:S(2)}, u32[]{:S(2)}) %all-to-all-start.1) | async-done | bytes 1179680 | tf_op jit(solution)/shard_map/all_to_all | solution.py:169
  71.9 1.7 %shard_map.69 = bf16[16,3,32,256]{3,2,1,0:T(8,128)(2,1)} custom-call(s32[32]{0:T(128)S(1)} %copy-done.7, bf16[32,72,256]{2,1,0:T(8,128)(2,1)S(1)} %all-to-all-done.1.in_ref, bf16[16,3,32,256]{3,2,1,0:T(8,128)(2,1)} %shard_map.68.part_ref), custom_call_target="tpu_custom_call", output_to_operand_aliasing={{}: (2, {})} | custom-call | tf_op jit(solution)/shard_map/pallas_call | solution.py:269
  73.6 10.4 %all-to-all-start.2 = ((bf16[16,3,32,256]{3,2,1,0:T(8,128)(2,1)}), bf16[16,3,32,256]{3,2,1,0:T(8,128)(2,1)S(1)}, u32[]{:S(2)}, u32[]{:S(2)}) async-start(bf16[16,3,32,256]{3,2,1,0:T(8,128)(2,1)} %shard_map.69), calls=%async_computation.2 | async-start | bytes 1572864 | tf_op jit(solution)/shard_map/all_to_all | solution.py:169
  83.9 0.6 dynamic_slice.4
  85.2 0.6 shard_map.67
  85.8 38.1 %all-to-all-done.2 = bf16[16,3,32,256]{3,2,1,0:T(8,128)(2,1)S(1)} async-done(((bf16[16,3,32,256]{3,2,1,0:T(8,128)(2,1)}), bf16[16,3,32,256]{3,2,1,0:T(8,128)(2,1)S(1)}, u32[]{:S(2)}, u32[]{:S(2)}) %all-to-all-start.2) | async-done | bytes 786464 | tf_op jit(solution)/shard_map/all_to_all | solution.py:169
  123.9 0.3 convolution_bitcast_fusion
  124.1 1.0 fusion.2
  (20 shorter events, 0.1 us)
Async XLA Ops:
  4.4 39.8 %copy-start = (bf16[16,256,256]{2,1,0:T(8,128)(2,1)S(1)}, bf16[16,256,256]{2,1,0:T(8,128)(2,1)}, u32[]{:S(2)}) copy-start(bf16[16,256,256]{2,1,0:T(8,128)(2,1)} %a_ref.1) | copy-start | bytes 6291460
  4.4 39.7 %copy-start.1 = (s32[32,16]{0,1:T(8,128)S(1)}, s32[32,16]{0,1:T(8,128)}, u32[]{:S(2)}) copy-start(s32[32,16]{0,1:T(8,128)} %param.11) | copy-start | bytes 6148
  4.4 39.7 %copy-start.6 = (s32[32]{0:T(128)S(1)}, s32[32]{0:T(128)}, u32[]{:S(2)}) copy-start(s32[32]{0:T(128)} %count_ref.1) | copy-start | bytes 388
  4.5 39.7 %all-to-all-start = ((bf16[32,80,256]{2,1,0:T(8,128)(2,1)}), bf16[32,80,256]{2,1,0:T(8,128)(2,1)S(1)}, u32[]{:S(2)}, u32[]{:S(2)}) async-start(bf16[32,80,256]{2,1,0:T(8,128)(2,1)} %get-tuple-element.28), calls=%async_computation | async-start | bytes 2621440 | tf_op jit(solution)/shard_map/all_to_all | solution.py:169
  12.2 21.1 %collective-permute-start = (bf16[4,32,256]{2,1,0:T(8,128)(2,1)}, bf16[4,32,256]{2,1,0:T(8,128)(2,1)S(1)}, u32[]{:S(2)}, u32[]{:S(2)}) collective-permute-start(bf16[4,32,256]{2,1,0:T(8,128)(2,1)} %get-tuple-element.30), channel_id=1, source_target_pairs={{0,128},{32,160},{64,192},{96,224},{128,0},{160,32},{192,64},{224,... | collective-permute-start | bytes 196616 | tf_op jit(solution)/shard_map/ppermute | solution.py:176
  21.3 15.3 %collective-permute-start.1 = (bf16[4,32,256]{2,1,0:T(8,128)(2,1)}, bf16[4,32,256]{2,1,0:T(8,128)(2,1)S(1)}, u32[]{:S(2)}, u32[]{:S(2)}) collective-permute-start(bf16[4,32,256]{2,1,0:T(8,128)(2,1)} %get-tuple-element.31), channel_id=1, source_target_pairs={{0,256},{32,288},{64,320},{96,352},{128,384},{160,416},{192,448},{... | collective-permute-start | bytes 196616 | tf_op jit(solution)/shard_map/ppermute | solution.py:176
  31.3 12.2 %collective-permute-start.2 = (bf16[4,32,256]{2,1,0:T(8,128)(2,1)}, bf16[4,32,256]{2,1,0:T(8,128)(2,1)S(1)}, u32[]{:S(2)}, u32[]{:S(2)}) collective-permute-start(bf16[4,32,256]{2,1,0:T(8,128)(2,1)} %get-tuple-element.32), channel_id=1, source_target_pairs={{0,384},{32,416},{64,448},{96,480},{128,256},{160,288},{192,320},{... | collective-permute-start | bytes 196616 | tf_op jit(solution)/shard_map/ppermute | solution.py:176
  43.5 0.6 copy-start.4
  46.8 7.6 %copy-start.3 = (bf16[4,32,256]{2,1,0:T(8,128)(2,1)S(1)}, bf16[4,32,256]{2,1,0:T(8,128)(2,1)}, u32[]{:S(2)}) copy-start(bf16[4,32,256]{2,1,0:T(8,128)(2,1)} %get-tuple-element.34.in0_ref) | copy-start | bytes 196612
  46.8 7.6 %copy-start.5 = (bf16[4,32,256]{2,1,0:T(8,128)(2,1)S(1)}, bf16[4,32,256]{2,1,0:T(8,128)(2,1)}, u32[]{:S(2)}) copy-start(bf16[4,32,256]{2,1,0:T(8,128)(2,1)} %copy-done.4) | copy-start | bytes 196612
  46.8 18.2 %copy-start.7 = (s32[32]{0:T(128)S(1)}, s32[32]{0:T(128)}, u32[]{:S(2)}) copy-start(s32[32]{0:T(128)} %get-tuple-element.26.mine_ref) | copy-start | bytes 388
  46.8 25.1 %all-to-all-start.1 = ((bf16[32,72,256]{2,1,0:T(8,128)(2,1)}), bf16[32,72,256]{2,1,0:T(8,128)(2,1)S(1)}, u32[]{:S(2)}, u32[]{:S(2)}) async-start(bf16[32,72,256]{2,1,0:T(8,128)(2,1)} %shard_map.65), calls=%async_computation.1 | async-start | bytes 2359296 | tf_op jit(solution)/shard_map/all_to_all | solution.py:169
  55.6 10.9 %collective-permute-start.3 = (bf16[4,32,256]{2,1,0:T(8,128)(2,1)}, bf16[4,32,256]{2,1,0:T(8,128)(2,1)S(1)}, u32[]{:S(2)}, u32[]{:S(2)}) collective-permute-start(bf16[4,32,256]{2,1,0:T(8,128)(2,1)} %get-tuple-element.39), channel_id=1, source_target_pairs={{0,32},{32,0},{64,96},{96,64},{128,160},{160,128},{192,224},{224,1... | collective-permute-start | bytes 196616 | tf_op jit(solution)/shard_map/ppermute | solution.py:176
  58.5 8.0 %collective-permute-start.4 = (bf16[4,32,256]{2,1,0:T(8,128)(2,1)}, bf16[4,32,256]{2,1,0:T(8,128)(2,1)S(1)}, u32[]{:S(2)}, u32[]{:S(2)}) collective-permute-start(bf16[4,32,256]{2,1,0:T(8,128)(2,1)} %get-tuple-element.40), channel_id=1, source_target_pairs={{0,64},{32,96},{64,0},{96,32},{128,192},{160,224},{192,128},{224,1... | collective-permute-start | bytes 196616 | tf_op jit(solution)/shard_map/ppermute | solution.py:176
  62.6 6.4 %collective-permute-start.5 = (bf16[4,32,256]{2,1,0:T(8,128)(2,1)}, bf16[4,32,256]{2,1,0:T(8,128)(2,1)S(1)}, u32[]{:S(2)}, u32[]{:S(2)}) collective-permute-start(bf16[4,32,256]{2,1,0:T(8,128)(2,1)} %get-tuple-element.41), channel_id=1, source_target_pairs={{0,96},{32,64},{64,32},{96,0},{128,224},{160,192},{192,160},{224,1... | collective-permute-start | bytes 196616 | tf_op jit(solution)/shard_map/ppermute | solution.py:176
  73.6 11.6 %copy-start.2 = (bf16[4,32,256]{2,1,0:T(8,128)(2,1)S(1)}, bf16[4,32,256]{2,1,0:T(8,128)(2,1)}, u32[]{:S(2)}) copy-start(bf16[4,32,256]{2,1,0:T(8,128)(2,1)} %get-tuple-element.42.in0_ref) | copy-start | bytes 196612
  73.6 50.3 %all-to-all-start.2 = ((bf16[16,3,32,256]{3,2,1,0:T(8,128)(2,1)}), bf16[16,3,32,256]{3,2,1,0:T(8,128)(2,1)S(1)}, u32[]{:S(2)}, u32[]{:S(2)}) async-start(bf16[16,3,32,256]{3,2,1,0:T(8,128)(2,1)} %shard_map.69), calls=%async_computation.2 | async-start | bytes 1572864 | tf_op jit(solution)/shard_map/all_to_all | solution.py:169

commit v7 on v6

--- a/solution.py
+++ b/solution.py
@@ -227,7 +227,6 @@
     )
     xg_in = exchange(xg_out, "rows")
     dy_parts = [swap(part, GROUP * step) for step, part in enumerate(dy_parts)]
-    xg_in, *dy_parts = lax.optimization_barrier((xg_in, *dy_parts))
     hg_out = pl.pallas_call(
         h_kernel,
         out_shape=hbm(hg_type),
@@ -242,6 +241,7 @@
             pltpu.SemaphoreType.DMA((STORES,)),
         ],
     )(far(mine), far(asked), near(cols), near(counts), near(xg_in), near(adjacency))
+    hg_out, *dy_parts = lax.optimization_barrier((hg_out, *dy_parts))
     hg_in = exchange(hg_out, "rows")
     dy_parts = pl.pallas_call(
         turn_kernel,
@@ -251,14 +251,6 @@
         compiler_params=PARAMS,
     )(own, *dy_parts)
     dy_parts = [swap(part, step) for step, part in enumerate(dy_parts)]
-    hg_in, *dy_parts = lax.optimization_barrier((hg_in, *dy_parts))
-    dy = pl.pallas_call(
-        order_kernel,
-        out_shape=slot_type,
-        in_specs=[SMEM] + [VMEM] * GROUP,
-        out_specs=VMEM,
-        compiler_params=PARAMS,
-    )(own, *dy_parts)
     z_part = pl.pallas_call(
         fill_kernel,
         out_shape=z_type,
@@ -279,6 +271,14 @@
             pltpu.SemaphoreType.DMA((2 * slots,)),
         ],
     )(mine, near(hg_in), z_part)
+    z_out, *dy_parts = lax.optimization_barrier((z_out, *dy_parts))
+    dy = pl.pallas_call(
+        order_kernel,
+        out_shape=slot_type,
+        in_specs=[SMEM] + [VMEM] * GROUP,
+        out_specs=VMEM,
+        compiler_params=PARAMS,
+    )(own, *dy_parts)
     z_in = exchange(z_out, "depth")
     result = jnp.einsum("qfa,qfb->ab", dy, z_in[:, 2], preferred_element_type=jnp.float32)
     result += jnp.einsum("qfa,qfb->ab", z_in[:, 0], z_in[:, 1], preferred_element_type=jnp.float32)

time: 126 us -> 123 us (0.976)
  waiting for transfers between devices: 53.7 us -> 50.7 us
    ppermute x6, waiting for transfers between devices: 12.6 us -> 7.7 us  [swap(): lax.ppermute(value, 'depth', [(place, place ^ step) for place in places])]
    all_to_all x3, waiting for transfers between devices: 41 us -> 43 us  [exchange(): return lax.all_to_all(value, axis, 0, 0, tiled=True)]
  transfers between devices with their start and end apart: 9 -> 9, of which waited for: 5 -> 4; matrix products, arithmetic and copies ran while one was open for 0% -> 1% of each run, Pallas kernels for 3% -> 6%
where the time goes in v7:
time: 123 us; the launch traced here: 122 us
  starting transfers between devices  55.9 us (45%)
  waiting for transfers between devices  50.7 us (41%)
  Pallas kernels  12.3 us (10%)
  matrix products  1.24 us (1%)
    all_to_all x3, waiting for transfers between devices, exchange(): return lax.all_to_all(value, axis, 0, 0, tiled=True)  43 us
    ppermute x6, starting transfers between devices, swap(): lax.ppermute(value, 'depth', [(place, place ^ step) for place in places])  30.4 us
    all_to_all x3, starting transfers between devices, exchange(): return lax.all_to_all(value, axis, 0, 0, tiled=True)  25.5 us
    ppermute x6, waiting for transfers between devices, swap(): lax.ppermute(value, 'depth', [(place, place ^ step) for place in places])  7.7 us
    pallas_call x1, Pallas kernels, body(): pl.pallas_call(send_xg_kernel, out_shape=(hbm(xg_type), hbm(asked_type),...  4.34 us
    pallas_call x1, Pallas kernels, body(): pl.pallas_call(h_kernel, out_shape=hbm(hg_type), in_specs=[SMEM, SMEM, VM...  2.62 us
  transfers between devices with their start and end apart: 9, of which 4 were waited for; matrix products, arithmetic and copies ran while one was open for 1% of the time, Pallas kernels for 6%

profile of v7, /device:TPU:34, one launch (start us, length us, event | category | flops | bytes accessed | tf_op | source)
XLA Modules:
  0.0 121.8 jit_solution(7327197647266601467)
XLA Ops:
  0.0 0.1 pad_add_fusion.own_ref
  0.1 4.3 %shard_map.64 = (bf16[32,80,256]{2,1,0:T(8,128)(2,1)}, s32[2,32]{1,0:T(2,128)}, s32[32]{0:T(128)}, bf16[4,32,256]{2,1,0:T(8,128)(2,1)}, bf16[4,32,256]{2,1,0:T(8...) custom-call(s32[2]{0:T(128)S(1)} %pad_add_fusion.own_ref, s32[16,32]{1,0:T(8,128)} %bitcast.28, ...), custom_call_target="tpu_custom_call" | custom-call | tf_op jit(solution)/shard_map/pallas_call | solution.py:211
  4.4 0.0 copy-start
  4.5 7.8 %all-to-all-start = ((bf16[32,80,256]{2,1,0:T(8,128)(2,1)}), bf16[32,80,256]{2,1,0:T(8,128)(2,1)S(1)}, u32[]{:S(2)}, u32[]{:S(2)}) async-start(bf16[32,80,256]{2,1,0:T(8,128)(2,1)} %get-tuple-element.28), calls=%async_computation | async-start | bytes 2621440 | tf_op jit(solution)/shard_map/all_to_all | solution.py:169
  12.2 9.1 %collective-permute-start = (bf16[4,32,256]{2,1,0:T(8,128)(2,1)}, bf16[4,32,256]{2,1,0:T(8,128)(2,1)S(1)}, u32[]{:S(2)}, u32[]{:S(2)}) collective-permute-start(bf16[4,32,256]{2,1,0:T(8,128)(2,1)} %get-tuple-element.30), channel_id=1, source_target_pairs={{0,128},{32,160},{64,192},{96,224},{128,0},{160,32},{192,64},{224,... | collective-permute-start | bytes 196616 | tf_op jit(solution)/shard_map/ppermute | solution.py:176
  21.3 10.0 %collective-permute-start.1 = (bf16[4,32,256]{2,1,0:T(8,128)(2,1)}, bf16[4,32,256]{2,1,0:T(8,128)(2,1)S(1)}, u32[]{:S(2)}, u32[]{:S(2)}) collective-permute-start(bf16[4,32,256]{2,1,0:T(8,128)(2,1)} %get-tuple-element.31), channel_id=1, source_target_pairs={{0,256},{32,288},{64,320},{96,352},{128,384},{160,416},{192,448},{... | collective-permute-start | bytes 196616 | tf_op jit(solution)/shard_map/ppermute | solution.py:176
  31.4 1.9 %collective-permute-start.2 = (bf16[4,32,256]{2,1,0:T(8,128)(2,1)}, bf16[4,32,256]{2,1,0:T(8,128)(2,1)}, u32[]{:S(2)}, u32[]{:S(2)}) collective-permute-start(bf16[4,32,256]{2,1,0:T(8,128)(2,1)} %get-tuple-element.32), channel_id=1, source_target_pairs={{0,384},{32,416},{64,448},{96,480},{128,256},{160,288},{192,320},{... | collective-permute-start | bytes 196616 | tf_op jit(solution)/shard_map/ppermute | solution.py:176
  33.3 2.6 %shard_map.65 = bf16[32,72,256]{2,1,0:T(8,128)(2,1)} custom-call(s32[32]{0:T(128)} %get-tuple-element.26.mine_ref, s32[2,32]{1,0:T(2,128)} %get-tuple-element.27.asked_ref, s32[16,32]{1,0:T(8,128)S(1)} %bitcast.30, s32[1,32]{1,0:T(1,128)S(1)} %bitcast.32, bf16[32,80,256]{2,1,0:T(8,128)(2,1)S(1)} %all-to-all-done.in_ref, bf16[16,256,256]{2,1,0:T(8,128)(2,1)S(1)} %copy-done), custom_call_target="tpu_custom_call" | custom-call | tf_op jit(solution)/shard_map/pallas_call | solution.py:230
  36.0 0.7 collective-permute-done.1.in2_ref
  36.6 7.0 %collective-permute-done.2.in3_ref = bf16[4,32,256]{2,1,0:T(8,128)(2,1)} collective-permute-done((bf16[4,32,256]{2,1,0:T(8,128)(2,1)}, bf16[4,32,256]{2,1,0:T(8,128)(2,1)}, u32[]{:S(2)}, u32[]{:S(2)}) %collective-permute-start.2) | collective-permute-done | bytes 65568 | tf_op jit(solution)/shard_map/ppermute | solution.py:176
  43.7 7.5 %all-to-all-start.1 = ((bf16[32,72,256]{2,1,0:T(8,128)(2,1)}), bf16[32,72,256]{2,1,0:T(8,128)(2,1)S(1)}, u32[]{:S(2)}, u32[]{:S(2)}) async-start(bf16[32,72,256]{2,1,0:T(8,128)(2,1)} %shard_map.65), calls=%async_computation.1 | async-start | bytes 2359296 | tf_op jit(solution)/shard_map/all_to_all | solution.py:169
  51.2 1.6 %shard_map.68 = (bf16[4,32,256]{2,1,0:T(8,128)(2,1)}, bf16[4,32,256]{2,1,0:T(8,128)(2,1)}, bf16[4,32,256]{2,1,0:T(8,128)(2,1)}, bf16[4,32,256]{2,1,0:T(8,128)(2,1)}) custom-call(s32[2]{0:T(128)S(1)} %pad_add_fusion.own_ref, bf16[4,32,256]{2,1,0:T(8,128)(2,1)S(1)} %copy-done.3, bf16[4,32,256]{2,1,0:T(8,128)(2,1)S(1)} %collective-permute-done.in1_ref, ...), custom_call_target="tpu_custom_call" | custom-call | tf_op jit(solution)/shard_map/pallas_call | solution.py:246
  52.8 2.8 %collective-permute-start.3 = (bf16[4,32,256]{2,1,0:T(8,128)(2,1)}, bf16[4,32,256]{2,1,0:T(8,128)(2,1)S(1)}, u32[]{:S(2)}, u32[]{:S(2)}) collective-permute-start(bf16[4,32,256]{2,1,0:T(8,128)(2,1)} %get-tuple-element.39), channel_id=1, source_target_pairs={{0,32},{32,0},{64,96},{96,64},{128,160},{160,128},{192,224},{224,1... | collective-permute-start | bytes 196616 | tf_op jit(solution)/shard_map/ppermute | solution.py:176
  55.5 4.1 %collective-permute-start.4 = (bf16[4,32,256]{2,1,0:T(8,128)(2,1)}, bf16[4,32,256]{2,1,0:T(8,128)(2,1)S(1)}, u32[]{:S(2)}, u32[]{:S(2)}) collective-permute-start(bf16[4,32,256]{2,1,0:T(8,128)(2,1)} %get-tuple-element.40), channel_id=1, source_target_pairs={{0,64},{32,96},{64,0},{96,32},{128,192},{160,224},{192,128},{224,1... | collective-permute-start | bytes 196616 | tf_op jit(solution)/shard_map/ppermute | solution.py:176
  59.7 2.5 %collective-permute-start.5 = (bf16[4,32,256]{2,1,0:T(8,128)(2,1)}, bf16[4,32,256]{2,1,0:T(8,128)(2,1)S(1)}, u32[]{:S(2)}, u32[]{:S(2)}) collective-permute-start(bf16[4,32,256]{2,1,0:T(8,128)(2,1)} %get-tuple-element.41), channel_id=1, source_target_pairs={{0,96},{32,64},{64,32},{96,0},{128,224},{160,192},{192,160},{224,1... | collective-permute-start | bytes 196616 | tf_op jit(solution)/shard_map/ppermute | solution.py:176
  62.2 1.5 %shard_map.66.part_ref = bf16[16,3,32,256]{3,2,1,0:T(8,128)(2,1)} custom-call(s32[32]{0:T(128)S(1)} %copy-done.5, bf16[32,80,256]{2,1,0:T(8,128)(2,1)S(1)} %all-to-all-done.in_ref), custom_call_target="tpu_custom_call" | custom-call | tf_op jit(solution)/shard_map/pallas_call | solution.py:254
  63.7 5.0 %all-to-all-done.1.in_ref = bf16[32,72,256]{2,1,0:T(8,128)(2,1)S(1)} async-done(((bf16[32,72,256]{2,1,0:T(8,128)(2,1)}), bf16[32,72,256]{2,1,0:T(8,128)(2,1)S(1)}, u32[]{:S(2)}, u32[]{:S(2)}) %all-to-all-start.1) | async-done | bytes 1179680 | tf_op jit(solution)/shard_map/all_to_all | solution.py:169
  68.7 1.7 %shard_map.67 = bf16[16,3,32,256]{3,2,1,0:T(8,128)(2,1)} custom-call(s32[32]{0:T(128)S(1)} %copy-done.5, bf16[32,72,256]{2,1,0:T(8,128)(2,1)S(1)} %all-to-all-done.1.in_ref, bf16[16,3,32,256]{3,2,1,0:T(8,128)(2,1)} %shard_map.66.part_ref), custom_call_target="tpu_custom_call", output_to_operand_aliasing={{}: (2, {})} | custom-call | tf_op jit(solution)/shard_map/pallas_call | solution.py:261
  70.4 10.2 %all-to-all-start.2 = ((bf16[16,3,32,256]{3,2,1,0:T(8,128)(2,1)}), bf16[16,3,32,256]{3,2,1,0:T(8,128)(2,1)S(1)}, u32[]{:S(2)}, u32[]{:S(2)}) async-start(bf16[16,3,32,256]{3,2,1,0:T(8,128)(2,1)} %shard_map.67), calls=%async_computation.2 | async-start | bytes 1572864 | tf_op jit(solution)/shard_map/all_to_all | solution.py:169
  80.7 0.6 dynamic_slice.4
  82.0 0.6 shard_map.69
  82.6 38.0 %all-to-all-done.2 = bf16[16,3,32,256]{3,2,1,0:T(8,128)(2,1)S(1)} async-done(((bf16[16,3,32,256]{3,2,1,0:T(8,128)(2,1)}), bf16[16,3,32,256]{3,2,1,0:T(8,128)(2,1)S(1)}, u32[]{:S(2)}, u32[]{:S(2)}) %all-to-all-start.2) | async-done | bytes 786464 | tf_op jit(solution)/shard_map/all_to_all | solution.py:169
  120.6 0.3 convolution_bitcast_fusion
  120.9 1.0 fusion.2
  (16 shorter events, 0.0 us)
Async XLA Ops:
  4.4 28.9 %copy-start = (bf16[16,256,256]{2,1,0:T(8,128)(2,1)S(1)}, bf16[16,256,256]{2,1,0:T(8,128)(2,1)}, u32[]{:S(2)}) copy-start(bf16[16,256,256]{2,1,0:T(8,128)(2,1)} %a_ref.1) | copy-start | bytes 6291460
  4.4 28.9 %copy-start.1 = (s32[32,16]{0,1:T(8,128)S(1)}, s32[32,16]{0,1:T(8,128)}, u32[]{:S(2)}) copy-start(s32[32,16]{0,1:T(8,128)} %param.11) | copy-start | bytes 6148
  4.4 28.9 %copy-start.4 = (s32[32]{0:T(128)S(1)}, s32[32]{0:T(128)}, u32[]{:S(2)}) copy-start(s32[32]{0:T(128)} %count_ref.1) | copy-start | bytes 388
  4.5 28.8 %all-to-all-start = ((bf16[32,80,256]{2,1,0:T(8,128)(2,1)}), bf16[32,80,256]{2,1,0:T(8,128)(2,1)S(1)}, u32[]{:S(2)}, u32[]{:S(2)}) async-start(bf16[32,80,256]{2,1,0:T(8,128)(2,1)} %get-tuple-element.28), calls=%async_computation | async-start | bytes 2621440 | tf_op jit(solution)/shard_map/all_to_all | solution.py:169
  12.2 23.7 %collective-permute-start = (bf16[4,32,256]{2,1,0:T(8,128)(2,1)}, bf16[4,32,256]{2,1,0:T(8,128)(2,1)S(1)}, u32[]{:S(2)}, u32[]{:S(2)}) collective-permute-start(bf16[4,32,256]{2,1,0:T(8,128)(2,1)} %get-tuple-element.30), channel_id=1, source_target_pairs={{0,128},{32,160},{64,192},{96,224},{128,0},{160,32},{192,64},{224,... | collective-permute-start | bytes 196616 | tf_op jit(solution)/shard_map/ppermute | solution.py:176
  21.3 15.3 %collective-permute-start.1 = (bf16[4,32,256]{2,1,0:T(8,128)(2,1)}, bf16[4,32,256]{2,1,0:T(8,128)(2,1)S(1)}, u32[]{:S(2)}, u32[]{:S(2)}) collective-permute-start(bf16[4,32,256]{2,1,0:T(8,128)(2,1)} %get-tuple-element.31), channel_id=1, source_target_pairs={{0,256},{32,288},{64,320},{96,352},{128,384},{160,416},{192,448},{... | collective-permute-start | bytes 196616 | tf_op jit(solution)/shard_map/ppermute | solution.py:176
  31.4 12.3 %collective-permute-start.2 = (bf16[4,32,256]{2,1,0:T(8,128)(2,1)}, bf16[4,32,256]{2,1,0:T(8,128)(2,1)}, u32[]{:S(2)}, u32[]{:S(2)}) collective-permute-start(bf16[4,32,256]{2,1,0:T(8,128)(2,1)} %get-tuple-element.32), channel_id=1, source_target_pairs={{0,384},{32,416},{64,448},{96,480},{128,256},{160,288},{192,320},{... | collective-permute-start | bytes 196616 | tf_op jit(solution)/shard_map/ppermute | solution.py:176
  36.0 15.2 %copy-start.3 = (bf16[4,32,256]{2,1,0:T(8,128)(2,1)S(1)}, bf16[4,32,256]{2,1,0:T(8,128)(2,1)}, u32[]{:S(2)}) copy-start(bf16[4,32,256]{2,1,0:T(8,128)(2,1)} %get-tuple-element.34.in0_ref) | copy-start | bytes 196612
  43.7 18.5 %copy-start.5 = (s32[32]{0:T(128)S(1)}, s32[32]{0:T(128)}, u32[]{:S(2)}) copy-start(s32[32]{0:T(128)} %get-tuple-element.26.mine_ref) | copy-start | bytes 388
  43.7 25.0 %all-to-all-start.1 = ((bf16[32,72,256]{2,1,0:T(8,128)(2,1)}), bf16[32,72,256]{2,1,0:T(8,128)(2,1)S(1)}, u32[]{:S(2)}, u32[]{:S(2)}) async-start(bf16[32,72,256]{2,1,0:T(8,128)(2,1)} %shard_map.65), calls=%async_computation.1 | async-start | bytes 2359296 | tf_op jit(solution)/shard_map/all_to_all | solution.py:169
  52.8 17.6 %collective-permute-start.3 = (bf16[4,32,256]{2,1,0:T(8,128)(2,1)}, bf16[4,32,256]{2,1,0:T(8,128)(2,1)S(1)}, u32[]{:S(2)}, u32[]{:S(2)}) collective-permute-start(bf16[4,32,256]{2,1,0:T(8,128)(2,1)} %get-tuple-element.39), channel_id=1, source_target_pairs={{0,32},{32,0},{64,96},{96,64},{128,160},{160,128},{192,224},{224,1... | collective-permute-start | bytes 196616 | tf_op jit(solution)/shard_map/ppermute | solution.py:176
  55.5 14.9 %collective-permute-start.4 = (bf16[4,32,256]{2,1,0:T(8,128)(2,1)}, bf16[4,32,256]{2,1,0:T(8,128)(2,1)S(1)}, u32[]{:S(2)}, u32[]{:S(2)}) collective-permute-start(bf16[4,32,256]{2,1,0:T(8,128)(2,1)} %get-tuple-element.40), channel_id=1, source_target_pairs={{0,64},{32,96},{64,0},{96,32},{128,192},{160,224},{192,128},{224,1... | collective-permute-start | bytes 196616 | tf_op jit(solution)/shard_map/ppermute | solution.py:176
  59.7 10.8 %collective-permute-start.5 = (bf16[4,32,256]{2,1,0:T(8,128)(2,1)}, bf16[4,32,256]{2,1,0:T(8,128)(2,1)S(1)}, u32[]{:S(2)}, u32[]{:S(2)}) collective-permute-start(bf16[4,32,256]{2,1,0:T(8,128)(2,1)} %get-tuple-element.41), channel_id=1, source_target_pairs={{0,96},{32,64},{64,32},{96,0},{128,224},{160,192},{192,160},{224,1... | collective-permute-start | bytes 196616 | tf_op jit(solution)/shard_map/ppermute | solution.py:176
  70.4 11.6 %copy-start.2 = (bf16[4,32,256]{2,1,0:T(8,128)(2,1)S(1)}, bf16[4,32,256]{2,1,0:T(8,128)(2,1)}, u32[]{:S(2)}) copy-start(bf16[4,32,256]{2,1,0:T(8,128)(2,1)} %get-tuple-element.42.in0_ref) | copy-start | bytes 196612
  70.4 50.1 %all-to-all-start.2 = ((bf16[16,3,32,256]{3,2,1,0:T(8,128)(2,1)}), bf16[16,3,32,256]{3,2,1,0:T(8,128)(2,1)S(1)}, u32[]{:S(2)}, u32[]{:S(2)}) async-start(bf16[16,3,32,256]{3,2,1,0:T(8,128)(2,1)} %shard_map.67), calls=%async_computation.2 | async-start | bytes 1572864 | tf_op jit(solution)/shard_map/all_to_all | solution.py:169

commit v8 on v7

--- a/solution.py
+++ b/solution.py
@@ -23,7 +23,7 @@
 
 def send_xg_kernel(
     own_ref, col_ref, row_ref, count_ref, cols_ref, counts_ref, x_ref, dy_ref, a_hbm,
-    out_ref, asked_ref, mine_ref, dy0_ref, dy1_ref, dy2_ref, dy3_ref, a_ref, term_ref, code_ref, a_sem, code_sem,
+    out_hbm, asked_ref, mine_ref, dy0_ref, dy1_ref, dy2_ref, dy3_ref, out_ref, a_ref, term_ref, code_ref, a_sem, code_sem, out_sem,
 ):
     slots, width = a_ref.shape[0], a_ref.shape[1]
     peers, most = out_ref.shape[0], PAIR_MOST
@@ -63,6 +63,12 @@
         for k in range(most):
             t = jnp.maximum(asked_ref[k, r] - 1, 0)
             out_ref[r, k * feat : (k + 1) * feat] = x_ref[:, tile_cols(t, width)]
+    x_rows, g_rows = pl.ds(0, most * feat), pl.ds(most * feat, slots)
+    stores = [
+        pltpu.make_async_copy(out_ref.at[:, rows], out_hbm.at[:, rows], out_sem.at[k])
+        for k, rows in enumerate((x_rows, g_rows))
+    ]
+    stores[0].start()
     for s in range(slots):
         if s % (slots // LOADS) == 0:
             loads[s // (slots // LOADS)].wait()
@@ -74,20 +80,27 @@
         for lanes, half in enumerate(term_ref):
             of_feature = half[pl.ds(r, slots, stride=feat)].astype(out_ref.dtype)
             out_ref[r, most * feat :, lanes * LANES : (lanes + 1) * LANES] = of_feature
+    stores[1].start()
+    for store in stores:
+        store.wait()
 
 
 def h_kernel(
     mine_ref, asked_ref, cols_ref, counts_ref, in_ref, a_ref,
-    out_hbm, acc_ref, pick_ref, sum_ref, out_ref, out_sem,
+    out_hbm, z_ref, acc_ref, pick_ref, sum_ref, out_ref, out_sem, x_sem,
 ):
     slots = a_ref.shape[0]
     peers, most = out_ref.shape[0], PAIR_MOST
     row_tiles, feat, width = acc_ref.shape
     sums = [jnp.zeros((feat, width), jnp.float32) for _ in range(row_tiles)]
+    stores = []
     for s in range(slots):
         held = jnp.maximum(mine_ref[s], 0)
         row = mine_ref[slots + s]
-        x = in_ref[held // most, pl.ds(pl.multiple_of(held % most * feat, feat), feat)]
+        place = pl.ds(pl.multiple_of(held % most * feat, feat), feat)
+        x = in_ref[held // most, place]
+        stores.append(pltpu.make_async_copy(in_ref.at[held // most, place], z_ref.at[s, 1], x_sem.at[s]))
+        stores[s].start()
         term = lax.dot_general(x, a_ref[s], (((1,), (1,)), ((), ())), preferred_element_type=jnp.float32)
         for t in range(row_tiles):
             sums[t] = sums[t] + jnp.where((row == t) & (mine_ref[s] >= 0), term, 0.0)
@@ -104,7 +117,6 @@
         pick_ref[...], terms, (((0,), (0,)), ((), ())), preferred_element_type=jnp.float32
     )
     sum_ref[peers * row_tiles :] = jnp.zeros((row_tiles, width), jnp.float32)
-    stores = []
     for r in range(peers):
         for k in range(most):
             out_ref[r, k * feat : (k + 1) * feat] = acc_ref[jnp.maximum(asked_ref[k, r] - 1, 0)]
@@ -112,7 +124,7 @@
         out_ref[r, most * feat :] = of_tiles.astype(out_ref.dtype)
         if (r + 1) % (peers // STORES) == 0:
             part = pl.ds(r + 1 - peers // STORES, peers // STORES)
-            copy = pltpu.make_async_copy(out_ref.at[part], out_hbm.at[part], out_sem.at[len(stores)])
+            copy = pltpu.make_async_copy(out_ref.at[part], out_hbm.at[part], out_sem.at[len(stores) - slots])
             copy.start()
             stores.append(copy)
     for copy in stores:
@@ -129,13 +141,6 @@
     for e, in_ref in enumerate((in0_ref, in1_ref, in2_ref, in3_ref)):
         for g in range(GROUP):
             out_ref[own_ref[1] ^ (g * GROUP + e)] = in_ref[g]
-
-
-def fill_kernel(mine_ref, in_ref, z_ref):
-    slots, _, feat, _ = z_ref.shape
-    for s in range(slots):
-        held = jnp.maximum(mine_ref[s], 0)
-        z_ref[s, 1] = in_ref[held // PAIR_MOST, pl.ds(pl.multiple_of(held % PAIR_MOST * feat, feat), feat)]
 
 
 def join_kernel(mine_ref, in_ref, part_ref, z_ref, rows_ref, g_ref, sem):
@@ -212,14 +217,16 @@
         send_xg_kernel,
         out_shape=(hbm(xg_type), hbm(asked_type), hbm(mine_type)) + (hbm(four_type),) * GROUP,
         in_specs=[SMEM, SMEM, SMEM, SMEM, VMEM, VMEM, VMEM, VMEM, ANY],
-        out_specs=(VMEM, SMEM, SMEM) + (VMEM,) * GROUP,
+        out_specs=(HBM, SMEM, SMEM) + (VMEM,) * GROUP,
         compiler_params=PARAMS,
         scratch_shapes=[
+            pltpu.VMEM(xg_type.shape, bf16),
             pltpu.VMEM(adjacency.shape, bf16),
             [pltpu.VMEM((slots * feat, LANES), jnp.float32)] * (width // LANES),
             pltpu.VMEM(asked_type.shape, jnp.int32),
             pltpu.SemaphoreType.DMA((LOADS,)),
             pltpu.SemaphoreType.DMA,
+            pltpu.SemaphoreType.DMA((2,)),
         ],
     )(
         own, far(cols), far(tile_row.T), far(tile_count), far(cols), far(counts),
@@ -227,11 +234,11 @@
     )
     xg_in = exchange(xg_out, "rows")
     dy_parts = [swap(part, GROUP * step) for step, part in enumerate(dy_parts)]
-    hg_out = pl.pallas_call(
+    hg_out, z_part = pl.pallas_call(
         h_kernel,
-        out_shape=hbm(hg_type),
+        out_shape=(hbm(hg_type), hbm(z_type)),
         in_specs=[SMEM, SMEM, VMEM, VMEM, VMEM, VMEM],
-        out_specs=HBM,
+        out_specs=(HBM, HBM),
         compiler_params=PARAMS,
         scratch_shapes=[
             tiles,
@@ -239,6 +246,7 @@
             pltpu.VMEM(((peers + 1) * row_tiles, width), jnp.float32),
             pltpu.VMEM(hg_type.shape, bf16),
             pltpu.SemaphoreType.DMA((STORES,)),
+            pltpu.SemaphoreType.DMA((slots,)),
         ],
     )(far(mine), far(asked), near(cols), near(counts), near(xg_in), near(adjacency))
     hg_out, *dy_parts = lax.optimization_barrier((hg_out, *dy_parts))
@@ -251,13 +259,6 @@
         compiler_params=PARAMS,
     )(own, *dy_parts)
     dy_parts = [swap(part, step) for step, part in enumerate(dy_parts)]
-    z_part = pl.pallas_call(
-        fill_kernel,
-        out_shape=z_type,
-        in_specs=[SMEM, VMEM],
-        out_specs=VMEM,
-        compiler_params=PARAMS,
-    )(mine, near(xg_in))
     z_out = pl.pallas_call(
         join_kernel,
         out_shape=z_type,

time: 123 us -> 123 us (level)
  waiting for transfers between devices: 50.7 us -> 52.2 us
    all_to_all x3, waiting for transfers between devices: 43 us -> 44.8 us  [exchange(): return lax.all_to_all(value, axis, 0, 0, tiled=True)]
    pallas_call x2 -> x1, Pallas kernels: 4.12 us -> 2.9 us  [body(): pl.pallas_call(h_kernel, out_shape=(hbm(hg_type), hbm(z_type)), in_specs=...]
  transfers between devices with their start and end apart: 9 -> 9, of which waited for: 4 -> 4; matrix products, arithmetic and copies ran while one was open for 1% -> 0% of each run, Pallas kernels for 6% -> 6%
where the time goes in v8:
time: 123 us; the launch traced here: 122 us
  starting transfers between devices  55.9 us (45%)
  waiting for transfers between devices  52.2 us (42%)
  Pallas kernels  11.4 us (9%)
  matrix products  1.24 us (1%)
    all_to_all x3, waiting for transfers between devices, exchange(): return lax.all_to_all(value, axis, 0, 0, tiled=True)  44.8 us
    ppermute x6, starting transfers between devices, swap(): lax.ppermute(value, 'depth', [(place, place ^ step) for place in places])  30.4 us
    all_to_all x3, starting transfers between devices, exchange(): return lax.all_to_all(value, axis, 0, 0, tiled=True)  25.5 us
    ppermute x6, waiting for transfers between devices, swap(): lax.ppermute(value, 'depth', [(place, place ^ step) for place in places])  7.41 us
    pallas_call x1, Pallas kernels, body(): pl.pallas_call(send_xg_kernel, out_shape=(hbm(xg_type), hbm(asked_type),...  4.68 us
    pallas_call x1, Pallas kernels, body(): pl.pallas_call(h_kernel, out_shape=(hbm(hg_type), hbm(z_type)), in_specs=...  2.9 us
  transfers between devices with their start and end apart: 9, of which 4 were waited for; matrix products, arithmetic and copies ran while one was open for 0% of the time, Pallas kernels for 6%

profile of v8, /device:TPU:34, one launch (start us, length us, event | category | flops | bytes accessed | tf_op | source)
XLA Modules:
  0.0 122.2 jit_solution(12557665337481791057)
XLA Ops:
  0.0 0.1 pad_add_fusion.own_ref
  0.1 4.7 %shard_map.64 = (bf16[32,80,256]{2,1,0:T(8,128)(2,1)}, s32[2,32]{1,0:T(2,128)}, s32[32]{0:T(128)}, bf16[4,32,256]{2,1,0:T(8,128)(2,1)}, bf16[4,32,256]{2,1,0:T(8...) custom-call(s32[2]{0:T(128)S(1)} %pad_add_fusion.own_ref, s32[16,32]{1,0:T(8,128)} %bitcast.28, ...), custom_call_target="tpu_custom_call" | custom-call | tf_op jit(solution)/shard_map/pallas_call | solution.py:216
  4.8 0.0 copy-start
  4.8 0.0 copy-start.1
  4.8 7.8 %all-to-all-start = ((bf16[32,80,256]{2,1,0:T(8,128)(2,1)}), bf16[32,80,256]{2,1,0:T(8,128)(2,1)S(1)}, u32[]{:S(2)}, u32[]{:S(2)}) async-start(bf16[32,80,256]{2,1,0:T(8,128)(2,1)} %get-tuple-element.30), calls=%async_computation | async-start | bytes 2621440 | tf_op jit(solution)/shard_map/all_to_all | solution.py:174
  12.6 9.1 %collective-permute-start = (bf16[4,32,256]{2,1,0:T(8,128)(2,1)}, bf16[4,32,256]{2,1,0:T(8,128)(2,1)S(1)}, u32[]{:S(2)}, u32[]{:S(2)}) collective-permute-start(bf16[4,32,256]{2,1,0:T(8,128)(2,1)} %get-tuple-element.33), channel_id=1, source_target_pairs={{0,128},{32,160},{64,192},{96,224},{128,0},{160,32},{192,64},{224,... | collective-permute-start | bytes 196616 | tf_op jit(solution)/shard_map/ppermute | solution.py:181
  21.7 10.0 %collective-permute-start.1 = (bf16[4,32,256]{2,1,0:T(8,128)(2,1)}, bf16[4,32,256]{2,1,0:T(8,128)(2,1)S(1)}, u32[]{:S(2)}, u32[]{:S(2)}) collective-permute-start(bf16[4,32,256]{2,1,0:T(8,128)(2,1)} %get-tuple-element.34), channel_id=1, source_target_pairs={{0,256},{32,288},{64,320},{96,352},{128,384},{160,416},{192,448},{... | collective-permute-start | bytes 196616 | tf_op jit(solution)/shard_map/ppermute | solution.py:181
  31.7 1.9 %collective-permute-start.2 = (bf16[4,32,256]{2,1,0:T(8,128)(2,1)}, bf16[4,32,256]{2,1,0:T(8,128)(2,1)}, u32[]{:S(2)}, u32[]{:S(2)}) collective-permute-start(bf16[4,32,256]{2,1,0:T(8,128)(2,1)} %get-tuple-element.35), channel_id=1, source_target_pairs={{0,384},{32,416},{64,448},{96,480},{128,256},{160,288},{192,320},{... | collective-permute-start | bytes 196616 | tf_op jit(solution)/shard_map/ppermute | solution.py:181
  33.7 2.9 %shard_map.65 = (bf16[32,72,256]{2,1,0:T(8,128)(2,1)}, bf16[16,3,32,256]{3,2,1,0:T(8,128)(2,1)}) custom-call(s32[32]{0:T(128)} %get-tuple-element.28.mine_ref, s32[2,32]{1,0:T(2,128)} %get-tuple-element.29.asked_ref, s32[16,32]{1,0:T(8,128)S(1)} %bitcast.30, s32[1,32]{1,0:T(1,128)S(1)} %bitcast.32, bf16[32,80,256]{2,1,0:T(8,128)(2,1)S(1)} %all-to-all-done.in_ref, ...), custom_call_target="tpu_custom_call" | custom-call | tf_op jit(solution)/shard_map/pallas_call | solution.py:237
  36.6 0.4 collective-permute-done.1.in2_ref
  37.0 7.0 %collective-permute-done.2.in3_ref = bf16[4,32,256]{2,1,0:T(8,128)(2,1)} collective-permute-done((bf16[4,32,256]{2,1,0:T(8,128)(2,1)}, bf16[4,32,256]{2,1,0:T(8,128)(2,1)}, u32[]{:S(2)}, u32[]{:S(2)}) %collective-permute-start.2) | collective-permute-done | bytes 65568 | tf_op jit(solution)/shard_map/ppermute | solution.py:181
  44.0 7.5 %all-to-all-start.1 = ((bf16[32,72,256]{2,1,0:T(8,128)(2,1)}), bf16[32,72,256]{2,1,0:T(8,128)(2,1)S(1)}, u32[]{:S(2)}, u32[]{:S(2)}) async-start(bf16[32,72,256]{2,1,0:T(8,128)(2,1)} %get-tuple-element.36), calls=%async_computation.1 | async-start | bytes 2359296 | tf_op jit(solution)/shard_map/all_to_all | solution.py:174
  51.5 1.6 %shard_map.67 = (bf16[4,32,256]{2,1,0:T(8,128)(2,1)}, bf16[4,32,256]{2,1,0:T(8,128)(2,1)}, bf16[4,32,256]{2,1,0:T(8,128)(2,1)}, bf16[4,32,256]{2,1,0:T(8,128)(2,1)}) custom-call(s32[2]{0:T(128)S(1)} %pad_add_fusion.own_ref, bf16[4,32,256]{2,1,0:T(8,128)(2,1)S(1)} %copy-done.3, bf16[4,32,256]{2,1,0:T(8,128)(2,1)S(1)} %collective-permute-done.in1_ref, ...), custom_call_target="tpu_custom_call" | custom-call | tf_op jit(solution)/shard_map/pallas_call | solution.py:254
  53.1 2.8 %collective-permute-start.3 = (bf16[4,32,256]{2,1,0:T(8,128)(2,1)}, bf16[4,32,256]{2,1,0:T(8,128)(2,1)S(1)}, u32[]{:S(2)}, u32[]{:S(2)}) collective-permute-start(bf16[4,32,256]{2,1,0:T(8,128)(2,1)} %get-tuple-element.43), channel_id=1, source_target_pairs={{0,32},{32,0},{64,96},{96,64},{128,160},{160,128},{192,224},{224,1... | collective-permute-start | bytes 196616 | tf_op jit(solution)/shard_map/ppermute | solution.py:181
  55.9 4.1 %collective-permute-start.4 = (bf16[4,32,256]{2,1,0:T(8,128)(2,1)}, bf16[4,32,256]{2,1,0:T(8,128)(2,1)S(1)}, u32[]{:S(2)}, u32[]{:S(2)}) collective-permute-start(bf16[4,32,256]{2,1,0:T(8,128)(2,1)} %get-tuple-element.44), channel_id=1, source_target_pairs={{0,64},{32,96},{64,0},{96,32},{128,192},{160,224},{192,128},{224,1... | collective-permute-start | bytes 196616 | tf_op jit(solution)/shard_map/ppermute | solution.py:181
  60.0 2.5 %collective-permute-start.5 = (bf16[4,32,256]{2,1,0:T(8,128)(2,1)}, bf16[4,32,256]{2,1,0:T(8,128)(2,1)S(1)}, u32[]{:S(2)}, u32[]{:S(2)}) collective-permute-start(bf16[4,32,256]{2,1,0:T(8,128)(2,1)} %get-tuple-element.45), channel_id=1, source_target_pairs={{0,96},{32,64},{64,32},{96,0},{128,224},{160,192},{192,160},{224,1... | collective-permute-start | bytes 196616 | tf_op jit(solution)/shard_map/ppermute | solution.py:181
  62.5 6.5 %all-to-all-done.1.in_ref = bf16[32,72,256]{2,1,0:T(8,128)(2,1)S(1)} async-done(((bf16[32,72,256]{2,1,0:T(8,128)(2,1)}), bf16[32,72,256]{2,1,0:T(8,128)(2,1)S(1)}, u32[]{:S(2)}, u32[]{:S(2)}) %all-to-all-start.1) | async-done | bytes 1179680 | tf_op jit(solution)/shard_map/all_to_all | solution.py:174
  69.1 1.7 %shard_map.66 = bf16[16,3,32,256]{3,2,1,0:T(8,128)(2,1)} custom-call(s32[32]{0:T(128)S(1)} %copy-done.5, bf16[32,72,256]{2,1,0:T(8,128)(2,1)S(1)} %all-to-all-done.1.in_ref, bf16[16,3,32,256]{3,2,1,0:T(8,128)(2,1)} %get-tuple-element.37.part_ref), custom_call_target="tpu_custom_call", output_to_operand_aliasing={{}: (2, {})} | custom-call | tf_op jit(solution)/shard_map/pallas_call | solution.py:262
  70.8 10.2 %all-to-all-start.2 = ((bf16[16,3,32,256]{3,2,1,0:T(8,128)(2,1)}), bf16[16,3,32,256]{3,2,1,0:T(8,128)(2,1)S(1)}, u32[]{:S(2)}, u32[]{:S(2)}) async-start(bf16[16,3,32,256]{3,2,1,0:T(8,128)(2,1)} %shard_map.66), calls=%async_computation.2 | async-start | bytes 1572864 | tf_op jit(solution)/shard_map/all_to_all | solution.py:174
  81.0 0.6 dynamic_slice.4
  82.2 0.6 shard_map.68
  82.7 38.2 %all-to-all-done.2 = bf16[16,3,32,256]{3,2,1,0:T(8,128)(2,1)S(1)} async-done(((bf16[16,3,32,256]{3,2,1,0:T(8,128)(2,1)}), bf16[16,3,32,256]{3,2,1,0:T(8,128)(2,1)S(1)}, u32[]{:S(2)}, u32[]{:S(2)}) %all-to-all-start.2) | async-done | bytes 786464 | tf_op jit(solution)/shard_map/all_to_all | solution.py:174
  121.0 0.3 convolution_bitcast_fusion
  121.2 1.0 fusion.2
  (15 shorter events, 0.0 us)
Async XLA Ops:
  4.8 28.9 %copy-start = (bf16[16,256,256]{2,1,0:T(8,128)(2,1)S(1)}, bf16[16,256,256]{2,1,0:T(8,128)(2,1)}, u32[]{:S(2)}) copy-start(bf16[16,256,256]{2,1,0:T(8,128)(2,1)} %a_ref.1) | copy-start | bytes 6291460
  4.8 28.9 %copy-start.1 = (s32[32,16]{0,1:T(8,128)S(1)}, s32[32,16]{0,1:T(8,128)}, u32[]{:S(2)}) copy-start(s32[32,16]{0,1:T(8,128)} %param.11) | copy-start | bytes 6148
  4.8 28.9 %copy-start.4 = (s32[32]{0:T(128)S(1)}, s32[32]{0:T(128)}, u32[]{:S(2)}) copy-start(s32[32]{0:T(128)} %count_ref.1) | copy-start | bytes 388
  4.8 28.8 %all-to-all-start = ((bf16[32,80,256]{2,1,0:T(8,128)(2,1)}), bf16[32,80,256]{2,1,0:T(8,128)(2,1)S(1)}, u32[]{:S(2)}, u32[]{:S(2)}) async-start(bf16[32,80,256]{2,1,0:T(8,128)(2,1)} %get-tuple-element.30), calls=%async_computation | async-start | bytes 2621440 | tf_op jit(solution)/shard_map/all_to_all | solution.py:174
  12.6 24.0 %collective-permute-start = (bf16[4,32,256]{2,1,0:T(8,128)(2,1)}, bf16[4,32,256]{2,1,0:T(8,128)(2,1)S(1)}, u32[]{:S(2)}, u32[]{:S(2)}) collective-permute-start(bf16[4,32,256]{2,1,0:T(8,128)(2,1)} %get-tuple-element.33), channel_id=1, source_target_pairs={{0,128},{32,160},{64,192},{96,224},{128,0},{160,32},{192,64},{224,... | collective-permute-start | bytes 196616 | tf_op jit(solution)/shard_map/ppermute | solution.py:181
  21.7 15.3 %collective-permute-start.1 = (bf16[4,32,256]{2,1,0:T(8,128)(2,1)}, bf16[4,32,256]{2,1,0:T(8,128)(2,1)S(1)}, u32[]{:S(2)}, u32[]{:S(2)}) collective-permute-start(bf16[4,32,256]{2,1,0:T(8,128)(2,1)} %get-tuple-element.34), channel_id=1, source_target_pairs={{0,256},{32,288},{64,320},{96,352},{128,384},{160,416},{192,448},{... | collective-permute-start | bytes 196616 | tf_op jit(solution)/shard_map/ppermute | solution.py:181
  31.7 12.3 %collective-permute-start.2 = (bf16[4,32,256]{2,1,0:T(8,128)(2,1)}, bf16[4,32,256]{2,1,0:T(8,128)(2,1)}, u32[]{:S(2)}, u32[]{:S(2)}) collective-permute-start(bf16[4,32,256]{2,1,0:T(8,128)(2,1)} %get-tuple-element.35), channel_id=1, source_target_pairs={{0,384},{32,416},{64,448},{96,480},{128,256},{160,288},{192,320},{... | collective-permute-start | bytes 196616 | tf_op jit(solution)/shard_map/ppermute | solution.py:181
  36.6 14.9 %copy-start.3 = (bf16[4,32,256]{2,1,0:T(8,128)(2,1)S(1)}, bf16[4,32,256]{2,1,0:T(8,128)(2,1)}, u32[]{:S(2)}) copy-start(bf16[4,32,256]{2,1,0:T(8,128)(2,1)} %get-tuple-element.38.in0_ref) | copy-start | bytes 196612
  44.0 25.0 %copy-start.5 = (s32[32]{0:T(128)S(1)}, s32[32]{0:T(128)}, u32[]{:S(2)}) copy-start(s32[32]{0:T(128)} %get-tuple-element.28.mine_ref) | copy-start | bytes 388
  44.0 25.0 %all-to-all-start.1 = ((bf16[32,72,256]{2,1,0:T(8,128)(2,1)}), bf16[32,72,256]{2,1,0:T(8,128)(2,1)S(1)}, u32[]{:S(2)}, u32[]{:S(2)}) async-start(bf16[32,72,256]{2,1,0:T(8,128)(2,1)} %get-tuple-element.36), calls=%async_computation.1 | async-start | bytes 2359296 | tf_op jit(solution)/shard_map/all_to_all | solution.py:174
  53.1 17.7 %collective-permute-start.3 = (bf16[4,32,256]{2,1,0:T(8,128)(2,1)}, bf16[4,32,256]{2,1,0:T(8,128)(2,1)S(1)}, u32[]{:S(2)}, u32[]{:S(2)}) collective-permute-start(bf16[4,32,256]{2,1,0:T(8,128)(2,1)} %get-tuple-element.43), channel_id=1, source_target_pairs={{0,32},{32,0},{64,96},{96,64},{128,160},{160,128},{192,224},{224,1... | collective-permute-start | bytes 196616 | tf_op jit(solution)/shard_map/ppermute | solution.py:181
  55.9 14.9 %collective-permute-start.4 = (bf16[4,32,256]{2,1,0:T(8,128)(2,1)}, bf16[4,32,256]{2,1,0:T(8,128)(2,1)S(1)}, u32[]{:S(2)}, u32[]{:S(2)}) collective-permute-start(bf16[4,32,256]{2,1,0:T(8,128)(2,1)} %get-tuple-element.44), channel_id=1, source_target_pairs={{0,64},{32,96},{64,0},{96,32},{128,192},{160,224},{192,128},{224,1... | collective-permute-start | bytes 196616 | tf_op jit(solution)/shard_map/ppermute | solution.py:181
  60.0 10.8 %collective-permute-start.5 = (bf16[4,32,256]{2,1,0:T(8,128)(2,1)}, bf16[4,32,256]{2,1,0:T(8,128)(2,1)S(1)}, u32[]{:S(2)}, u32[]{:S(2)}) collective-permute-start(bf16[4,32,256]{2,1,0:T(8,128)(2,1)} %get-tuple-element.45), channel_id=1, source_target_pairs={{0,96},{32,64},{64,32},{96,0},{128,224},{160,192},{192,160},{224,1... | collective-permute-start | bytes 196616 | tf_op jit(solution)/shard_map/ppermute | solution.py:181
  70.8 11.4 %copy-start.2 = (bf16[4,32,256]{2,1,0:T(8,128)(2,1)S(1)}, bf16[4,32,256]{2,1,0:T(8,128)(2,1)}, u32[]{:S(2)}) copy-start(bf16[4,32,256]{2,1,0:T(8,128)(2,1)} %get-tuple-element.46.in0_ref) | copy-start | bytes 196612
  70.8 50.1 %all-to-all-start.2 = ((bf16[16,3,32,256]{3,2,1,0:T(8,128)(2,1)}), bf16[16,3,32,256]{3,2,1,0:T(8,128)(2,1)S(1)}, u32[]{:S(2)}, u32[]{:S(2)}) async-start(bf16[16,3,32,256]{3,2,1,0:T(8,128)(2,1)} %shard_map.66), calls=%async_computation.2 | async-start | bytes 1572864 | tf_op jit(solution)/shard_map/all_to_all | solution.py:174

commit v9 on v7

--- a/solution.py
+++ b/solution.py
@@ -241,7 +241,6 @@
             pltpu.SemaphoreType.DMA((STORES,)),
         ],
     )(far(mine), far(asked), near(cols), near(counts), near(xg_in), near(adjacency))
-    hg_out, *dy_parts = lax.optimization_barrier((hg_out, *dy_parts))
     hg_in = exchange(hg_out, "rows")
     dy_parts = pl.pallas_call(
         turn_kernel,
@@ -249,6 +248,7 @@
         in_specs=[SMEM] + [VMEM] * GROUP,
         out_specs=(VMEM,) * GROUP,
         compiler_params=PARAMS,
+        cost_estimate=pl.CostEstimate(flops=int(5e10), bytes_accessed=0, transcendentals=0),
     )(own, *dy_parts)
     dy_parts = [swap(part, step) for step, part in enumerate(dy_parts)]
     z_part = pl.pallas_call(

time: 123 us -> 116 us (0.943)
  waiting for transfers between devices: 50.7 us -> 43 us
  starting transfers between devices: 55.9 us -> 57.2 us
    ppermute x6, waiting for transfers between devices: 7.7 us -> 0.16 us  [swap(): lax.ppermute(value, 'depth', [(place, place ^ step) for place in places])]
    all_to_all x3, starting transfers between devices: 25.5 us -> 26.8 us  [exchange(): return lax.all_to_all(value, axis, 0, 0, tiled=True)]
  transfers between devices with their start and end apart: 9 -> 9, of which waited for: 4 -> 3; matrix products, arithmetic and copies ran while one was open for 1% -> 1% of each run, Pallas kernels for 6% -> 7%
where the time goes in v9:
time: 116 us; the launch traced here: 115 us
  starting transfers between devices  57.2 us (49%)
  waiting for transfers between devices  43 us (37%)
  Pallas kernels  12.3 us (11%)
  matrix products  1.24 us (1%)
    all_to_all x3, waiting for transfers between devices, exchange(): return lax.all_to_all(value, axis, 0, 0, tiled=True)  42.9 us
    ppermute x6, starting transfers between devices, swap(): lax.ppermute(value, 'depth', [(place, place ^ step) for place in places])  30.4 us
    all_to_all x3, starting transfers between devices, exchange(): return lax.all_to_all(value, axis, 0, 0, tiled=True)  26.8 us
    pallas_call x1, Pallas kernels, body(): pl.pallas_call(send_xg_kernel, out_shape=(hbm(xg_type), hbm(asked_type),...  4.34 us
    pallas_call x1, Pallas kernels, body(): pl.pallas_call(h_kernel, out_shape=hbm(hg_type), in_specs=[SMEM, SMEM, VM...  2.62 us
  transfers between devices with their start and end apart: 9, of which 3 were waited for; matrix products, arithmetic and copies ran while one was open for 1% of the time, Pallas kernels for 7%

profile of v9, /device:TPU:34, one launch (start us, length us, event | category | flops | bytes accessed | tf_op | source)
XLA Modules:
  0.0 115.4 jit_solution(11267411340151430451)
XLA Ops:
  0.0 0.1 pad_add_fusion.own_ref
  0.1 4.3 %shard_map.64 = (bf16[32,80,256]{2,1,0:T(8,128)(2,1)}, s32[2,32]{1,0:T(2,128)}, s32[32]{0:T(128)}, bf16[4,32,256]{2,1,0:T(8,128)(2,1)}, bf16[4,32,256]{2,1,0:T(8...) custom-call(s32[2]{0:T(128)S(1)} %pad_add_fusion.own_ref, s32[16,32]{1,0:T(8,128)} %bitcast.28, ...), custom_call_target="tpu_custom_call" | custom-call | tf_op jit(solution)/shard_map/pallas_call | solution.py:211
  4.4 0.0 copy-start
  4.4 0.0 copy-start.1
  4.5 7.8 %all-to-all-start = ((bf16[32,80,256]{2,1,0:T(8,128)(2,1)}), bf16[32,80,256]{2,1,0:T(8,128)(2,1)S(1)}, u32[]{:S(2)}, u32[]{:S(2)}) async-start(bf16[32,80,256]{2,1,0:T(8,128)(2,1)} %get-tuple-element.23), calls=%async_computation | async-start | bytes 2621440 | tf_op jit(solution)/shard_map/all_to_all | solution.py:169
  12.2 9.1 %collective-permute-start = (bf16[4,32,256]{2,1,0:T(8,128)(2,1)}, bf16[4,32,256]{2,1,0:T(8,128)(2,1)S(1)}, u32[]{:S(2)}, u32[]{:S(2)}) collective-permute-start(bf16[4,32,256]{2,1,0:T(8,128)(2,1)} %get-tuple-element.25), channel_id=1, source_target_pairs={{0,128},{32,160},{64,192},{96,224},{128,0},{160,32},{192,64},{224,... | collective-permute-start | bytes 196616 | tf_op jit(solution)/shard_map/ppermute | solution.py:176
  21.3 10.0 %collective-permute-start.1 = (bf16[4,32,256]{2,1,0:T(8,128)(2,1)}, bf16[4,32,256]{2,1,0:T(8,128)(2,1)S(1)}, u32[]{:S(2)}, u32[]{:S(2)}) collective-permute-start(bf16[4,32,256]{2,1,0:T(8,128)(2,1)} %get-tuple-element.26), channel_id=1, source_target_pairs={{0,256},{32,288},{64,320},{96,352},{128,384},{160,416},{192,448},{... | collective-permute-start | bytes 196616 | tf_op jit(solution)/shard_map/ppermute | solution.py:176
  31.4 1.9 %collective-permute-start.2 = (bf16[4,32,256]{2,1,0:T(8,128)(2,1)}, bf16[4,32,256]{2,1,0:T(8,128)(2,1)}, u32[]{:S(2)}, u32[]{:S(2)}) collective-permute-start(bf16[4,32,256]{2,1,0:T(8,128)(2,1)} %get-tuple-element.27), channel_id=1, source_target_pairs={{0,384},{32,416},{64,448},{96,480},{128,256},{160,288},{192,320},{... | collective-permute-start | bytes 196616 | tf_op jit(solution)/shard_map/ppermute | solution.py:176
  33.3 2.6 %shard_map.65 = bf16[32,72,256]{2,1,0:T(8,128)(2,1)} custom-call(s32[32]{0:T(128)} %get-tuple-element.21.mine_ref, s32[2,32]{1,0:T(2,128)} %get-tuple-element.22.asked_ref, s32[16,32]{1,0:T(8,128)S(1)} %bitcast.30, s32[1,32]{1,0:T(1,128)S(1)} %bitcast.32, bf16[32,80,256]{2,1,0:T(8,128)(2,1)S(1)} %all-to-all-done.in_ref, bf16[16,256,256]{2,1,0:T(8,128)(2,1)S(1)} %copy-done), custom_call_target="tpu_custom_call" | custom-call | tf_op jit(solution)/shard_map/pallas_call | solution.py:230
  36.0 7.5 %all-to-all-start.1 = ((bf16[32,72,256]{2,1,0:T(8,128)(2,1)}), bf16[32,72,256]{2,1,0:T(8,128)(2,1)S(1)}, u32[]{:S(2)}, u32[]{:S(2)}) async-start(bf16[32,72,256]{2,1,0:T(8,128)(2,1)} %shard_map.65), calls=%async_computation.1 | async-start | bytes 2359296 | tf_op jit(solution)/shard_map/all_to_all | solution.py:169
  43.5 0.1 collective-permute-done.2.in3_ref
  43.7 1.6 %shard_map.68 = (bf16[4,32,256]{2,1,0:T(8,128)(2,1)}, bf16[4,32,256]{2,1,0:T(8,128)(2,1)}, bf16[4,32,256]{2,1,0:T(8,128)(2,1)}, bf16[4,32,256]{2,1,0:T(8,128)(2,1)}) custom-call(s32[2]{0:T(128)S(1)} %pad_add_fusion.own_ref, bf16[4,32,256]{2,1,0:T(8,128)(2,1)S(1)} %copy-done.5, bf16[4,32,256]{2,1,0:T(8,128)(2,1)S(1)} %collective-permute-done.in1_ref, ...), custom_call_target="tpu_custom_call" | custom-call | flops 49999998976 | tf_op jit(solution)/shard_map/pallas_call | solution.py:245
  45.2 2.8 %collective-permute-start.3 = (bf16[4,32,256]{2,1,0:T(8,128)(2,1)}, bf16[4,32,256]{2,1,0:T(8,128)(2,1)S(1)}, u32[]{:S(2)}, u32[]{:S(2)}) collective-permute-start(bf16[4,32,256]{2,1,0:T(8,128)(2,1)} %get-tuple-element.29), channel_id=1, source_target_pairs={{0,32},{32,0},{64,96},{96,64},{128,160},{160,128},{192,224},{224,1... | collective-permute-start | bytes 196616 | tf_op jit(solution)/shard_map/ppermute | solution.py:176
  48.0 4.1 %collective-permute-start.4 = (bf16[4,32,256]{2,1,0:T(8,128)(2,1)}, bf16[4,32,256]{2,1,0:T(8,128)(2,1)S(1)}, u32[]{:S(2)}, u32[]{:S(2)}) collective-permute-start(bf16[4,32,256]{2,1,0:T(8,128)(2,1)} %get-tuple-element.30), channel_id=1, source_target_pairs={{0,64},{32,96},{64,0},{96,32},{128,192},{160,224},{192,128},{224,1... | collective-permute-start | bytes 196616 | tf_op jit(solution)/shard_map/ppermute | solution.py:176
  52.1 2.5 %collective-permute-start.5 = (bf16[4,32,256]{2,1,0:T(8,128)(2,1)}, bf16[4,32,256]{2,1,0:T(8,128)(2,1)S(1)}, u32[]{:S(2)}, u32[]{:S(2)}) collective-permute-start(bf16[4,32,256]{2,1,0:T(8,128)(2,1)} %get-tuple-element.31), channel_id=1, source_target_pairs={{0,96},{32,64},{64,32},{96,0},{128,224},{160,192},{192,160},{224,1... | collective-permute-start | bytes 196616 | tf_op jit(solution)/shard_map/ppermute | solution.py:176
  54.6 1.5 %shard_map.66.part_ref = bf16[16,3,32,256]{3,2,1,0:T(8,128)(2,1)} custom-call(s32[32]{0:T(128)S(1)} %copy-done.4, bf16[32,80,256]{2,1,0:T(8,128)(2,1)S(1)} %all-to-all-done.in_ref), custom_call_target="tpu_custom_call" | custom-call | tf_op jit(solution)/shard_map/pallas_call | solution.py:254
  56.1 4.9 %all-to-all-done.1.in_ref = bf16[32,72,256]{2,1,0:T(8,128)(2,1)S(1)} async-done(((bf16[32,72,256]{2,1,0:T(8,128)(2,1)}), bf16[32,72,256]{2,1,0:T(8,128)(2,1)S(1)}, u32[]{:S(2)}, u32[]{:S(2)}) %all-to-all-start.1) | async-done | bytes 1179680 | tf_op jit(solution)/shard_map/all_to_all | solution.py:169
  61.0 1.7 %shard_map.67 = bf16[16,3,32,256]{3,2,1,0:T(8,128)(2,1)} custom-call(s32[32]{0:T(128)S(1)} %copy-done.4, bf16[32,72,256]{2,1,0:T(8,128)(2,1)S(1)} %all-to-all-done.1.in_ref, bf16[16,3,32,256]{3,2,1,0:T(8,128)(2,1)} %shard_map.66.part_ref), custom_call_target="tpu_custom_call", output_to_operand_aliasing={{}: (2, {})} | custom-call | tf_op jit(solution)/shard_map/pallas_call | solution.py:261
  62.7 11.5 %all-to-all-start.2 = ((bf16[16,3,32,256]{3,2,1,0:T(8,128)(2,1)}), bf16[16,3,32,256]{3,2,1,0:T(8,128)(2,1)S(1)}, u32[]{:S(2)}, u32[]{:S(2)}) async-start(bf16[16,3,32,256]{3,2,1,0:T(8,128)(2,1)} %shard_map.67), calls=%async_computation.2 | async-start | bytes 1572864 | tf_op jit(solution)/shard_map/all_to_all | solution.py:169
  74.2 0.6 dynamic_slice.4
  75.6 0.6 shard_map.69
  76.1 38.0 %all-to-all-done.2 = bf16[16,3,32,256]{3,2,1,0:T(8,128)(2,1)S(1)} async-done(((bf16[16,3,32,256]{3,2,1,0:T(8,128)(2,1)}), bf16[16,3,32,256]{3,2,1,0:T(8,128)(2,1)S(1)}, u32[]{:S(2)}, u32[]{:S(2)}) %all-to-all-start.2) | async-done | bytes 786464 | tf_op jit(solution)/shard_map/all_to_all | solution.py:169
  114.1 0.3 convolution_bitcast_fusion
  114.4 1.0 fusion.2
  (16 shorter events, 0.0 us)
Async XLA Ops:
  4.4 28.9 %copy-start = (bf16[16,256,256]{2,1,0:T(8,128)(2,1)S(1)}, bf16[16,256,256]{2,1,0:T(8,128)(2,1)}, u32[]{:S(2)}) copy-start(bf16[16,256,256]{2,1,0:T(8,128)(2,1)} %a_ref.1) | copy-start | bytes 6291460
  4.4 28.9 %copy-start.1 = (s32[32,16]{0,1:T(8,128)S(1)}, s32[32,16]{0,1:T(8,128)}, u32[]{:S(2)}) copy-start(s32[32,16]{0,1:T(8,128)} %param.11) | copy-start | bytes 6148
  4.5 28.9 %copy-start.3 = (s32[32]{0:T(128)S(1)}, s32[32]{0:T(128)}, u32[]{:S(2)}) copy-start(s32[32]{0:T(128)} %count_ref.1) | copy-start | bytes 388
  4.5 28.8 %all-to-all-start = ((bf16[32,80,256]{2,1,0:T(8,128)(2,1)}), bf16[32,80,256]{2,1,0:T(8,128)(2,1)S(1)}, u32[]{:S(2)}, u32[]{:S(2)}) async-start(bf16[32,80,256]{2,1,0:T(8,128)(2,1)} %get-tuple-element.23), calls=%async_computation | async-start | bytes 2621440 | tf_op jit(solution)/shard_map/all_to_all | solution.py:169
  12.2 31.3 %collective-permute-start = (bf16[4,32,256]{2,1,0:T(8,128)(2,1)}, bf16[4,32,256]{2,1,0:T(8,128)(2,1)S(1)}, u32[]{:S(2)}, u32[]{:S(2)}) collective-permute-start(bf16[4,32,256]{2,1,0:T(8,128)(2,1)} %get-tuple-element.25), channel_id=1, source_target_pairs={{0,128},{32,160},{64,192},{96,224},{128,0},{160,32},{192,64},{224,... | collective-permute-start | bytes 196616 | tf_op jit(solution)/shard_map/ppermute | solution.py:176
  21.3 22.2 %collective-permute-start.1 = (bf16[4,32,256]{2,1,0:T(8,128)(2,1)}, bf16[4,32,256]{2,1,0:T(8,128)(2,1)S(1)}, u32[]{:S(2)}, u32[]{:S(2)}) collective-permute-start(bf16[4,32,256]{2,1,0:T(8,128)(2,1)} %get-tuple-element.26), channel_id=1, source_target_pairs={{0,256},{32,288},{64,320},{96,352},{128,384},{160,416},{192,448},{... | collective-permute-start | bytes 196616 | tf_op jit(solution)/shard_map/ppermute | solution.py:176
  31.4 12.3 %collective-permute-start.2 = (bf16[4,32,256]{2,1,0:T(8,128)(2,1)}, bf16[4,32,256]{2,1,0:T(8,128)(2,1)}, u32[]{:S(2)}, u32[]{:S(2)}) collective-permute-start(bf16[4,32,256]{2,1,0:T(8,128)(2,1)} %get-tuple-element.27), channel_id=1, source_target_pairs={{0,384},{32,416},{64,448},{96,480},{128,256},{160,288},{192,320},{... | collective-permute-start | bytes 196616 | tf_op jit(solution)/shard_map/ppermute | solution.py:176
  36.0 7.7 %copy-start.5 = (bf16[4,32,256]{2,1,0:T(8,128)(2,1)S(1)}, bf16[4,32,256]{2,1,0:T(8,128)(2,1)}, u32[]{:S(2)}) copy-start(bf16[4,32,256]{2,1,0:T(8,128)(2,1)} %get-tuple-element.24.in0_ref) | copy-start | bytes 196612
  36.0 25.0 %all-to-all-start.1 = ((bf16[32,72,256]{2,1,0:T(8,128)(2,1)}), bf16[32,72,256]{2,1,0:T(8,128)(2,1)S(1)}, u32[]{:S(2)}, u32[]{:S(2)}) async-start(bf16[32,72,256]{2,1,0:T(8,128)(2,1)} %shard_map.65), calls=%async_computation.1 | async-start | bytes 2359296 | tf_op jit(solution)/shard_map/all_to_all | solution.py:169
  43.7 11.0 %copy-start.4 = (s32[32]{0:T(128)S(1)}, s32[32]{0:T(128)}, u32[]{:S(2)}) copy-start(s32[32]{0:T(128)} %get-tuple-element.21.mine_ref) | copy-start | bytes 388
  45.2 17.5 %collective-permute-start.3 = (bf16[4,32,256]{2,1,0:T(8,128)(2,1)}, bf16[4,32,256]{2,1,0:T(8,128)(2,1)S(1)}, u32[]{:S(2)}, u32[]{:S(2)}) collective-permute-start(bf16[4,32,256]{2,1,0:T(8,128)(2,1)} %get-tuple-element.29), channel_id=1, source_target_pairs={{0,32},{32,0},{64,96},{96,64},{128,160},{160,128},{192,224},{224,1... | collective-permute-start | bytes 196616 | tf_op jit(solution)/shard_map/ppermute | solution.py:176
  48.0 14.7 %collective-permute-start.4 = (bf16[4,32,256]{2,1,0:T(8,128)(2,1)}, bf16[4,32,256]{2,1,0:T(8,128)(2,1)S(1)}, u32[]{:S(2)}, u32[]{:S(2)}) collective-permute-start(bf16[4,32,256]{2,1,0:T(8,128)(2,1)} %get-tuple-element.30), channel_id=1, source_target_pairs={{0,64},{32,96},{64,0},{96,32},{128,192},{160,224},{192,128},{224,1... | collective-permute-start | bytes 196616 | tf_op jit(solution)/shard_map/ppermute | solution.py:176
  52.1 10.6 %collective-permute-start.5 = (bf16[4,32,256]{2,1,0:T(8,128)(2,1)}, bf16[4,32,256]{2,1,0:T(8,128)(2,1)S(1)}, u32[]{:S(2)}, u32[]{:S(2)}) collective-permute-start(bf16[4,32,256]{2,1,0:T(8,128)(2,1)} %get-tuple-element.31), channel_id=1, source_target_pairs={{0,96},{32,64},{64,32},{96,0},{128,224},{160,192},{192,160},{224,1... | collective-permute-start | bytes 196616 | tf_op jit(solution)/shard_map/ppermute | solution.py:176
  62.7 12.9 %copy-start.2 = (bf16[4,32,256]{2,1,0:T(8,128)(2,1)S(1)}, bf16[4,32,256]{2,1,0:T(8,128)(2,1)}, u32[]{:S(2)}) copy-start(bf16[4,32,256]{2,1,0:T(8,128)(2,1)} %get-tuple-element.32.in0_ref) | copy-start | bytes 196612
  62.7 51.4 %all-to-all-start.2 = ((bf16[16,3,32,256]{3,2,1,0:T(8,128)(2,1)}), bf16[16,3,32,256]{3,2,1,0:T(8,128)(2,1)S(1)}, u32[]{:S(2)}, u32[]{:S(2)}) async-start(bf16[16,3,32,256]{3,2,1,0:T(8,128)(2,1)} %shard_map.67), calls=%async_computation.2 | async-start | bytes 1572864 | tf_op jit(solution)/shard_map/all_to_all | solution.py:169

commit v10 on v9

--- a/solution.py
+++ b/solution.py
@@ -6,7 +6,7 @@
 from jax.sharding import PartitionSpec as P
 
 PAIR_MOST = 2
-LOADS = 4
+LOADS = 2
 STORES = 4
 LANES = 128
 GROUP = 4
@@ -22,19 +22,39 @@
 
 
 def send_xg_kernel(
-    own_ref, col_ref, row_ref, count_ref, cols_ref, counts_ref, x_ref, dy_ref, a_hbm,
-    out_ref, asked_ref, mine_ref, dy0_ref, dy1_ref, dy2_ref, dy3_ref, a_ref, term_ref, code_ref, a_sem, code_sem,
+    own_ref, col_hbm, row_hbm, count_hbm, counts_hbm, x_hbm, dy_hbm, a_hbm,
+    out_ref, asked_ref, mine_ref, dy0_ref, dy1_ref, dy2_ref, dy3_ref,
+    col_ref, row_ref, count_ref, cols_ref, counts_ref, x_ref, dy_ref,
+    a_ref, term_ref, code_ref, load_sem, a_sem, code_sem,
 ):
     slots, width = a_ref.shape[0], a_ref.shape[1]
     peers, most = out_ref.shape[0], PAIR_MOST
     feat = x_ref.shape[0]
     row_tiles = x_ref.shape[1] // width
+    small = [
+        pltpu.make_async_copy(source, target, load_sem.at[k])
+        for k, (source, target) in enumerate(
+            (
+                (col_hbm, cols_ref),
+                (counts_hbm, counts_ref),
+                (col_hbm, col_ref),
+                (row_hbm, row_ref),
+                (count_hbm, count_ref),
+                (dy_hbm, dy_ref),
+                (x_hbm, x_ref),
+            )
+        )
+    ]
+    for load in small:
+        load.start()
     loads = []
     for c in range(LOADS):
         part = pl.ds(c * (slots // LOADS), slots // LOADS)
         loads.append(pltpu.make_async_copy(a_hbm.at[part], a_ref.at[part], a_sem.at[c]))
         loads[c].start()
     own = own_ref[0]
+    for load in small[:2]:
+        load.wait()
     cols = cols_ref[...]
     slot_ids = lax.broadcasted_iota(jnp.int32, cols.shape, 0)
     wanted = (slot_ids < counts_ref[...]) & (cols // row_tiles == own)
@@ -46,6 +66,8 @@
     code_ref[1:2] = jnp.where(two, last % 8, 0)
     to_scalars = pltpu.make_async_copy(code_ref, asked_ref, code_sem)
     to_scalars.start()
+    for load in small[2:]:
+        load.wait()
     owners = [col_ref[s, own] // row_tiles for s in range(slots)]
     for s in range(slots):
         row = row_ref[s, own]
@@ -100,16 +122,20 @@
     for r in range(peers):
         pick_ref[r * slots : (r + 1) * slots] = (cols[:, r : r + 1] == tile_ids).astype(pick_ref.dtype)
     terms = in_ref[:, most * feat :].reshape(peers * slots, width)
-    sum_ref[: peers * row_tiles] = lax.dot_general(
+    sum_ref[...] = lax.dot_general(
         pick_ref[...], terms, (((0,), (0,)), ((), ())), preferred_element_type=jnp.float32
     )
-    sum_ref[peers * row_tiles :] = jnp.zeros((row_tiles, width), jnp.float32)
     stores = []
     for r in range(peers):
-        for k in range(most):
-            out_ref[r, k * feat : (k + 1) * feat] = acc_ref[jnp.maximum(asked_ref[k, r] - 1, 0)]
-        of_tiles = sum_ref[r * row_tiles : (r + 2) * row_tiles]
-        out_ref[r, most * feat :] = of_tiles.astype(out_ref.dtype)
+        of_tiles = sum_ref[r * row_tiles : (r + 1) * row_tiles]
+        halves = []
+        for half in range(width // LANES):
+            lanes = slice(half * LANES, (half + 1) * LANES)
+            for k in range(most):
+                first = (half * most + k) * feat
+                out_ref[r, first : first + feat] = acc_ref[jnp.maximum(asked_ref[k, r] - 1, 0), :, lanes]
+            halves.append(of_tiles[:, lanes])
+        out_ref[r, width // LANES * most * feat :] = jnp.concatenate(halves).astype(out_ref.dtype)
         if (r + 1) % (peers // STORES) == 0:
             part = pl.ds(r + 1 - peers // STORES, peers // STORES)
             copy = pltpu.make_async_copy(out_ref.at[part], out_hbm.at[part], out_sem.at[len(stores)])
@@ -138,29 +164,31 @@
         z_ref[s, 1] = in_ref[held // PAIR_MOST, pl.ds(pl.multiple_of(held % PAIR_MOST * feat, feat), feat)]
 
 
-def join_kernel(mine_ref, in_ref, part_ref, z_ref, rows_ref, g_ref, sem):
+def join_kernel(mine_ref, in_ref, part_ref, z_ref, rows_ref, g_ref, h_sem, g_sem):
     del part_ref
     peers, most = in_ref.shape[0], PAIR_MOST
     slots = z_ref.shape[0]
-    row_tiles, feat, _ = g_ref.shape
+    row_tiles, feat, width = g_ref.shape
+    halves = width // LANES
     copies = []
     for s in range(slots):
         held = jnp.maximum(mine_ref[s], 0)
-        tile = in_ref.at[held // most, pl.ds(pl.multiple_of(held % most * feat, feat), feat)]
-        copies.append(pltpu.make_async_copy(tile, z_ref.at[s, 2], sem.at[s]))
-        copies[s].start()
-    step = in_ref.shape[1] - most * feat
-    for r in range(peers):
-        of_tiles = in_ref[r, most * feat :].astype(jnp.float32)
-        for lanes, half in enumerate(rows_ref):
-            half[r * step : (r + 1) * step] = of_tiles[:, lanes * LANES : (lanes + 1) * LANES]
+        for half in range(halves):
+            first = pl.multiple_of((half * most + held % most) * feat, feat)
+            tile = in_ref.at[held // most, pl.ds(first, feat)]
+            place = z_ref.at[s, 2, :, pl.ds(half * LANES, LANES)]
+            copies.append(pltpu.make_async_copy(tile, place, h_sem.at[s * halves + half]))
+            copies[-1].start()
+    step = halves * row_tiles
+    for r in range(peers):
+        rows_ref[r * step : (r + 1) * step] = in_ref[r, halves * most * feat :].astype(jnp.float32)
     for t in range(row_tiles):
-        for lanes, half in enumerate(rows_ref):
-            of_tile = half[pl.ds(t, feat, stride=step)].astype(g_ref.dtype)
-            g_ref[t, :, lanes * LANES : (lanes + 1) * LANES] = of_tile
-    for s in range(slots):
-        copies.append(pltpu.make_async_copy(g_ref.at[mine_ref[slots + s]], z_ref.at[s, 0], sem.at[slots + s]))
-        copies[slots + s].start()
+        for half in range(halves):
+            of_tile = rows_ref[pl.ds(half * row_tiles + t, feat, stride=step)].astype(g_ref.dtype)
+            g_ref[t, :, half * LANES : (half + 1) * LANES] = of_tile
+    for s in range(slots):
+        copies.append(pltpu.make_async_copy(g_ref.at[mine_ref[slots + s]], z_ref.at[s, 0], g_sem.at[s]))
+        copies[-1].start()
     for copy in copies:
         copy.wait()
 
@@ -197,7 +225,7 @@
     bf16 = node_feat.dtype
     wanted_rows = PAIR_MOST * feat
     xg_type = jax.ShapeDtypeStruct((peers, wanted_rows + slots, width), bf16)
-    hg_type = jax.ShapeDtypeStruct((peers, wanted_rows + 2 * row_tiles, width), bf16)
+    hg_type = jax.ShapeDtypeStruct((peers, (wanted_rows + row_tiles) * (width // LANES), LANES), bf16)
     asked_type = jax.ShapeDtypeStruct((PAIR_MOST, peers), jnp.int32)
     mine_type = jax.ShapeDtypeStruct((2 * slots,), jnp.int32)
     z_type = jax.ShapeDtypeStruct((slots, 3, feat, width), bf16)
@@ -211,20 +239,25 @@
     xg_out, asked, mine, *dy_parts = pl.pallas_call(
         send_xg_kernel,
         out_shape=(hbm(xg_type), hbm(asked_type), hbm(mine_type)) + (hbm(four_type),) * GROUP,
-        in_specs=[SMEM, SMEM, SMEM, SMEM, VMEM, VMEM, VMEM, VMEM, ANY],
+        in_specs=[SMEM] + [ANY] * 7,
         out_specs=(VMEM, SMEM, SMEM) + (VMEM,) * GROUP,
         compiler_params=PARAMS,
         scratch_shapes=[
+            pltpu.SMEM(cols.shape, jnp.int32),
+            pltpu.SMEM(cols.shape, jnp.int32),
+            pltpu.SMEM(tile_count.shape, jnp.int32),
+            pltpu.VMEM(cols.shape, jnp.int32),
+            pltpu.VMEM(counts.shape, jnp.int32),
+            pltpu.VMEM(node_feat.shape, bf16),
+            pltpu.VMEM(grad_out.shape, bf16),
             pltpu.VMEM(adjacency.shape, bf16),
             [pltpu.VMEM((slots * feat, LANES), jnp.float32)] * (width // LANES),
             pltpu.VMEM(asked_type.shape, jnp.int32),
+            pltpu.SemaphoreType.DMA((7,)),
             pltpu.SemaphoreType.DMA((LOADS,)),
             pltpu.SemaphoreType.DMA,
         ],
-    )(
-        own, far(cols), far(tile_row.T), far(tile_count), far(cols), far(counts),
-        node_feat, grad_out, adjacency,
-    )
+    )(own, far(cols), far(tile_row.T), far(tile_count), far(counts), node_feat, grad_out, adjacency)
     xg_in = exchange(xg_out, "rows")
     dy_parts = [swap(part, GROUP * step) for step, part in enumerate(dy_parts)]
     hg_out = pl.pallas_call(
@@ -236,7 +269,7 @@
         scratch_shapes=[
             tiles,
             pltpu.VMEM((peers * slots, peers * row_tiles), bf16),
-            pltpu.VMEM(((peers + 1) * row_tiles, width), jnp.float32),
+            pltpu.VMEM((peers * row_tiles, width), jnp.float32),
             pltpu.VMEM(hg_type.shape, bf16),
             pltpu.SemaphoreType.DMA((STORES,)),
         ],
@@ -266,9 +299,10 @@
         compiler_params=PARAMS,
         input_output_aliases={2: 0},
         scratch_shapes=[
-            [pltpu.VMEM((peers * 2 * row_tiles, LANES), jnp.float32)] * (width // LANES),
+            pltpu.VMEM((hg_type.shape[0] * row_tiles * (width // LANES), LANES), jnp.float32),
             tiles,
-            pltpu.SemaphoreType.DMA((2 * slots,)),
+            pltpu.SemaphoreType.DMA((slots * (width // LANES),)),
+            pltpu.SemaphoreType.DMA((slots,)),
         ],
     )(mine, near(hg_in), z_part)
     z_out, *dy_parts = lax.optimization_barrier((z_out, *dy_parts))

time: 116 us -> 115 us (level)
  no operation moved by 1% of the time
where the time goes in v10:
time: 115 us
  starting transfers between devices  57.2 us (50%)
  waiting for transfers between devices  42.3 us (37%)
  Pallas kernels  12.2 us (11%)
  matrix products  1.24 us (1%)
    all_to_all x3, waiting for transfers between devices, exchange(): return lax.all_to_all(value, axis, 0, 0, tiled=True)  42.1 us
    ppermute x6, starting transfers between devices, swap(): lax.ppermute(value, 'depth', [(place, place ^ step) for place in places])  30.4 us
    all_to_all x3, starting transfers between devices, exchange(): return lax.all_to_all(value, axis, 0, 0, tiled=True)  26.8 us
    pallas_call x1, Pallas kernels, body(): pl.pallas_call(send_xg_kernel, out_shape=(hbm(xg_type), hbm(asked_type),...  4.1 us
    pallas_call x1, Pallas kernels, body(): pl.pallas_call(h_kernel, out_shape=hbm(hg_type), in_specs=[SMEM, SMEM, VM...  2.58 us
  transfers between devices with their start and end apart: 9, of which 3 were waited for; matrix products, arithmetic and copies ran while one was open for 1% of the time, Pallas kernels for 7%

profile of v10, /device:TPU:34, one launch (start us, length us, event | category | flops | bytes accessed | tf_op | source)
XLA Modules:
  0.0 114.6 jit_solution(4064354856797473378)
XLA Ops:
  0.0 0.1 pad_add_fusion.own_ref
  0.1 4.1 %shard_map.64 = (bf16[32,80,256]{2,1,0:T(8,128)(2,1)}, s32[2,32]{1,0:T(2,128)}, s32[32]{0:T(128)}, bf16[4,32,256]{2,1,0:T(8,128)(2,1)}, bf16[4,32,256]{2,1,0:T(8...) custom-call(s32[2]{0:T(128)S(1)} %pad_add_fusion.own_ref, s32[16,32]{1,0:T(8,128)} %bitcast.28, ...), custom_call_target="tpu_custom_call" | custom-call | tf_op jit(solution)/shard_map/pallas_call | solution.py:239
  4.2 0.0 copy-start.2
  4.2 0.0 copy-start.3
  4.2 7.8 %all-to-all-start = ((bf16[32,80,256]{2,1,0:T(8,128)(2,1)}), bf16[32,80,256]{2,1,0:T(8,128)(2,1)S(1)}, u32[]{:S(2)}, u32[]{:S(2)}) async-start(bf16[32,80,256]{2,1,0:T(8,128)(2,1)} %get-tuple-element.23), calls=%async_computation | async-start | bytes 2621440 | tf_op jit(solution)/shard_map/all_to_all | solution.py:197
  12.0 9.1 %collective-permute-start = (bf16[4,32,256]{2,1,0:T(8,128)(2,1)}, bf16[4,32,256]{2,1,0:T(8,128)(2,1)S(1)}, u32[]{:S(2)}, u32[]{:S(2)}) collective-permute-start(bf16[4,32,256]{2,1,0:T(8,128)(2,1)} %get-tuple-element.25), channel_id=1, source_target_pairs={{0,128},{32,160},{64,192},{96,224},{128,0},{160,32},{192,64},{224,... | collective-permute-start | bytes 196616 | tf_op jit(solution)/shard_map/ppermute | solution.py:204
  21.1 10.0 %collective-permute-start.1 = (bf16[4,32,256]{2,1,0:T(8,128)(2,1)}, bf16[4,32,256]{2,1,0:T(8,128)(2,1)S(1)}, u32[]{:S(2)}, u32[]{:S(2)}) collective-permute-start(bf16[4,32,256]{2,1,0:T(8,128)(2,1)} %get-tuple-element.26), channel_id=1, source_target_pairs={{0,256},{32,288},{64,320},{96,352},{128,384},{160,416},{192,448},{... | collective-permute-start | bytes 196616 | tf_op jit(solution)/shard_map/ppermute | solution.py:204
  31.1 1.9 %collective-permute-start.2 = (bf16[4,32,256]{2,1,0:T(8,128)(2,1)}, bf16[4,32,256]{2,1,0:T(8,128)(2,1)}, u32[]{:S(2)}, u32[]{:S(2)}) collective-permute-start(bf16[4,32,256]{2,1,0:T(8,128)(2,1)} %get-tuple-element.27), channel_id=1, source_target_pairs={{0,384},{32,416},{64,448},{96,480},{128,256},{160,288},{192,320},{... | collective-permute-start | bytes 196616 | tf_op jit(solution)/shard_map/ppermute | solution.py:204
  33.1 2.6 %shard_map.65 = bf16[32,136,128]{2,1,0:T(8,128)(2,1)} custom-call(s32[32]{0:T(128)} %get-tuple-element.21.mine_ref, s32[2,32]{1,0:T(2,128)} %get-tuple-element.22.asked_ref, s32[16,32]{1,0:T(8,128)S(1)} %bitcast.29, s32[1,32]{1,0:T(1,128)S(1)} %bitcast.31, bf16[32,80,256]{2,1,0:T(8,128)(2,1)S(1)} %all-to-all-done.in_ref, bf16[16,256,256]{2,1,0:T(8,128)(2,1)S(1)} %copy-done), custom_call_target="tpu_custom_call" | custom-call | tf_op jit(solution)/shard_map/pallas_call | solution.py:263
  35.7 7.5 %all-to-all-start.1 = ((bf16[32,136,128]{2,1,0:T(8,128)(2,1)}), bf16[32,136,128]{2,1,0:T(8,128)(2,1)S(1)}, u32[]{:S(2)}, u32[]{:S(2)}) async-start(bf16[32,136,128]{2,1,0:T(8,128)(2,1)} %shard_map.65), calls=%async_computation.1 | async-start | bytes 2228224 | tf_op jit(solution)/shard_map/all_to_all | solution.py:197
  43.2 0.2 collective-permute-done.2.in3_ref
  43.4 1.6 %shard_map.68 = (bf16[4,32,256]{2,1,0:T(8,128)(2,1)}, bf16[4,32,256]{2,1,0:T(8,128)(2,1)}, bf16[4,32,256]{2,1,0:T(8,128)(2,1)}, bf16[4,32,256]{2,1,0:T(8,128)(2,1)}) custom-call(s32[2]{0:T(128)S(1)} %pad_add_fusion.own_ref, bf16[4,32,256]{2,1,0:T(8,128)(2,1)S(1)} %copy-done.5, bf16[4,32,256]{2,1,0:T(8,128)(2,1)S(1)} %collective-permute-done.in1_ref, ...), custom_call_target="tpu_custom_call" | custom-call | flops 49999998976 | tf_op jit(solution)/shard_map/pallas_call | solution.py:278
  45.0 2.8 %collective-permute-start.3 = (bf16[4,32,256]{2,1,0:T(8,128)(2,1)}, bf16[4,32,256]{2,1,0:T(8,128)(2,1)S(1)}, u32[]{:S(2)}, u32[]{:S(2)}) collective-permute-start(bf16[4,32,256]{2,1,0:T(8,128)(2,1)} %get-tuple-element.29), channel_id=1, source_target_pairs={{0,32},{32,0},{64,96},{96,64},{128,160},{160,128},{192,224},{224,1... | collective-permute-start | bytes 196616 | tf_op jit(solution)/shard_map/ppermute | solution.py:204
  47.8 4.1 %collective-permute-start.4 = (bf16[4,32,256]{2,1,0:T(8,128)(2,1)}, bf16[4,32,256]{2,1,0:T(8,128)(2,1)S(1)}, u32[]{:S(2)}, u32[]{:S(2)}) collective-permute-start(bf16[4,32,256]{2,1,0:T(8,128)(2,1)} %get-tuple-element.30), channel_id=1, source_target_pairs={{0,64},{32,96},{64,0},{96,32},{128,192},{160,224},{192,128},{224,1... | collective-permute-start | bytes 196616 | tf_op jit(solution)/shard_map/ppermute | solution.py:204
  51.9 2.5 %collective-permute-start.5 = (bf16[4,32,256]{2,1,0:T(8,128)(2,1)}, bf16[4,32,256]{2,1,0:T(8,128)(2,1)S(1)}, u32[]{:S(2)}, u32[]{:S(2)}) collective-permute-start(bf16[4,32,256]{2,1,0:T(8,128)(2,1)} %get-tuple-element.31), channel_id=1, source_target_pairs={{0,96},{32,64},{64,32},{96,0},{128,224},{160,192},{192,160},{224,1... | collective-permute-start | bytes 196616 | tf_op jit(solution)/shard_map/ppermute | solution.py:204
  54.4 1.5 %shard_map.66.part_ref = bf16[16,3,32,256]{3,2,1,0:T(8,128)(2,1)} custom-call(s32[32]{0:T(128)S(1)} %copy-done.4, bf16[32,80,256]{2,1,0:T(8,128)(2,1)S(1)} %all-to-all-done.in_ref), custom_call_target="tpu_custom_call" | custom-call | tf_op jit(solution)/shard_map/pallas_call | solution.py:287
  55.9 4.1 %all-to-all-done.1.in_ref = bf16[32,136,128]{2,1,0:T(8,128)(2,1)S(1)} async-done(((bf16[32,136,128]{2,1,0:T(8,128)(2,1)}), bf16[32,136,128]{2,1,0:T(8,128)(2,1)S(1)}, u32[]{:S(2)}, u32[]{:S(2)}) %all-to-all-start.1) | async-done | bytes 1114144 | tf_op jit(solution)/shard_map/all_to_all | solution.py:197
  60.0 1.8 %shard_map.67 = bf16[16,3,32,256]{3,2,1,0:T(8,128)(2,1)} custom-call(s32[32]{0:T(128)S(1)} %copy-done.4, bf16[32,136,128]{2,1,0:T(8,128)(2,1)S(1)} %all-to-all-done.1.in_ref, bf16[16,3,32,256]{3,2,1,0:T(8,128)(2,1)} %shard_map.66.part_ref), custom_call_target="tpu_custom_call", output_to_operand_aliasing={{}: (2, {})} | custom-call | tf_op jit(solution)/shard_map/pallas_call | solution.py:294
  61.9 11.5 %all-to-all-start.2 = ((bf16[16,3,32,256]{3,2,1,0:T(8,128)(2,1)}), bf16[16,3,32,256]{3,2,1,0:T(8,128)(2,1)S(1)}, u32[]{:S(2)}, u32[]{:S(2)}) async-start(bf16[16,3,32,256]{3,2,1,0:T(8,128)(2,1)} %shard_map.67), calls=%async_computation.2 | async-start | bytes 1572864 | tf_op jit(solution)/shard_map/all_to_all | solution.py:197
  73.4 0.6 dynamic_slice.4
  74.7 0.6 shard_map.69
  75.3 38.0 %all-to-all-done.2 = bf16[16,3,32,256]{3,2,1,0:T(8,128)(2,1)S(1)} async-done(((bf16[16,3,32,256]{3,2,1,0:T(8,128)(2,1)}), bf16[16,3,32,256]{3,2,1,0:T(8,128)(2,1)S(1)}, u32[]{:S(2)}, u32[]{:S(2)}) %all-to-all-start.2) | async-done | bytes 786464 | tf_op jit(solution)/shard_map/all_to_all | solution.py:197
  113.3 0.3 convolution_bitcast_fusion
  113.6 1.0 fusion.2
  (16 shorter events, 0.0 us)
Async XLA Ops:
  4.2 28.9 %copy-start = (bf16[16,256,256]{2,1,0:T(8,128)(2,1)S(1)}, bf16[16,256,256]{2,1,0:T(8,128)(2,1)}, u32[]{:S(2)}) copy-start(bf16[16,256,256]{2,1,0:T(8,128)(2,1)} %a_ref.1) | copy-start | bytes 6291460
  4.2 28.9 %copy-start.2 = (s32[32,16]{0,1:T(8,128)S(1)}, s32[32,16]{0,1:T(8,128)}, u32[]{:S(2)}) copy-start(s32[32,16]{0,1:T(8,128)} %param.11) | copy-start | bytes 6148
  4.2 28.9 %copy-start.3 = (s32[32]{0:T(128)S(1)}, s32[32]{0:T(128)}, u32[]{:S(2)}) copy-start(s32[32]{0:T(128)} %count_hbm.1) | copy-start | bytes 388
  4.2 28.8 %all-to-all-start = ((bf16[32,80,256]{2,1,0:T(8,128)(2,1)}), bf16[32,80,256]{2,1,0:T(8,128)(2,1)S(1)}, u32[]{:S(2)}, u32[]{:S(2)}) async-start(bf16[32,80,256]{2,1,0:T(8,128)(2,1)} %get-tuple-element.23), calls=%async_computation | async-start | bytes 2621440 | tf_op jit(solution)/shard_map/all_to_all | solution.py:197
  12.0 31.2 %collective-permute-start = (bf16[4,32,256]{2,1,0:T(8,128)(2,1)}, bf16[4,32,256]{2,1,0:T(8,128)(2,1)S(1)}, u32[]{:S(2)}, u32[]{:S(2)}) collective-permute-start(bf16[4,32,256]{2,1,0:T(8,128)(2,1)} %get-tuple-element.25), channel_id=1, source_target_pairs={{0,128},{32,160},{64,192},{96,224},{128,0},{160,32},{192,64},{224,... | collective-permute-start | bytes 196616 | tf_op jit(solution)/shard_map/ppermute | solution.py:204
  21.1 22.1 %collective-permute-start.1 = (bf16[4,32,256]{2,1,0:T(8,128)(2,1)}, bf16[4,32,256]{2,1,0:T(8,128)(2,1)S(1)}, u32[]{:S(2)}, u32[]{:S(2)}) collective-permute-start(bf16[4,32,256]{2,1,0:T(8,128)(2,1)} %get-tuple-element.26), channel_id=1, source_target_pairs={{0,256},{32,288},{64,320},{96,352},{128,384},{160,416},{192,448},{... | collective-permute-start | bytes 196616 | tf_op jit(solution)/shard_map/ppermute | solution.py:204
  31.1 12.3 %collective-permute-start.2 = (bf16[4,32,256]{2,1,0:T(8,128)(2,1)}, bf16[4,32,256]{2,1,0:T(8,128)(2,1)}, u32[]{:S(2)}, u32[]{:S(2)}) collective-permute-start(bf16[4,32,256]{2,1,0:T(8,128)(2,1)} %get-tuple-element.27), channel_id=1, source_target_pairs={{0,384},{32,416},{64,448},{96,480},{128,256},{160,288},{192,320},{... | collective-permute-start | bytes 196616 | tf_op jit(solution)/shard_map/ppermute | solution.py:204
  35.7 7.8 %copy-start.5 = (bf16[4,32,256]{2,1,0:T(8,128)(2,1)S(1)}, bf16[4,32,256]{2,1,0:T(8,128)(2,1)}, u32[]{:S(2)}) copy-start(bf16[4,32,256]{2,1,0:T(8,128)(2,1)} %get-tuple-element.24.in0_ref) | copy-start | bytes 196612
  35.7 24.3 %all-to-all-start.1 = ((bf16[32,136,128]{2,1,0:T(8,128)(2,1)}), bf16[32,136,128]{2,1,0:T(8,128)(2,1)S(1)}, u32[]{:S(2)}, u32[]{:S(2)}) async-start(bf16[32,136,128]{2,1,0:T(8,128)(2,1)} %shard_map.65), calls=%async_computation.1 | async-start | bytes 2228224 | tf_op jit(solution)/shard_map/all_to_all | solution.py:197
  43.4 10.9 %copy-start.4 = (s32[32]{0:T(128)S(1)}, s32[32]{0:T(128)}, u32[]{:S(2)}) copy-start(s32[32]{0:T(128)} %get-tuple-element.21.mine_ref) | copy-start | bytes 388
  45.0 16.9 %collective-permute-start.3 = (bf16[4,32,256]{2,1,0:T(8,128)(2,1)}, bf16[4,32,256]{2,1,0:T(8,128)(2,1)S(1)}, u32[]{:S(2)}, u32[]{:S(2)}) collective-permute-start(bf16[4,32,256]{2,1,0:T(8,128)(2,1)} %get-tuple-element.29), channel_id=1, source_target_pairs={{0,32},{32,0},{64,96},{96,64},{128,160},{160,128},{192,224},{224,1... | collective-permute-start | bytes 196616 | tf_op jit(solution)/shard_map/ppermute | solution.py:204
  47.8 14.1 %collective-permute-start.4 = (bf16[4,32,256]{2,1,0:T(8,128)(2,1)}, bf16[4,32,256]{2,1,0:T(8,128)(2,1)S(1)}, u32[]{:S(2)}, u32[]{:S(2)}) collective-permute-start(bf16[4,32,256]{2,1,0:T(8,128)(2,1)} %get-tuple-element.30), channel_id=1, source_target_pairs={{0,64},{32,96},{64,0},{96,32},{128,192},{160,224},{192,128},{224,1... | collective-permute-start | bytes 196616 | tf_op jit(solution)/shard_map/ppermute | solution.py:204
  51.9 10.0 %collective-permute-start.5 = (bf16[4,32,256]{2,1,0:T(8,128)(2,1)}, bf16[4,32,256]{2,1,0:T(8,128)(2,1)S(1)}, u32[]{:S(2)}, u32[]{:S(2)}) collective-permute-start(bf16[4,32,256]{2,1,0:T(8,128)(2,1)} %get-tuple-element.31), channel_id=1, source_target_pairs={{0,96},{32,64},{64,32},{96,0},{128,224},{160,192},{192,160},{224,1... | collective-permute-start | bytes 196616 | tf_op jit(solution)/shard_map/ppermute | solution.py:204
  61.9 12.9 %copy-start.1 = (bf16[4,32,256]{2,1,0:T(8,128)(2,1)S(1)}, bf16[4,32,256]{2,1,0:T(8,128)(2,1)}, u32[]{:S(2)}) copy-start(bf16[4,32,256]{2,1,0:T(8,128)(2,1)} %get-tuple-element.32.in0_ref) | copy-start | bytes 196612
  61.9 51.4 %all-to-all-start.2 = ((bf16[16,3,32,256]{3,2,1,0:T(8,128)(2,1)}), bf16[16,3,32,256]{3,2,1,0:T(8,128)(2,1)S(1)}, u32[]{:S(2)}, u32[]{:S(2)}) async-start(bf16[16,3,32,256]{3,2,1,0:T(8,128)(2,1)} %shard_map.67), calls=%async_computation.2 | async-start | bytes 1572864 | tf_op jit(solution)/shard_map/all_to_all | solution.py:197

commit v11 on v10

--- a/solution.py
+++ b/solution.py
@@ -22,7 +22,7 @@
 
 
 def send_xg_kernel(
-    own_ref, col_hbm, row_hbm, count_hbm, counts_hbm, x_hbm, dy_hbm, a_hbm,
+    col_hbm, row_hbm, count_hbm, counts_hbm, x_hbm, dy_hbm, a_hbm,
     out_ref, asked_ref, mine_ref, dy0_ref, dy1_ref, dy2_ref, dy3_ref,
     col_ref, row_ref, count_ref, cols_ref, counts_ref, x_ref, dy_ref,
     a_ref, term_ref, code_ref, load_sem, a_sem, code_sem,
@@ -52,7 +52,7 @@
         part = pl.ds(c * (slots // LOADS), slots // LOADS)
         loads.append(pltpu.make_async_copy(a_hbm.at[part], a_ref.at[part], a_sem.at[c]))
         loads[c].start()
-    own = own_ref[0]
+    own = lax.axis_index("rows")
     for load in small[:2]:
         load.wait()
     cols = cols_ref[...]
@@ -77,7 +77,7 @@
         mine_ref[s] = jnp.where(s < count_ref[own], owners[s] * most + rank, -1)
         mine_ref[slots + s] = row
     for step, part_ref in enumerate((dy0_ref, dy1_ref, dy2_ref, dy3_ref)):
-        group = own_ref[1] // GROUP ^ step
+        group = lax.axis_index("depth") // GROUP ^ step
         for e in range(GROUP):
             part_ref[e] = dy_ref[:, tile_cols(row_ref[group * GROUP + e, own], width)]
     to_scalars.wait()
@@ -145,16 +145,16 @@
         copy.wait()
 
 
-def turn_kernel(own_ref, in0_ref, in1_ref, in2_ref, in3_ref, out0_ref, out1_ref, out2_ref, out3_ref):
+def turn_kernel(in0_ref, in1_ref, in2_ref, in3_ref, out0_ref, out1_ref, out2_ref, out3_ref):
     for e, out_ref in enumerate((out0_ref, out1_ref, out2_ref, out3_ref)):
         for g, in_ref in enumerate((in0_ref, in1_ref, in2_ref, in3_ref)):
-            out_ref[g] = in_ref[own_ref[1] % GROUP ^ e]
-
-
-def order_kernel(own_ref, in0_ref, in1_ref, in2_ref, in3_ref, out_ref):
+            out_ref[g] = in_ref[lax.axis_index("depth") % GROUP ^ e]
+
+
+def order_kernel(in0_ref, in1_ref, in2_ref, in3_ref, out_ref):
     for e, in_ref in enumerate((in0_ref, in1_ref, in2_ref, in3_ref)):
         for g in range(GROUP):
-            out_ref[own_ref[1] ^ (g * GROUP + e)] = in_ref[g]
+            out_ref[lax.axis_index("depth") ^ (g * GROUP + e)] = in_ref[g]
 
 
 def fill_kernel(mine_ref, in_ref, z_ref):
@@ -235,11 +235,10 @@
     cols, counts = tile_col.T, tile_count[None]
 
     four_type = jax.ShapeDtypeStruct((GROUP, feat, width), bf16)
-    own = jnp.stack([own_index, lax.axis_index("depth")])
     xg_out, asked, mine, *dy_parts = pl.pallas_call(
         send_xg_kernel,
         out_shape=(hbm(xg_type), hbm(asked_type), hbm(mine_type)) + (hbm(four_type),) * GROUP,
-        in_specs=[SMEM] + [ANY] * 7,
+        in_specs=[ANY] * 7,
         out_specs=(VMEM, SMEM, SMEM) + (VMEM,) * GROUP,
         compiler_params=PARAMS,
         scratch_shapes=[
@@ -257,7 +256,7 @@
             pltpu.SemaphoreType.DMA((LOADS,)),
             pltpu.SemaphoreType.DMA,
         ],
-    )(own, far(cols), far(tile_row.T), far(tile_count), far(counts), node_feat, grad_out, adjacency)
+    )(far(cols), far(tile_row.T), far(tile_count), far(counts), node_feat, grad_out, adjacency)
     xg_in = exchange(xg_out, "rows")
     dy_parts = [swap(part, GROUP * step) for step, part in enumerate(dy_parts)]
     hg_out = pl.pallas_call(
@@ -278,11 +277,11 @@
     dy_parts = pl.pallas_call(
         turn_kernel,
         out_shape=(hbm(four_type),) * GROUP,
-        in_specs=[SMEM] + [VMEM] * GROUP,
+        in_specs=[VMEM] * GROUP,
         out_specs=(VMEM,) * GROUP,
         compiler_params=PARAMS,
         cost_estimate=pl.CostEstimate(flops=int(5e10), bytes_accessed=0, transcendentals=0),
-    )(own, *dy_parts)
+    )(*dy_parts)
     dy_parts = [swap(part, step) for step, part in enumerate(dy_parts)]
     z_part = pl.pallas_call(
         fill_kernel,
@@ -309,10 +308,10 @@
     dy = pl.pallas_call(
         order_kernel,
         out_shape=slot_type,
-        in_specs=[SMEM] + [VMEM] * GROUP,
+        in_specs=[VMEM] * GROUP,
         out_specs=VMEM,
         compiler_params=PARAMS,
-    )(own, *dy_parts)
+    )(*dy_parts)
     z_in = exchange(z_out, "depth")
     result = jnp.einsum("qfa,qfb->ab", dy, z_in[:, 2], preferred_element_type=jnp.float32)
     result += jnp.einsum("qfa,qfb->ab", z_in[:, 0], z_in[:, 1], preferred_element_type=jnp.float32)

time: 115 us -> 115 us (level)
  no operation moved by 1% of the time
where the time goes in v11:
time: 115 us; the launch traced here: 114 us
  starting transfers between devices  57.2 us (50%)
  waiting for transfers between devices  42.9 us (37%)
  Pallas kernels  11.1 us (10%)
  matrix products  1.24 us (1%)
    all_to_all x3, waiting for transfers between devices, exchange(): return lax.all_to_all(value, axis, 0, 0, tiled=True)  42.6 us
    ppermute x6, starting transfers between devices, swap(): lax.ppermute(value, 'depth', [(place, place ^ step) for place in places])  30.4 us
    all_to_all x3, starting transfers between devices, exchange(): return lax.all_to_all(value, axis, 0, 0, tiled=True)  26.8 us
    pallas_call x1, Pallas kernels, body(): pl.pallas_call(send_xg_kernel, out_shape=(hbm(xg_type), hbm(asked_type),...  3.56 us
    pallas_call x1, Pallas kernels, body(): pl.pallas_call(h_kernel, out_shape=hbm(hg_type), in_specs=[SMEM, SMEM, VM...  2.57 us
  transfers between devices with their start and end apart: 9, of which 3 were waited for; matrix products, arithmetic and copies ran while one was open for 1% of the time, Pallas kernels for 7%

profile of v11, /device:TPU:34, one launch (start us, length us, event | category | flops | bytes accessed | tf_op | source)
XLA Modules:
  0.0 114.0 jit_solution(15602228182980318202)
XLA Ops:
  0.0 3.6 %shard_map.64 = (bf16[32,80,256]{2,1,0:T(8,128)(2,1)}, s32[2,32]{1,0:T(2,128)}, s32[32]{0:T(128)}, bf16[4,32,256]{2,1,0:T(8,128)(2,1)}, bf16[4,32,256]{2,1,0:T(8...) custom-call(s32[16,32]{1,0:T(8,128)} %bitcast.26, s32[16,32]{1,0:T(8,128)} %bitcast.30, ...), custom_call_target="tpu_custom_call" | custom-call | tf_op jit(solution)/shard_map/pallas_call | solution.py:238
  3.6 0.0 copy-start
  3.6 0.0 copy-start.2
  3.6 0.0 copy-start.4
  3.6 7.8 %all-to-all-start = ((bf16[32,80,256]{2,1,0:T(8,128)(2,1)}), bf16[32,80,256]{2,1,0:T(8,128)(2,1)S(1)}, u32[]{:S(2)}, u32[]{:S(2)}) async-start(bf16[32,80,256]{2,1,0:T(8,128)(2,1)} %get-tuple-element.23), calls=%async_computation | async-start | bytes 2621440 | tf_op jit(solution)/shard_map/all_to_all | solution.py:197
  11.4 9.1 %collective-permute-start = (bf16[4,32,256]{2,1,0:T(8,128)(2,1)}, bf16[4,32,256]{2,1,0:T(8,128)(2,1)S(1)}, u32[]{:S(2)}, u32[]{:S(2)}) collective-permute-start(bf16[4,32,256]{2,1,0:T(8,128)(2,1)} %get-tuple-element.25), channel_id=1, source_target_pairs={{0,128},{32,160},{64,192},{96,224},{128,0},{160,32},{192,64},{224,... | collective-permute-start | bytes 196616 | tf_op jit(solution)/shard_map/ppermute | solution.py:204
  20.5 10.0 %collective-permute-start.1 = (bf16[4,32,256]{2,1,0:T(8,128)(2,1)}, bf16[4,32,256]{2,1,0:T(8,128)(2,1)S(1)}, u32[]{:S(2)}, u32[]{:S(2)}) collective-permute-start(bf16[4,32,256]{2,1,0:T(8,128)(2,1)} %get-tuple-element.26), channel_id=1, source_target_pairs={{0,256},{32,288},{64,320},{96,352},{128,384},{160,416},{192,448},{... | collective-permute-start | bytes 196616 | tf_op jit(solution)/shard_map/ppermute | solution.py:204
  30.5 1.9 %collective-permute-start.2 = (bf16[4,32,256]{2,1,0:T(8,128)(2,1)}, bf16[4,32,256]{2,1,0:T(8,128)(2,1)}, u32[]{:S(2)}, u32[]{:S(2)}) collective-permute-start(bf16[4,32,256]{2,1,0:T(8,128)(2,1)} %get-tuple-element.27), channel_id=1, source_target_pairs={{0,384},{32,416},{64,448},{96,480},{128,256},{160,288},{192,320},{... | collective-permute-start | bytes 196616 | tf_op jit(solution)/shard_map/ppermute | solution.py:204
  32.5 2.6 %shard_map.65 = bf16[32,136,128]{2,1,0:T(8,128)(2,1)} custom-call(s32[32]{0:T(128)} %get-tuple-element.21.mine_ref, s32[2,32]{1,0:T(2,128)} %get-tuple-element.22.asked_ref, s32[16,32]{1,0:T(8,128)S(1)} %bitcast.27, s32[1,32]{1,0:T(1,128)S(1)} %bitcast.29, bf16[32,80,256]{2,1,0:T(8,128)(2,1)S(1)} %all-to-all-done.in_ref, bf16[16,256,256]{2,1,0:T(8,128)(2,1)S(1)} %copy-done), custom_call_target="tpu_custom_call" | custom-call | tf_op jit(solution)/shard_map/pallas_call | solution.py:262
  35.1 7.5 %all-to-all-start.1 = ((bf16[32,136,128]{2,1,0:T(8,128)(2,1)}), bf16[32,136,128]{2,1,0:T(8,128)(2,1)S(1)}, u32[]{:S(2)}, u32[]{:S(2)}) async-start(bf16[32,136,128]{2,1,0:T(8,128)(2,1)} %shard_map.65), calls=%async_computation.1 | async-start | bytes 2228224 | tf_op jit(solution)/shard_map/all_to_all | solution.py:197
  42.6 0.2 collective-permute-done.2.in3_ref
  42.8 1.5 %shard_map.68 = (bf16[4,32,256]{2,1,0:T(8,128)(2,1)}, bf16[4,32,256]{2,1,0:T(8,128)(2,1)}, bf16[4,32,256]{2,1,0:T(8,128)(2,1)}, bf16[4,32,256]{2,1,0:T(8,128)(2,1)}) custom-call(bf16[4,32,256]{2,1,0:T(8,128)(2,1)S(1)} %copy-done.5, bf16[4,32,256]{2,1,0:T(8,128)(2,1)S(1)} %collective-permute-done.in1_ref, ...), custom_call_target="tpu_custom_call" | custom-call | flops 49999998976 | tf_op jit(solution)/shard_map/pallas_call | solution.py:277
  44.4 2.8 %collective-permute-start.3 = (bf16[4,32,256]{2,1,0:T(8,128)(2,1)}, bf16[4,32,256]{2,1,0:T(8,128)(2,1)S(1)}, u32[]{:S(2)}, u32[]{:S(2)}) collective-permute-start(bf16[4,32,256]{2,1,0:T(8,128)(2,1)} %get-tuple-element.29), channel_id=1, source_target_pairs={{0,32},{32,0},{64,96},{96,64},{128,160},{160,128},{192,224},{224,1... | collective-permute-start | bytes 196616 | tf_op jit(solution)/shard_map/ppermute | solution.py:204
  47.1 4.1 %collective-permute-start.4 = (bf16[4,32,256]{2,1,0:T(8,128)(2,1)}, bf16[4,32,256]{2,1,0:T(8,128)(2,1)S(1)}, u32[]{:S(2)}, u32[]{:S(2)}) collective-permute-start(bf16[4,32,256]{2,1,0:T(8,128)(2,1)} %get-tuple-element.30), channel_id=1, source_target_pairs={{0,64},{32,96},{64,0},{96,32},{128,192},{160,224},{192,128},{224,1... | collective-permute-start | bytes 196616 | tf_op jit(solution)/shard_map/ppermute | solution.py:204
  51.3 2.5 %collective-permute-start.5 = (bf16[4,32,256]{2,1,0:T(8,128)(2,1)}, bf16[4,32,256]{2,1,0:T(8,128)(2,1)S(1)}, u32[]{:S(2)}, u32[]{:S(2)}) collective-permute-start(bf16[4,32,256]{2,1,0:T(8,128)(2,1)} %get-tuple-element.31), channel_id=1, source_target_pairs={{0,96},{32,64},{64,32},{96,0},{128,224},{160,192},{192,160},{224,1... | collective-permute-start | bytes 196616 | tf_op jit(solution)/shard_map/ppermute | solution.py:204
  53.8 1.5 %shard_map.66.part_ref = bf16[16,3,32,256]{3,2,1,0:T(8,128)(2,1)} custom-call(s32[32]{0:T(128)S(1)} %copy-done.3, bf16[32,80,256]{2,1,0:T(8,128)(2,1)S(1)} %all-to-all-done.in_ref), custom_call_target="tpu_custom_call" | custom-call | tf_op jit(solution)/shard_map/pallas_call | solution.py:286
  55.3 4.1 %all-to-all-done.1.in_ref = bf16[32,136,128]{2,1,0:T(8,128)(2,1)S(1)} async-done(((bf16[32,136,128]{2,1,0:T(8,128)(2,1)}), bf16[32,136,128]{2,1,0:T(8,128)(2,1)S(1)}, u32[]{:S(2)}, u32[]{:S(2)}) %all-to-all-start.1) | async-done | bytes 1114144 | tf_op jit(solution)/shard_map/all_to_all | solution.py:197
  59.4 1.8 %shard_map.67 = bf16[16,3,32,256]{3,2,1,0:T(8,128)(2,1)} custom-call(s32[32]{0:T(128)S(1)} %copy-done.3, bf16[32,136,128]{2,1,0:T(8,128)(2,1)S(1)} %all-to-all-done.1.in_ref, bf16[16,3,32,256]{3,2,1,0:T(8,128)(2,1)} %shard_map.66.part_ref), custom_call_target="tpu_custom_call", output_to_operand_aliasing={{}: (2, {})} | custom-call | tf_op jit(solution)/shard_map/pallas_call | solution.py:293
  61.3 0.0 copy-start.1
  61.3 11.5 %all-to-all-start.2 = ((bf16[16,3,32,256]{3,2,1,0:T(8,128)(2,1)}), bf16[16,3,32,256]{3,2,1,0:T(8,128)(2,1)S(1)}, u32[]{:S(2)}, u32[]{:S(2)}) async-start(bf16[16,3,32,256]{3,2,1,0:T(8,128)(2,1)} %shard_map.67), calls=%async_computation.2 | async-start | bytes 1572864 | tf_op jit(solution)/shard_map/all_to_all | solution.py:197
  72.8 0.7 dynamic_slice.4
  74.2 38.5 %all-to-all-done.2 = bf16[16,3,32,256]{3,2,1,0:T(8,128)(2,1)S(1)} async-done(((bf16[16,3,32,256]{3,2,1,0:T(8,128)(2,1)}), bf16[16,3,32,256]{3,2,1,0:T(8,128)(2,1)S(1)}, u32[]{:S(2)}, u32[]{:S(2)}) %all-to-all-start.2) | async-done | bytes 786464 | tf_op jit(solution)/shard_map/all_to_all | solution.py:197
  112.7 0.3 convolution_bitcast_fusion
  113.0 1.0 fusion.2
  (15 shorter events, 0.1 us)
Async XLA Ops:
  3.6 28.9 %copy-start = (bf16[16,256,256]{2,1,0:T(8,128)(2,1)S(1)}, bf16[16,256,256]{2,1,0:T(8,128)(2,1)}, u32[]{:S(2)}) copy-start(bf16[16,256,256]{2,1,0:T(8,128)(2,1)} %a_ref.1) | copy-start | bytes 6291460
  3.6 28.9 %copy-start.2 = (s32[32,16]{0,1:T(8,128)S(1)}, s32[32,16]{0,1:T(8,128)}, u32[]{:S(2)}) copy-start(s32[32,16]{0,1:T(8,128)} %param.11) | copy-start | bytes 6148
  3.6 28.9 %copy-start.4 = (s32[32]{0:T(128)S(1)}, s32[32]{0:T(128)}, u32[]{:S(2)}) copy-start(s32[32]{0:T(128)} %count_hbm.1) | copy-start | bytes 388
  3.6 28.8 %all-to-all-start = ((bf16[32,80,256]{2,1,0:T(8,128)(2,1)}), bf16[32,80,256]{2,1,0:T(8,128)(2,1)S(1)}, u32[]{:S(2)}, u32[]{:S(2)}) async-start(bf16[32,80,256]{2,1,0:T(8,128)(2,1)} %get-tuple-element.23), calls=%async_computation | async-start | bytes 2621440 | tf_op jit(solution)/shard_map/all_to_all | solution.py:197
  11.4 31.2 %collective-permute-start = (bf16[4,32,256]{2,1,0:T(8,128)(2,1)}, bf16[4,32,256]{2,1,0:T(8,128)(2,1)S(1)}, u32[]{:S(2)}, u32[]{:S(2)}) collective-permute-start(bf16[4,32,256]{2,1,0:T(8,128)(2,1)} %get-tuple-element.25), channel_id=1, source_target_pairs={{0,128},{32,160},{64,192},{96,224},{128,0},{160,32},{192,64},{224,... | collective-permute-start | bytes 196616 | tf_op jit(solution)/shard_map/ppermute | solution.py:204
  20.5 22.1 %collective-permute-start.1 = (bf16[4,32,256]{2,1,0:T(8,128)(2,1)}, bf16[4,32,256]{2,1,0:T(8,128)(2,1)S(1)}, u32[]{:S(2)}, u32[]{:S(2)}) collective-permute-start(bf16[4,32,256]{2,1,0:T(8,128)(2,1)} %get-tuple-element.26), channel_id=1, source_target_pairs={{0,256},{32,288},{64,320},{96,352},{128,384},{160,416},{192,448},{... | collective-permute-start | bytes 196616 | tf_op jit(solution)/shard_map/ppermute | solution.py:204
  30.5 12.3 %collective-permute-start.2 = (bf16[4,32,256]{2,1,0:T(8,128)(2,1)}, bf16[4,32,256]{2,1,0:T(8,128)(2,1)}, u32[]{:S(2)}, u32[]{:S(2)}) collective-permute-start(bf16[4,32,256]{2,1,0:T(8,128)(2,1)} %get-tuple-element.27), channel_id=1, source_target_pairs={{0,384},{32,416},{64,448},{96,480},{128,256},{160,288},{192,320},{... | collective-permute-start | bytes 196616 | tf_op jit(solution)/shard_map/ppermute | solution.py:204
  35.1 7.8 %copy-start.5 = (bf16[4,32,256]{2,1,0:T(8,128)(2,1)S(1)}, bf16[4,32,256]{2,1,0:T(8,128)(2,1)}, u32[]{:S(2)}) copy-start(bf16[4,32,256]{2,1,0:T(8,128)(2,1)} %get-tuple-element.24.in0_ref) | copy-start | bytes 196612
  35.1 24.3 %all-to-all-start.1 = ((bf16[32,136,128]{2,1,0:T(8,128)(2,1)}), bf16[32,136,128]{2,1,0:T(8,128)(2,1)S(1)}, u32[]{:S(2)}, u32[]{:S(2)}) async-start(bf16[32,136,128]{2,1,0:T(8,128)(2,1)} %shard_map.65), calls=%async_computation.1 | async-start | bytes 2228224 | tf_op jit(solution)/shard_map/all_to_all | solution.py:197
  42.8 10.9 %copy-start.3 = (s32[32]{0:T(128)S(1)}, s32[32]{0:T(128)}, u32[]{:S(2)}) copy-start(s32[32]{0:T(128)} %get-tuple-element.21.mine_ref) | copy-start | bytes 388
  44.4 16.9 %collective-permute-start.3 = (bf16[4,32,256]{2,1,0:T(8,128)(2,1)}, bf16[4,32,256]{2,1,0:T(8,128)(2,1)S(1)}, u32[]{:S(2)}, u32[]{:S(2)}) collective-permute-start(bf16[4,32,256]{2,1,0:T(8,128)(2,1)} %get-tuple-element.29), channel_id=1, source_target_pairs={{0,32},{32,0},{64,96},{96,64},{128,160},{160,128},{192,224},{224,1... | collective-permute-start | bytes 196616 | tf_op jit(solution)/shard_map/ppermute | solution.py:204
  47.1 14.1 %collective-permute-start.4 = (bf16[4,32,256]{2,1,0:T(8,128)(2,1)}, bf16[4,32,256]{2,1,0:T(8,128)(2,1)S(1)}, u32[]{:S(2)}, u32[]{:S(2)}) collective-permute-start(bf16[4,32,256]{2,1,0:T(8,128)(2,1)} %get-tuple-element.30), channel_id=1, source_target_pairs={{0,64},{32,96},{64,0},{96,32},{128,192},{160,224},{192,128},{224,1... | collective-permute-start | bytes 196616 | tf_op jit(solution)/shard_map/ppermute | solution.py:204
  51.3 10.0 %collective-permute-start.5 = (bf16[4,32,256]{2,1,0:T(8,128)(2,1)}, bf16[4,32,256]{2,1,0:T(8,128)(2,1)S(1)}, u32[]{:S(2)}, u32[]{:S(2)}) collective-permute-start(bf16[4,32,256]{2,1,0:T(8,128)(2,1)} %get-tuple-element.31), channel_id=1, source_target_pairs={{0,96},{32,64},{64,32},{96,0},{128,224},{160,192},{192,160},{224,1... | collective-permute-start | bytes 196616 | tf_op jit(solution)/shard_map/ppermute | solution.py:204
  61.3 12.9 %copy-start.1 = (bf16[4,32,256]{2,1,0:T(8,128)(2,1)S(1)}, bf16[4,32,256]{2,1,0:T(8,128)(2,1)}, u32[]{:S(2)}) copy-start(bf16[4,32,256]{2,1,0:T(8,128)(2,1)} %get-tuple-element.32.in0_ref) | copy-start | bytes 196612
  61.3 51.4 %all-to-all-start.2 = ((bf16[16,3,32,256]{3,2,1,0:T(8,128)(2,1)}), bf16[16,3,32,256]{3,2,1,0:T(8,128)(2,1)S(1)}, u32[]{:S(2)}, u32[]{:S(2)}) async-start(bf16[16,3,32,256]{3,2,1,0:T(8,128)(2,1)} %shard_map.67), calls=%async_computation.2 | async-start | bytes 1572864 | tf_op jit(solution)/shard_map/all_to_all | solution.py:197

commit v12 on v11

--- a/solution.py
+++ b/solution.py
@@ -99,12 +99,30 @@
 
 
 def h_kernel(
-    mine_ref, asked_ref, cols_ref, counts_ref, in_ref, a_ref,
-    out_hbm, acc_ref, pick_ref, sum_ref, out_ref, out_sem,
+    mine_hbm, asked_hbm, cols_ref, counts_ref, in_ref, a_ref,
+    out_hbm, mine_ref, asked_ref, acc_ref, pick_ref, sum_ref, out_ref, small_sem, out_sem,
 ):
     slots = a_ref.shape[0]
     peers, most = out_ref.shape[0], PAIR_MOST
     row_tiles, feat, width = acc_ref.shape
+    small = [
+        pltpu.make_async_copy(mine_hbm, mine_ref, small_sem.at[0]),
+        pltpu.make_async_copy(asked_hbm, asked_ref, small_sem.at[1]),
+    ]
+    for load in small:
+        load.start()
+    cols = cols_ref[...]
+    live = lax.broadcasted_iota(jnp.int32, cols.shape, 0) < counts_ref[...]
+    cols = jnp.where(live, cols, -1)
+    tile_ids = lax.broadcasted_iota(jnp.int32, (slots, peers * row_tiles), 1)
+    for r in range(peers):
+        pick_ref[r * slots : (r + 1) * slots] = (cols[:, r : r + 1] == tile_ids).astype(pick_ref.dtype)
+    terms = in_ref[:, most * feat :].reshape(peers * slots, width)
+    sum_ref[...] = lax.dot_general(
+        pick_ref[...], terms, (((0,), (0,)), ((), ())), preferred_element_type=jnp.float32
+    )
+    for load in small:
+        load.wait()
     sums = [jnp.zeros((feat, width), jnp.float32) for _ in range(row_tiles)]
     for s in range(slots):
         held = jnp.maximum(mine_ref[s], 0)
@@ -115,16 +133,6 @@
             sums[t] = sums[t] + jnp.where((row == t) & (mine_ref[s] >= 0), term, 0.0)
     for t in range(row_tiles):
         acc_ref[t] = sums[t].astype(acc_ref.dtype)
-    cols = cols_ref[...]
-    live = lax.broadcasted_iota(jnp.int32, cols.shape, 0) < counts_ref[...]
-    cols = jnp.where(live, cols, -1)
-    tile_ids = lax.broadcasted_iota(jnp.int32, (slots, peers * row_tiles), 1)
-    for r in range(peers):
-        pick_ref[r * slots : (r + 1) * slots] = (cols[:, r : r + 1] == tile_ids).astype(pick_ref.dtype)
-    terms = in_ref[:, most * feat :].reshape(peers * slots, width)
-    sum_ref[...] = lax.dot_general(
-        pick_ref[...], terms, (((0,), (0,)), ((), ())), preferred_element_type=jnp.float32
-    )
     stores = []
     for r in range(peers):
         of_tiles = sum_ref[r * row_tiles : (r + 1) * row_tiles]
@@ -164,12 +172,22 @@
         z_ref[s, 1] = in_ref[held // PAIR_MOST, pl.ds(pl.multiple_of(held % PAIR_MOST * feat, feat), feat)]
 
 
-def join_kernel(mine_ref, in_ref, part_ref, z_ref, rows_ref, g_ref, h_sem, g_sem):
+def join_kernel(mine_hbm, in_ref, part_ref, z_ref, mine_ref, rows_ref, g_ref, mine_sem, h_sem, g_sem):
     del part_ref
     peers, most = in_ref.shape[0], PAIR_MOST
     slots = z_ref.shape[0]
     row_tiles, feat, width = g_ref.shape
     halves = width // LANES
+    load = pltpu.make_async_copy(mine_hbm, mine_ref, mine_sem)
+    load.start()
+    step = halves * row_tiles
+    for r in range(peers):
+        rows_ref[r * step : (r + 1) * step] = in_ref[r, halves * most * feat :].astype(jnp.float32)
+    for t in range(row_tiles):
+        for half in range(halves):
+            of_tile = rows_ref[pl.ds(half * row_tiles + t, feat, stride=step)].astype(g_ref.dtype)
+            g_ref[t, :, half * LANES : (half + 1) * LANES] = of_tile
+    load.wait()
     copies = []
     for s in range(slots):
         held = jnp.maximum(mine_ref[s], 0)
@@ -179,13 +197,6 @@
             place = z_ref.at[s, 2, :, pl.ds(half * LANES, LANES)]
             copies.append(pltpu.make_async_copy(tile, place, h_sem.at[s * halves + half]))
             copies[-1].start()
-    step = halves * row_tiles
-    for r in range(peers):
-        rows_ref[r * step : (r + 1) * step] = in_ref[r, halves * most * feat :].astype(jnp.float32)
-    for t in range(row_tiles):
-        for half in range(halves):
-            of_tile = rows_ref[pl.ds(half * row_tiles + t, feat, stride=step)].astype(g_ref.dtype)
-            g_ref[t, :, half * LANES : (half + 1) * LANES] = of_tile
     for s in range(slots):
         copies.append(pltpu.make_async_copy(g_ref.at[mine_ref[slots + s]], z_ref.at[s, 0], g_sem.at[s]))
         copies[-1].start()
@@ -262,14 +273,17 @@
     hg_out = pl.pallas_call(
         h_kernel,
         out_shape=hbm(hg_type),
-        in_specs=[SMEM, SMEM, VMEM, VMEM, VMEM, VMEM],
+        in_specs=[ANY, ANY, VMEM, VMEM, VMEM, VMEM],
         out_specs=HBM,
         compiler_params=PARAMS,
         scratch_shapes=[
+            pltpu.SMEM(mine_type.shape, jnp.int32),
+            pltpu.SMEM(asked_type.shape, jnp.int32),
             tiles,
             pltpu.VMEM((peers * slots, peers * row_tiles), bf16),
             pltpu.VMEM((peers * row_tiles, width), jnp.float32),
             pltpu.VMEM(hg_type.shape, bf16),
+            pltpu.SemaphoreType.DMA((2,)),
             pltpu.SemaphoreType.DMA((STORES,)),
         ],
     )(far(mine), far(asked), near(cols), near(counts), near(xg_in), near(adjacency))
@@ -293,17 +307,19 @@
     z_out = pl.pallas_call(
         join_kernel,
         out_shape=z_type,
-        in_specs=[SMEM, VMEM, HBM],
+        in_specs=[ANY, VMEM, HBM],
         out_specs=HBM,
         compiler_params=PARAMS,
         input_output_aliases={2: 0},
         scratch_shapes=[
+            pltpu.SMEM(mine_type.shape, jnp.int32),
             pltpu.VMEM((hg_type.shape[0] * row_tiles * (width // LANES), LANES), jnp.float32),
             tiles,
+            pltpu.SemaphoreType.DMA,
             pltpu.SemaphoreType.DMA((slots * (width // LANES),)),
             pltpu.SemaphoreType.DMA((slots,)),
         ],
-    )(mine, near(hg_in), z_part)
+    )(far(mine), near(hg_in), z_part)
     z_out, *dy_parts = lax.optimization_barrier((z_out, *dy_parts))
     dy = pl.pallas_call(
         order_kernel,

time: 115 us -> 115 us (level)
  no operation moved by 1% of the time
where the time goes in v12:
time: 115 us; the launch traced here: 114 us
  starting transfers between devices  57.2 us (50%)
  waiting for transfers between devices  42.9 us (37%)
  Pallas kernels  11.2 us (10%)
  matrix products  1.24 us (1%)
    all_to_all x3, waiting for transfers between devices, exchange(): return lax.all_to_all(value, axis, 0, 0, tiled=True)  42.6 us
    ppermute x6, starting transfers between devices, swap(): lax.ppermute(value, 'depth', [(place, place ^ step) for place in places])  30.4 us
    all_to_all x3, starting transfers between devices, exchange(): return lax.all_to_all(value, axis, 0, 0, tiled=True)  26.8 us
    pallas_call x1, Pallas kernels, body(): pl.pallas_call(send_xg_kernel, out_shape=(hbm(xg_type), hbm(asked_type),...  3.57 us
    pallas_call x1, Pallas kernels, body(): pl.pallas_call(h_kernel, out_shape=hbm(hg_type), in_specs=[ANY, ANY, VMEM...  2.55 us
  transfers between devices with their start and end apart: 9, of which 3 were waited for; matrix products, arithmetic and copies ran while one was open for 1% of the time, Pallas kernels for 7%

profile of v12, /device:TPU:34, one launch (start us, length us, event | category | flops | bytes accessed | tf_op | source)
XLA Modules:
  0.0 114.1 jit_solution(4053013517275191633)
XLA Ops:
  0.0 3.6 %shard_map.64 = (bf16[32,80,256]{2,1,0:T(8,128)(2,1)}, s32[2,32]{1,0:T(2,128)}, s32[32]{0:T(128)}, bf16[4,32,256]{2,1,0:T(8,128)(2,1)}, bf16[4,32,256]{2,1,0:T(8...) custom-call(s32[16,32]{1,0:T(8,128)} %bitcast.26, s32[16,32]{1,0:T(8,128)} %bitcast.30, ...), custom_call_target="tpu_custom_call" | custom-call | tf_op jit(solution)/shard_map/pallas_call | solution.py:249
  3.6 0.0 copy-start
  3.6 0.0 copy-start.2
  3.6 0.0 copy-start.4
  3.6 7.8 %all-to-all-start = ((bf16[32,80,256]{2,1,0:T(8,128)(2,1)}), bf16[32,80,256]{2,1,0:T(8,128)(2,1)S(1)}, u32[]{:S(2)}, u32[]{:S(2)}) async-start(bf16[32,80,256]{2,1,0:T(8,128)(2,1)} %get-tuple-element.23), calls=%async_computation | async-start | bytes 2621440 | tf_op jit(solution)/shard_map/all_to_all | solution.py:208
  11.4 9.1 %collective-permute-start = (bf16[4,32,256]{2,1,0:T(8,128)(2,1)}, bf16[4,32,256]{2,1,0:T(8,128)(2,1)S(1)}, u32[]{:S(2)}, u32[]{:S(2)}) collective-permute-start(bf16[4,32,256]{2,1,0:T(8,128)(2,1)} %get-tuple-element.25), channel_id=1, source_target_pairs={{0,128},{32,160},{64,192},{96,224},{128,0},{160,32},{192,64},{224,... | collective-permute-start | bytes 196616 | tf_op jit(solution)/shard_map/ppermute | solution.py:215
  20.5 10.0 %collective-permute-start.1 = (bf16[4,32,256]{2,1,0:T(8,128)(2,1)}, bf16[4,32,256]{2,1,0:T(8,128)(2,1)S(1)}, u32[]{:S(2)}, u32[]{:S(2)}) collective-permute-start(bf16[4,32,256]{2,1,0:T(8,128)(2,1)} %get-tuple-element.26), channel_id=1, source_target_pairs={{0,256},{32,288},{64,320},{96,352},{128,384},{160,416},{192,448},{... | collective-permute-start | bytes 196616 | tf_op jit(solution)/shard_map/ppermute | solution.py:215
  30.5 1.9 %collective-permute-start.2 = (bf16[4,32,256]{2,1,0:T(8,128)(2,1)}, bf16[4,32,256]{2,1,0:T(8,128)(2,1)}, u32[]{:S(2)}, u32[]{:S(2)}) collective-permute-start(bf16[4,32,256]{2,1,0:T(8,128)(2,1)} %get-tuple-element.27), channel_id=1, source_target_pairs={{0,384},{32,416},{64,448},{96,480},{128,256},{160,288},{192,320},{... | collective-permute-start | bytes 196616 | tf_op jit(solution)/shard_map/ppermute | solution.py:215
  32.5 2.6 %shard_map.65 = bf16[32,136,128]{2,1,0:T(8,128)(2,1)} custom-call(s32[32]{0:T(128)} %get-tuple-element.21.mine_hbm.mine_ref, s32[2,32]{1,0:T(2,128)} %get-tuple-element.22.asked_hbm, s32[16,32]{1,0:T(8,128)S(1)} %bitcast.27, s32[1,32]{1,0:T(1,128)S(1)} %bitcast.29, bf16[32,80,256]{2,1,0:T(8,128)(2,1)S(1)} %all-to-all-done.in_ref, ...), custom_call_target="tpu_custom_call" | custom-call | tf_op jit(solution)/shard_map/pallas_call | solution.py:273
  35.0 0.0 copy-start.5
  35.1 7.5 %all-to-all-start.1 = ((bf16[32,136,128]{2,1,0:T(8,128)(2,1)}), bf16[32,136,128]{2,1,0:T(8,128)(2,1)S(1)}, u32[]{:S(2)}, u32[]{:S(2)}) async-start(bf16[32,136,128]{2,1,0:T(8,128)(2,1)} %shard_map.65), calls=%async_computation.1 | async-start | bytes 2228224 | tf_op jit(solution)/shard_map/all_to_all | solution.py:208
  42.6 0.2 collective-permute-done.2.in3_ref
  42.8 1.5 %shard_map.68 = (bf16[4,32,256]{2,1,0:T(8,128)(2,1)}, bf16[4,32,256]{2,1,0:T(8,128)(2,1)}, bf16[4,32,256]{2,1,0:T(8,128)(2,1)}, bf16[4,32,256]{2,1,0:T(8,128)(2,1)}) custom-call(bf16[4,32,256]{2,1,0:T(8,128)(2,1)S(1)} %copy-done.5, bf16[4,32,256]{2,1,0:T(8,128)(2,1)S(1)} %collective-permute-done.in1_ref, ...), custom_call_target="tpu_custom_call" | custom-call | flops 49999998976 | tf_op jit(solution)/shard_map/pallas_call | solution.py:291
  44.4 2.8 %collective-permute-start.3 = (bf16[4,32,256]{2,1,0:T(8,128)(2,1)}, bf16[4,32,256]{2,1,0:T(8,128)(2,1)S(1)}, u32[]{:S(2)}, u32[]{:S(2)}) collective-permute-start(bf16[4,32,256]{2,1,0:T(8,128)(2,1)} %get-tuple-element.29), channel_id=1, source_target_pairs={{0,32},{32,0},{64,96},{96,64},{128,160},{160,128},{192,224},{224,1... | collective-permute-start | bytes 196616 | tf_op jit(solution)/shard_map/ppermute | solution.py:215
  47.1 4.1 %collective-permute-start.4 = (bf16[4,32,256]{2,1,0:T(8,128)(2,1)}, bf16[4,32,256]{2,1,0:T(8,128)(2,1)S(1)}, u32[]{:S(2)}, u32[]{:S(2)}) collective-permute-start(bf16[4,32,256]{2,1,0:T(8,128)(2,1)} %get-tuple-element.30), channel_id=1, source_target_pairs={{0,64},{32,96},{64,0},{96,32},{128,192},{160,224},{192,128},{224,1... | collective-permute-start | bytes 196616 | tf_op jit(solution)/shard_map/ppermute | solution.py:215
  51.3 2.5 %collective-permute-start.5 = (bf16[4,32,256]{2,1,0:T(8,128)(2,1)}, bf16[4,32,256]{2,1,0:T(8,128)(2,1)S(1)}, u32[]{:S(2)}, u32[]{:S(2)}) collective-permute-start(bf16[4,32,256]{2,1,0:T(8,128)(2,1)} %get-tuple-element.31), channel_id=1, source_target_pairs={{0,96},{32,64},{64,32},{96,0},{128,224},{160,192},{192,160},{224,1... | collective-permute-start | bytes 196616 | tf_op jit(solution)/shard_map/ppermute | solution.py:215
  53.8 1.5 %shard_map.66.part_ref = bf16[16,3,32,256]{3,2,1,0:T(8,128)(2,1)} custom-call(s32[32]{0:T(128)S(1)} %copy-done.3, bf16[32,80,256]{2,1,0:T(8,128)(2,1)S(1)} %all-to-all-done.in_ref), custom_call_target="tpu_custom_call" | custom-call | tf_op jit(solution)/shard_map/pallas_call | solution.py:300
  55.3 4.1 %all-to-all-done.1.in_ref = bf16[32,136,128]{2,1,0:T(8,128)(2,1)S(1)} async-done(((bf16[32,136,128]{2,1,0:T(8,128)(2,1)}), bf16[32,136,128]{2,1,0:T(8,128)(2,1)S(1)}, u32[]{:S(2)}, u32[]{:S(2)}) %all-to-all-start.1) | async-done | bytes 1114144 | tf_op jit(solution)/shard_map/all_to_all | solution.py:208
  59.4 2.0 %shard_map.67 = bf16[16,3,32,256]{3,2,1,0:T(8,128)(2,1)} custom-call(s32[32]{0:T(128)} %get-tuple-element.21.mine_hbm.mine_ref, bf16[32,136,128]{2,1,0:T(8,128)(2,1)S(1)} %all-to-all-done.1.in_ref, bf16[16,3,32,256]{3,2,1,0:T(8,128)(2,1)} %shard_map.66.part_ref), custom_call_target="tpu_custom_call", output_to_operand_aliasing={{}: (2, {})} | custom-call | tf_op jit(solution)/shard_map/pallas_call | solution.py:307
  61.4 11.5 %all-to-all-start.2 = ((bf16[16,3,32,256]{3,2,1,0:T(8,128)(2,1)}), bf16[16,3,32,256]{3,2,1,0:T(8,128)(2,1)S(1)}, u32[]{:S(2)}, u32[]{:S(2)}) async-start(bf16[16,3,32,256]{3,2,1,0:T(8,128)(2,1)} %shard_map.67), calls=%async_computation.2 | async-start | bytes 1572864 | tf_op jit(solution)/shard_map/all_to_all | solution.py:208
  72.9 0.7 dynamic_slice.4
  74.3 38.5 %all-to-all-done.2 = bf16[16,3,32,256]{3,2,1,0:T(8,128)(2,1)S(1)} async-done(((bf16[16,3,32,256]{3,2,1,0:T(8,128)(2,1)}), bf16[16,3,32,256]{3,2,1,0:T(8,128)(2,1)S(1)}, u32[]{:S(2)}, u32[]{:S(2)}) %all-to-all-start.2) | async-done | bytes 786464 | tf_op jit(solution)/shard_map/all_to_all | solution.py:208
  112.8 0.3 convolution_bitcast_fusion
  113.1 1.0 fusion.2
  (15 shorter events, 0.1 us)
Async XLA Ops:
  3.6 28.9 %copy-start = (bf16[16,256,256]{2,1,0:T(8,128)(2,1)S(1)}, bf16[16,256,256]{2,1,0:T(8,128)(2,1)}, u32[]{:S(2)}) copy-start(bf16[16,256,256]{2,1,0:T(8,128)(2,1)} %a_ref.1) | copy-start | bytes 6291460
  3.6 28.9 %copy-start.2 = (s32[32,16]{0,1:T(8,128)S(1)}, s32[32,16]{0,1:T(8,128)}, u32[]{:S(2)}) copy-start(s32[32,16]{0,1:T(8,128)} %param.11) | copy-start | bytes 6148
  3.6 28.9 %copy-start.4 = (s32[32]{0:T(128)S(1)}, s32[32]{0:T(128)}, u32[]{:S(2)}) copy-start(s32[32]{0:T(128)} %count_hbm.1) | copy-start | bytes 388
  3.6 28.8 %all-to-all-start = ((bf16[32,80,256]{2,1,0:T(8,128)(2,1)}), bf16[32,80,256]{2,1,0:T(8,128)(2,1)S(1)}, u32[]{:S(2)}, u32[]{:S(2)}) async-start(bf16[32,80,256]{2,1,0:T(8,128)(2,1)} %get-tuple-element.23), calls=%async_computation | async-start | bytes 2621440 | tf_op jit(solution)/shard_map/all_to_all | solution.py:208
  11.4 31.2 %collective-permute-start = (bf16[4,32,256]{2,1,0:T(8,128)(2,1)}, bf16[4,32,256]{2,1,0:T(8,128)(2,1)S(1)}, u32[]{:S(2)}, u32[]{:S(2)}) collective-permute-start(bf16[4,32,256]{2,1,0:T(8,128)(2,1)} %get-tuple-element.25), channel_id=1, source_target_pairs={{0,128},{32,160},{64,192},{96,224},{128,0},{160,32},{192,64},{224,... | collective-permute-start | bytes 196616 | tf_op jit(solution)/shard_map/ppermute | solution.py:215
  20.5 22.1 %collective-permute-start.1 = (bf16[4,32,256]{2,1,0:T(8,128)(2,1)}, bf16[4,32,256]{2,1,0:T(8,128)(2,1)S(1)}, u32[]{:S(2)}, u32[]{:S(2)}) collective-permute-start(bf16[4,32,256]{2,1,0:T(8,128)(2,1)} %get-tuple-element.26), channel_id=1, source_target_pairs={{0,256},{32,288},{64,320},{96,352},{128,384},{160,416},{192,448},{... | collective-permute-start | bytes 196616 | tf_op jit(solution)/shard_map/ppermute | solution.py:215
  30.5 12.3 %collective-permute-start.2 = (bf16[4,32,256]{2,1,0:T(8,128)(2,1)}, bf16[4,32,256]{2,1,0:T(8,128)(2,1)}, u32[]{:S(2)}, u32[]{:S(2)}) collective-permute-start(bf16[4,32,256]{2,1,0:T(8,128)(2,1)} %get-tuple-element.27), channel_id=1, source_target_pairs={{0,384},{32,416},{64,448},{96,480},{128,256},{160,288},{192,320},{... | collective-permute-start | bytes 196616 | tf_op jit(solution)/shard_map/ppermute | solution.py:215
  35.0 7.8 %copy-start.5 = (bf16[4,32,256]{2,1,0:T(8,128)(2,1)S(1)}, bf16[4,32,256]{2,1,0:T(8,128)(2,1)}, u32[]{:S(2)}) copy-start(bf16[4,32,256]{2,1,0:T(8,128)(2,1)} %get-tuple-element.24.in0_ref) | copy-start | bytes 196612
  35.1 24.3 %all-to-all-start.1 = ((bf16[32,136,128]{2,1,0:T(8,128)(2,1)}), bf16[32,136,128]{2,1,0:T(8,128)(2,1)S(1)}, u32[]{:S(2)}, u32[]{:S(2)}) async-start(bf16[32,136,128]{2,1,0:T(8,128)(2,1)} %shard_map.65), calls=%async_computation.1 | async-start | bytes 2228224 | tf_op jit(solution)/shard_map/all_to_all | solution.py:208
  42.8 10.9 %copy-start.3 = (s32[32]{0:T(128)S(1)}, s32[32]{0:T(128)}, u32[]{:S(2)}) copy-start(s32[32]{0:T(128)} %get-tuple-element.21.mine_hbm.mine_ref) | copy-start | bytes 388
  44.4 17.0 %collective-permute-start.3 = (bf16[4,32,256]{2,1,0:T(8,128)(2,1)}, bf16[4,32,256]{2,1,0:T(8,128)(2,1)S(1)}, u32[]{:S(2)}, u32[]{:S(2)}) collective-permute-start(bf16[4,32,256]{2,1,0:T(8,128)(2,1)} %get-tuple-element.29), channel_id=1, source_target_pairs={{0,32},{32,0},{64,96},{96,64},{128,160},{160,128},{192,224},{224,1... | collective-permute-start | bytes 196616 | tf_op jit(solution)/shard_map/ppermute | solution.py:215
  47.1 14.3 %collective-permute-start.4 = (bf16[4,32,256]{2,1,0:T(8,128)(2,1)}, bf16[4,32,256]{2,1,0:T(8,128)(2,1)S(1)}, u32[]{:S(2)}, u32[]{:S(2)}) collective-permute-start(bf16[4,32,256]{2,1,0:T(8,128)(2,1)} %get-tuple-element.30), channel_id=1, source_target_pairs={{0,64},{32,96},{64,0},{96,32},{128,192},{160,224},{192,128},{224,1... | collective-permute-start | bytes 196616 | tf_op jit(solution)/shard_map/ppermute | solution.py:215
  51.3 10.1 %collective-permute-start.5 = (bf16[4,32,256]{2,1,0:T(8,128)(2,1)}, bf16[4,32,256]{2,1,0:T(8,128)(2,1)S(1)}, u32[]{:S(2)}, u32[]{:S(2)}) collective-permute-start(bf16[4,32,256]{2,1,0:T(8,128)(2,1)} %get-tuple-element.31), channel_id=1, source_target_pairs={{0,96},{32,64},{64,32},{96,0},{128,224},{160,192},{192,160},{224,1... | collective-permute-start | bytes 196616 | tf_op jit(solution)/shard_map/ppermute | solution.py:215
  61.4 12.9 %copy-start.1 = (bf16[4,32,256]{2,1,0:T(8,128)(2,1)S(1)}, bf16[4,32,256]{2,1,0:T(8,128)(2,1)}, u32[]{:S(2)}) copy-start(bf16[4,32,256]{2,1,0:T(8,128)(2,1)} %get-tuple-element.32.in0_ref) | copy-start | bytes 196612
  61.4 51.4 %all-to-all-start.2 = ((bf16[16,3,32,256]{3,2,1,0:T(8,128)(2,1)}), bf16[16,3,32,256]{3,2,1,0:T(8,128)(2,1)S(1)}, u32[]{:S(2)}, u32[]{:S(2)}) async-start(bf16[16,3,32,256]{3,2,1,0:T(8,128)(2,1)} %shard_map.67), calls=%async_computation.2 | async-start | bytes 1572864 | tf_op jit(solution)/shard_map/all_to_all | solution.py:208

commit v13 on v12

--- a/solution.py
+++ b/solution.py
@@ -10,6 +10,7 @@
 STORES = 4
 LANES = 128
 GROUP = 4
+ORDER = (0, 2, 1, 3)
 SMEM = pl.BlockSpec(memory_space=pltpu.SMEM)
 VMEM = pl.BlockSpec(memory_space=pltpu.VMEM)
 ANY = pl.BlockSpec(memory_space=pl.ANY)
@@ -155,7 +156,7 @@
 
 def turn_kernel(in0_ref, in1_ref, in2_ref, in3_ref, out0_ref, out1_ref, out2_ref, out3_ref):
     for e, out_ref in enumerate((out0_ref, out1_ref, out2_ref, out3_ref)):
-        for g, in_ref in enumerate((in0_ref, in1_ref, in2_ref, in3_ref)):
+        for g, in_ref in zip(ORDER, (in0_ref, in1_ref, in2_ref, in3_ref)):
             out_ref[g] = in_ref[lax.axis_index("depth") % GROUP ^ e]
 
 
@@ -269,7 +270,7 @@
         ],
     )(far(cols), far(tile_row.T), far(tile_count), far(counts), node_feat, grad_out, adjacency)
     xg_in = exchange(xg_out, "rows")
-    dy_parts = [swap(part, GROUP * step) for step, part in enumerate(dy_parts)]
+    dy_parts = [swap(dy_parts[step], GROUP * step) for step in ORDER]
     hg_out = pl.pallas_call(
         h_kernel,
         out_shape=hbm(hg_type),

time: 115 us -> 115 us (level)
  no operation moved by 1% of the time
where the time goes in v13:
time: 115 us; the launch traced here: 114 us
  starting transfers between devices  57 us (50%)
  waiting for transfers between devices  43 us (37%)
  Pallas kernels  11.2 us (10%)
  matrix products  1.24 us (1%)
    all_to_all x3, waiting for transfers between devices, exchange(): return lax.all_to_all(value, axis, 0, 0, tiled=True)  41.9 us
    ppermute x6, starting transfers between devices, swap(): lax.ppermute(value, 'depth', [(place, place ^ step) for place in places])  30.2 us
    all_to_all x3, starting transfers between devices, exchange(): return lax.all_to_all(value, axis, 0, 0, tiled=True)  26.8 us
    pallas_call x1, Pallas kernels, body(): pl.pallas_call(send_xg_kernel, out_shape=(hbm(xg_type), hbm(asked_type),...  3.56 us
    pallas_call x1, Pallas kernels, body(): pl.pallas_call(h_kernel, out_shape=hbm(hg_type), in_specs=[ANY, ANY, VMEM...  2.55 us
  transfers between devices with their start and end apart: 9, of which 3 were waited for; matrix products, arithmetic and copies ran while one was open for 1% of the time, Pallas kernels for 7%

profile of v13, /device:TPU:34, one launch (start us, length us, event | category | flops | bytes accessed | tf_op | source)
XLA Modules:
  0.0 114.1 jit_solution(3101832553426726914)
XLA Ops:
  0.0 3.6 %shard_map.64 = (bf16[32,80,256]{2,1,0:T(8,128)(2,1)}, s32[2,32]{1,0:T(2,128)}, s32[32]{0:T(128)}, bf16[4,32,256]{2,1,0:T(8,128)(2,1)}, bf16[4,32,256]{2,1,0:T(8...) custom-call(s32[16,32]{1,0:T(8,128)} %bitcast.26, s32[16,32]{1,0:T(8,128)} %bitcast.30, ...), custom_call_target="tpu_custom_call" | custom-call | tf_op jit(solution)/shard_map/pallas_call | solution.py:250
  3.6 0.0 copy-start
  3.6 0.0 copy-start.2
  3.6 0.0 copy-start.4
  3.6 7.8 %all-to-all-start = ((bf16[32,80,256]{2,1,0:T(8,128)(2,1)}), bf16[32,80,256]{2,1,0:T(8,128)(2,1)S(1)}, u32[]{:S(2)}, u32[]{:S(2)}) async-start(bf16[32,80,256]{2,1,0:T(8,128)(2,1)} %get-tuple-element.23), calls=%async_computation | async-start | bytes 2621440 | tf_op jit(solution)/shard_map/all_to_all | solution.py:209
  11.4 14.8 %collective-permute-start = (bf16[4,32,256]{2,1,0:T(8,128)(2,1)}, bf16[4,32,256]{2,1,0:T(8,128)(2,1)S(1)}, u32[]{:S(2)}, u32[]{:S(2)}) collective-permute-start(bf16[4,32,256]{2,1,0:T(8,128)(2,1)} %get-tuple-element.25), channel_id=1, source_target_pairs={{0,256},{32,288},{64,320},{96,352},{128,384},{160,416},{192,448},{... | collective-permute-start | bytes 196616 | tf_op jit(solution)/shard_map/ppermute | solution.py:216
  26.2 4.3 %collective-permute-start.1 = (bf16[4,32,256]{2,1,0:T(8,128)(2,1)}, bf16[4,32,256]{2,1,0:T(8,128)(2,1)S(1)}, u32[]{:S(2)}, u32[]{:S(2)}) collective-permute-start(bf16[4,32,256]{2,1,0:T(8,128)(2,1)} %get-tuple-element.26), channel_id=1, source_target_pairs={{0,128},{32,160},{64,192},{96,224},{128,0},{160,32},{192,64},{224,... | collective-permute-start | bytes 196616 | tf_op jit(solution)/shard_map/ppermute | solution.py:216
  30.5 1.9 %collective-permute-start.2 = (bf16[4,32,256]{2,1,0:T(8,128)(2,1)}, bf16[4,32,256]{2,1,0:T(8,128)(2,1)}, u32[]{:S(2)}, u32[]{:S(2)}) collective-permute-start(bf16[4,32,256]{2,1,0:T(8,128)(2,1)} %get-tuple-element.27), channel_id=1, source_target_pairs={{0,384},{32,416},{64,448},{96,480},{128,256},{160,288},{192,320},{... | collective-permute-start | bytes 196616 | tf_op jit(solution)/shard_map/ppermute | solution.py:216
  32.5 2.6 %shard_map.65 = bf16[32,136,128]{2,1,0:T(8,128)(2,1)} custom-call(s32[32]{0:T(128)} %get-tuple-element.21.mine_hbm.mine_ref, s32[2,32]{1,0:T(2,128)} %get-tuple-element.22.asked_hbm, s32[16,32]{1,0:T(8,128)S(1)} %bitcast.27, s32[1,32]{1,0:T(1,128)S(1)} %bitcast.29, bf16[32,80,256]{2,1,0:T(8,128)(2,1)S(1)} %all-to-all-done.in_ref, ...), custom_call_target="tpu_custom_call" | custom-call | tf_op jit(solution)/shard_map/pallas_call | solution.py:274
  35.1 7.5 %all-to-all-start.1 = ((bf16[32,136,128]{2,1,0:T(8,128)(2,1)}), bf16[32,136,128]{2,1,0:T(8,128)(2,1)S(1)}, u32[]{:S(2)}, u32[]{:S(2)}) async-start(bf16[32,136,128]{2,1,0:T(8,128)(2,1)} %shard_map.65), calls=%async_computation.1 | async-start | bytes 2228224 | tf_op jit(solution)/shard_map/all_to_all | solution.py:209
  42.6 1.1 collective-permute-done.2.in3_ref
  43.7 1.5 %shard_map.68 = (bf16[4,32,256]{2,1,0:T(8,128)(2,1)}, bf16[4,32,256]{2,1,0:T(8,128)(2,1)}, bf16[4,32,256]{2,1,0:T(8,128)(2,1)}, bf16[4,32,256]{2,1,0:T(8,128)(2,1)}) custom-call(bf16[4,32,256]{2,1,0:T(8,128)(2,1)S(1)} %copy-done.5, bf16[4,32,256]{2,1,0:T(8,128)(2,1)S(1)} %collective-permute-done.in1_ref, ...), custom_call_target="tpu_custom_call" | custom-call | flops 49999998976 | tf_op jit(solution)/shard_map/pallas_call | solution.py:292
  45.2 2.0 %collective-permute-start.3 = (bf16[4,32,256]{2,1,0:T(8,128)(2,1)}, bf16[4,32,256]{2,1,0:T(8,128)(2,1)S(1)}, u32[]{:S(2)}, u32[]{:S(2)}) collective-permute-start(bf16[4,32,256]{2,1,0:T(8,128)(2,1)} %get-tuple-element.29), channel_id=1, source_target_pairs={{0,32},{32,0},{64,96},{96,64},{128,160},{160,128},{192,224},{224,1... | collective-permute-start | bytes 196616 | tf_op jit(solution)/shard_map/ppermute | solution.py:216
  47.3 5.0 %collective-permute-start.4 = (bf16[4,32,256]{2,1,0:T(8,128)(2,1)}, bf16[4,32,256]{2,1,0:T(8,128)(2,1)S(1)}, u32[]{:S(2)}, u32[]{:S(2)}) collective-permute-start(bf16[4,32,256]{2,1,0:T(8,128)(2,1)} %get-tuple-element.30), channel_id=1, source_target_pairs={{0,64},{32,96},{64,0},{96,32},{128,192},{160,224},{192,128},{224,1... | collective-permute-start | bytes 196616 | tf_op jit(solution)/shard_map/ppermute | solution.py:216
  52.2 2.2 %collective-permute-start.5 = (bf16[4,32,256]{2,1,0:T(8,128)(2,1)}, bf16[4,32,256]{2,1,0:T(8,128)(2,1)S(1)}, u32[]{:S(2)}, u32[]{:S(2)}) collective-permute-start(bf16[4,32,256]{2,1,0:T(8,128)(2,1)} %get-tuple-element.31), channel_id=1, source_target_pairs={{0,96},{32,64},{64,32},{96,0},{128,224},{160,192},{192,160},{224,1... | collective-permute-start | bytes 196616 | tf_op jit(solution)/shard_map/ppermute | solution.py:216
  54.5 1.5 %shard_map.66.part_ref = bf16[16,3,32,256]{3,2,1,0:T(8,128)(2,1)} custom-call(s32[32]{0:T(128)S(1)} %copy-done.3, bf16[32,80,256]{2,1,0:T(8,128)(2,1)S(1)} %all-to-all-done.in_ref), custom_call_target="tpu_custom_call" | custom-call | tf_op jit(solution)/shard_map/pallas_call | solution.py:301
  56.0 3.4 %all-to-all-done.1.in_ref = bf16[32,136,128]{2,1,0:T(8,128)(2,1)S(1)} async-done(((bf16[32,136,128]{2,1,0:T(8,128)(2,1)}), bf16[32,136,128]{2,1,0:T(8,128)(2,1)S(1)}, u32[]{:S(2)}, u32[]{:S(2)}) %all-to-all-start.1) | async-done | bytes 1114144 | tf_op jit(solution)/shard_map/all_to_all | solution.py:209
  59.4 2.0 %shard_map.67 = bf16[16,3,32,256]{3,2,1,0:T(8,128)(2,1)} custom-call(s32[32]{0:T(128)} %get-tuple-element.21.mine_hbm.mine_ref, bf16[32,136,128]{2,1,0:T(8,128)(2,1)S(1)} %all-to-all-done.1.in_ref, bf16[16,3,32,256]{3,2,1,0:T(8,128)(2,1)} %shard_map.66.part_ref), custom_call_target="tpu_custom_call", output_to_operand_aliasing={{}: (2, {})} | custom-call | tf_op jit(solution)/shard_map/pallas_call | solution.py:308
  61.4 0.0 copy-start.1
  61.4 11.5 %all-to-all-start.2 = ((bf16[16,3,32,256]{3,2,1,0:T(8,128)(2,1)}), bf16[16,3,32,256]{3,2,1,0:T(8,128)(2,1)S(1)}, u32[]{:S(2)}, u32[]{:S(2)}) async-start(bf16[16,3,32,256]{3,2,1,0:T(8,128)(2,1)} %shard_map.67), calls=%async_computation.2 | async-start | bytes 1572864 | tf_op jit(solution)/shard_map/all_to_all | solution.py:209
  72.9 0.7 dynamic_slice.4
  74.3 38.5 %all-to-all-done.2 = bf16[16,3,32,256]{3,2,1,0:T(8,128)(2,1)S(1)} async-done(((bf16[16,3,32,256]{3,2,1,0:T(8,128)(2,1)}), bf16[16,3,32,256]{3,2,1,0:T(8,128)(2,1)S(1)}, u32[]{:S(2)}, u32[]{:S(2)}) %all-to-all-start.2) | async-done | bytes 786464 | tf_op jit(solution)/shard_map/all_to_all | solution.py:209
  112.8 0.3 convolution_bitcast_fusion
  113.1 1.0 fusion.2
  (15 shorter events, 0.1 us)
Async XLA Ops:
  3.6 28.9 %copy-start = (bf16[16,256,256]{2,1,0:T(8,128)(2,1)S(1)}, bf16[16,256,256]{2,1,0:T(8,128)(2,1)}, u32[]{:S(2)}) copy-start(bf16[16,256,256]{2,1,0:T(8,128)(2,1)} %a_ref.1) | copy-start | bytes 6291460
  3.6 28.9 %copy-start.2 = (s32[32,16]{0,1:T(8,128)S(1)}, s32[32,16]{0,1:T(8,128)}, u32[]{:S(2)}) copy-start(s32[32,16]{0,1:T(8,128)} %param.11) | copy-start | bytes 6148
  3.6 28.9 %copy-start.4 = (s32[32]{0:T(128)S(1)}, s32[32]{0:T(128)}, u32[]{:S(2)}) copy-start(s32[32]{0:T(128)} %count_hbm.1) | copy-start | bytes 388
  3.6 28.8 %all-to-all-start = ((bf16[32,80,256]{2,1,0:T(8,128)(2,1)}), bf16[32,80,256]{2,1,0:T(8,128)(2,1)S(1)}, u32[]{:S(2)}, u32[]{:S(2)}) async-start(bf16[32,80,256]{2,1,0:T(8,128)(2,1)} %get-tuple-element.23), calls=%async_computation | async-start | bytes 2621440 | tf_op jit(solution)/shard_map/all_to_all | solution.py:209
  11.4 31.2 %collective-permute-start = (bf16[4,32,256]{2,1,0:T(8,128)(2,1)}, bf16[4,32,256]{2,1,0:T(8,128)(2,1)S(1)}, u32[]{:S(2)}, u32[]{:S(2)}) collective-permute-start(bf16[4,32,256]{2,1,0:T(8,128)(2,1)} %get-tuple-element.25), channel_id=1, source_target_pairs={{0,256},{32,288},{64,320},{96,352},{128,384},{160,416},{192,448},{... | collective-permute-start | bytes 196616 | tf_op jit(solution)/shard_map/ppermute | solution.py:216
  26.2 16.4 %collective-permute-start.1 = (bf16[4,32,256]{2,1,0:T(8,128)(2,1)}, bf16[4,32,256]{2,1,0:T(8,128)(2,1)S(1)}, u32[]{:S(2)}, u32[]{:S(2)}) collective-permute-start(bf16[4,32,256]{2,1,0:T(8,128)(2,1)} %get-tuple-element.26), channel_id=1, source_target_pairs={{0,128},{32,160},{64,192},{96,224},{128,0},{160,32},{192,64},{224,... | collective-permute-start | bytes 196616 | tf_op jit(solution)/shard_map/ppermute | solution.py:216
  30.5 13.2 %collective-permute-start.2 = (bf16[4,32,256]{2,1,0:T(8,128)(2,1)}, bf16[4,32,256]{2,1,0:T(8,128)(2,1)}, u32[]{:S(2)}, u32[]{:S(2)}) collective-permute-start(bf16[4,32,256]{2,1,0:T(8,128)(2,1)} %get-tuple-element.27), channel_id=1, source_target_pairs={{0,384},{32,416},{64,448},{96,480},{128,256},{160,288},{192,320},{... | collective-permute-start | bytes 196616 | tf_op jit(solution)/shard_map/ppermute | solution.py:216
  35.0 8.6 %copy-start.5 = (bf16[4,32,256]{2,1,0:T(8,128)(2,1)S(1)}, bf16[4,32,256]{2,1,0:T(8,128)(2,1)}, u32[]{:S(2)}) copy-start(bf16[4,32,256]{2,1,0:T(8,128)(2,1)} %get-tuple-element.24.in0_ref) | copy-start | bytes 196612
  35.1 24.3 %all-to-all-start.1 = ((bf16[32,136,128]{2,1,0:T(8,128)(2,1)}), bf16[32,136,128]{2,1,0:T(8,128)(2,1)S(1)}, u32[]{:S(2)}, u32[]{:S(2)}) async-start(bf16[32,136,128]{2,1,0:T(8,128)(2,1)} %shard_map.65), calls=%async_computation.1 | async-start | bytes 2228224 | tf_op jit(solution)/shard_map/all_to_all | solution.py:209
  43.7 10.8 %copy-start.3 = (s32[32]{0:T(128)S(1)}, s32[32]{0:T(128)}, u32[]{:S(2)}) copy-start(s32[32]{0:T(128)} %get-tuple-element.21.mine_hbm.mine_ref) | copy-start | bytes 388
  45.2 16.2 %collective-permute-start.3 = (bf16[4,32,256]{2,1,0:T(8,128)(2,1)}, bf16[4,32,256]{2,1,0:T(8,128)(2,1)S(1)}, u32[]{:S(2)}, u32[]{:S(2)}) collective-permute-start(bf16[4,32,256]{2,1,0:T(8,128)(2,1)} %get-tuple-element.29), channel_id=1, source_target_pairs={{0,32},{32,0},{64,96},{96,64},{128,160},{160,128},{192,224},{224,1... | collective-permute-start | bytes 196616 | tf_op jit(solution)/shard_map/ppermute | solution.py:216
  47.3 14.1 %collective-permute-start.4 = (bf16[4,32,256]{2,1,0:T(8,128)(2,1)}, bf16[4,32,256]{2,1,0:T(8,128)(2,1)S(1)}, u32[]{:S(2)}, u32[]{:S(2)}) collective-permute-start(bf16[4,32,256]{2,1,0:T(8,128)(2,1)} %get-tuple-element.30), channel_id=1, source_target_pairs={{0,64},{32,96},{64,0},{96,32},{128,192},{160,224},{192,128},{224,1... | collective-permute-start | bytes 196616 | tf_op jit(solution)/shard_map/ppermute | solution.py:216
  52.2 9.2 %collective-permute-start.5 = (bf16[4,32,256]{2,1,0:T(8,128)(2,1)}, bf16[4,32,256]{2,1,0:T(8,128)(2,1)S(1)}, u32[]{:S(2)}, u32[]{:S(2)}) collective-permute-start(bf16[4,32,256]{2,1,0:T(8,128)(2,1)} %get-tuple-element.31), channel_id=1, source_target_pairs={{0,96},{32,64},{64,32},{96,0},{128,224},{160,192},{192,160},{224,1... | collective-permute-start | bytes 196616 | tf_op jit(solution)/shard_map/ppermute | solution.py:216
  61.4 12.9 %copy-start.1 = (bf16[4,32,256]{2,1,0:T(8,128)(2,1)S(1)}, bf16[4,32,256]{2,1,0:T(8,128)(2,1)}, u32[]{:S(2)}) copy-start(bf16[4,32,256]{2,1,0:T(8,128)(2,1)} %get-tuple-element.32.in0_ref) | copy-start | bytes 196612
  61.4 51.4 %all-to-all-start.2 = ((bf16[16,3,32,256]{3,2,1,0:T(8,128)(2,1)}), bf16[16,3,32,256]{3,2,1,0:T(8,128)(2,1)S(1)}, u32[]{:S(2)}, u32[]{:S(2)}) async-start(bf16[16,3,32,256]{3,2,1,0:T(8,128)(2,1)} %shard_map.67), calls=%async_computation.2 | async-start | bytes 1572864 | tf_op jit(solution)/shard_map/all_to_all | solution.py:209

commit v14 on v12

--- a/solution.py
+++ b/solution.py
@@ -7,7 +7,7 @@
 
 PAIR_MOST = 2
 LOADS = 2
-STORES = 4
+STORES = 2
 LANES = 128
 GROUP = 4
 SMEM = pl.BlockSpec(memory_space=pltpu.SMEM)

time: 115 us -> 115 us (level)
  no operation moved by 1% of the time
where the time goes in v14:
time: 115 us; the launch traced here: 114 us
  starting transfers between devices  57.2 us (50%)
  waiting for transfers between devices  42.9 us (37%)
  Pallas kernels  11.2 us (10%)
  matrix products  1.24 us (1%)
    all_to_all x3, waiting for transfers between devices, exchange(): return lax.all_to_all(value, axis, 0, 0, tiled=True)  42.7 us
    ppermute x6, starting transfers between devices, swap(): lax.ppermute(value, 'depth', [(place, place ^ step) for place in places])  30.4 us
    all_to_all x3, starting transfers between devices, exchange(): return lax.all_to_all(value, axis, 0, 0, tiled=True)  26.8 us
    pallas_call x1, Pallas kernels, body(): pl.pallas_call(send_xg_kernel, out_shape=(hbm(xg_type), hbm(asked_type),...  3.56 us
    pallas_call x1, Pallas kernels, body(): pl.pallas_call(h_kernel, out_shape=hbm(hg_type), in_specs=[ANY, ANY, VMEM...  2.59 us
  transfers between devices with their start and end apart: 9, of which 3 were waited for; matrix products, arithmetic and copies ran while one was open for 1% of the time, Pallas kernels for 7%

profile of v14, /device:TPU:34, one launch (start us, length us, event | category | flops | bytes accessed | tf_op | source)
XLA Modules:
  0.0 114.1 jit_solution(17206979324207687062)
XLA Ops:
  0.0 3.6 %shard_map.64 = (bf16[32,80,256]{2,1,0:T(8,128)(2,1)}, s32[2,32]{1,0:T(2,128)}, s32[32]{0:T(128)}, bf16[4,32,256]{2,1,0:T(8,128)(2,1)}, bf16[4,32,256]{2,1,0:T(8...) custom-call(s32[16,32]{1,0:T(8,128)} %bitcast.26, s32[16,32]{1,0:T(8,128)} %bitcast.30, ...), custom_call_target="tpu_custom_call" | custom-call | tf_op jit(solution)/shard_map/pallas_call | solution.py:249
  3.6 0.0 copy-start
  3.6 0.0 copy-start.2
  3.6 7.8 %all-to-all-start = ((bf16[32,80,256]{2,1,0:T(8,128)(2,1)}), bf16[32,80,256]{2,1,0:T(8,128)(2,1)S(1)}, u32[]{:S(2)}, u32[]{:S(2)}) async-start(bf16[32,80,256]{2,1,0:T(8,128)(2,1)} %get-tuple-element.23), calls=%async_computation | async-start | bytes 2621440 | tf_op jit(solution)/shard_map/all_to_all | solution.py:208
  11.4 9.1 %collective-permute-start = (bf16[4,32,256]{2,1,0:T(8,128)(2,1)}, bf16[4,32,256]{2,1,0:T(8,128)(2,1)S(1)}, u32[]{:S(2)}, u32[]{:S(2)}) collective-permute-start(bf16[4,32,256]{2,1,0:T(8,128)(2,1)} %get-tuple-element.25), channel_id=1, source_target_pairs={{0,128},{32,160},{64,192},{96,224},{128,0},{160,32},{192,64},{224,... | collective-permute-start | bytes 196616 | tf_op jit(solution)/shard_map/ppermute | solution.py:215
  20.5 10.0 %collective-permute-start.1 = (bf16[4,32,256]{2,1,0:T(8,128)(2,1)}, bf16[4,32,256]{2,1,0:T(8,128)(2,1)S(1)}, u32[]{:S(2)}, u32[]{:S(2)}) collective-permute-start(bf16[4,32,256]{2,1,0:T(8,128)(2,1)} %get-tuple-element.26), channel_id=1, source_target_pairs={{0,256},{32,288},{64,320},{96,352},{128,384},{160,416},{192,448},{... | collective-permute-start | bytes 196616 | tf_op jit(solution)/shard_map/ppermute | solution.py:215
  30.5 1.9 %collective-permute-start.2 = (bf16[4,32,256]{2,1,0:T(8,128)(2,1)}, bf16[4,32,256]{2,1,0:T(8,128)(2,1)}, u32[]{:S(2)}, u32[]{:S(2)}) collective-permute-start(bf16[4,32,256]{2,1,0:T(8,128)(2,1)} %get-tuple-element.27), channel_id=1, source_target_pairs={{0,384},{32,416},{64,448},{96,480},{128,256},{160,288},{192,320},{... | collective-permute-start | bytes 196616 | tf_op jit(solution)/shard_map/ppermute | solution.py:215
  32.5 2.6 %shard_map.65 = bf16[32,136,128]{2,1,0:T(8,128)(2,1)} custom-call(s32[32]{0:T(128)} %get-tuple-element.21.mine_hbm.mine_ref, s32[2,32]{1,0:T(2,128)} %get-tuple-element.22.asked_hbm, s32[16,32]{1,0:T(8,128)S(1)} %bitcast.27, s32[1,32]{1,0:T(1,128)S(1)} %bitcast.29, bf16[32,80,256]{2,1,0:T(8,128)(2,1)S(1)} %all-to-all-done.in_ref, ...), custom_call_target="tpu_custom_call" | custom-call | tf_op jit(solution)/shard_map/pallas_call | solution.py:273
  35.1 0.0 copy-start.5
  35.1 7.5 %all-to-all-start.1 = ((bf16[32,136,128]{2,1,0:T(8,128)(2,1)}), bf16[32,136,128]{2,1,0:T(8,128)(2,1)S(1)}, u32[]{:S(2)}, u32[]{:S(2)}) async-start(bf16[32,136,128]{2,1,0:T(8,128)(2,1)} %shard_map.65), calls=%async_computation.1 | async-start | bytes 2228224 | tf_op jit(solution)/shard_map/all_to_all | solution.py:208
  42.6 0.2 collective-permute-done.2.in3_ref
  42.8 1.5 %shard_map.68 = (bf16[4,32,256]{2,1,0:T(8,128)(2,1)}, bf16[4,32,256]{2,1,0:T(8,128)(2,1)}, bf16[4,32,256]{2,1,0:T(8,128)(2,1)}, bf16[4,32,256]{2,1,0:T(8,128)(2,1)}) custom-call(bf16[4,32,256]{2,1,0:T(8,128)(2,1)S(1)} %copy-done.5, bf16[4,32,256]{2,1,0:T(8,128)(2,1)S(1)} %collective-permute-done.in1_ref, ...), custom_call_target="tpu_custom_call" | custom-call | flops 49999998976 | tf_op jit(solution)/shard_map/pallas_call | solution.py:291
  44.4 2.8 %collective-permute-start.3 = (bf16[4,32,256]{2,1,0:T(8,128)(2,1)}, bf16[4,32,256]{2,1,0:T(8,128)(2,1)S(1)}, u32[]{:S(2)}, u32[]{:S(2)}) collective-permute-start(bf16[4,32,256]{2,1,0:T(8,128)(2,1)} %get-tuple-element.29), channel_id=1, source_target_pairs={{0,32},{32,0},{64,96},{96,64},{128,160},{160,128},{192,224},{224,1... | collective-permute-start | bytes 196616 | tf_op jit(solution)/shard_map/ppermute | solution.py:215
  47.1 4.1 %collective-permute-start.4 = (bf16[4,32,256]{2,1,0:T(8,128)(2,1)}, bf16[4,32,256]{2,1,0:T(8,128)(2,1)S(1)}, u32[]{:S(2)}, u32[]{:S(2)}) collective-permute-start(bf16[4,32,256]{2,1,0:T(8,128)(2,1)} %get-tuple-element.30), channel_id=1, source_target_pairs={{0,64},{32,96},{64,0},{96,32},{128,192},{160,224},{192,128},{224,1... | collective-permute-start | bytes 196616 | tf_op jit(solution)/shard_map/ppermute | solution.py:215
  51.3 2.5 %collective-permute-start.5 = (bf16[4,32,256]{2,1,0:T(8,128)(2,1)}, bf16[4,32,256]{2,1,0:T(8,128)(2,1)S(1)}, u32[]{:S(2)}, u32[]{:S(2)}) collective-permute-start(bf16[4,32,256]{2,1,0:T(8,128)(2,1)} %get-tuple-element.31), channel_id=1, source_target_pairs={{0,96},{32,64},{64,32},{96,0},{128,224},{160,192},{192,160},{224,1... | collective-permute-start | bytes 196616 | tf_op jit(solution)/shard_map/ppermute | solution.py:215
  53.8 1.5 %shard_map.66.part_ref = bf16[16,3,32,256]{3,2,1,0:T(8,128)(2,1)} custom-call(s32[32]{0:T(128)S(1)} %copy-done.3, bf16[32,80,256]{2,1,0:T(8,128)(2,1)S(1)} %all-to-all-done.in_ref), custom_call_target="tpu_custom_call" | custom-call | tf_op jit(solution)/shard_map/pallas_call | solution.py:300
  55.3 4.1 %all-to-all-done.1.in_ref = bf16[32,136,128]{2,1,0:T(8,128)(2,1)S(1)} async-done(((bf16[32,136,128]{2,1,0:T(8,128)(2,1)}), bf16[32,136,128]{2,1,0:T(8,128)(2,1)S(1)}, u32[]{:S(2)}, u32[]{:S(2)}) %all-to-all-start.1) | async-done | bytes 1114144 | tf_op jit(solution)/shard_map/all_to_all | solution.py:208
  59.4 2.0 %shard_map.67 = bf16[16,3,32,256]{3,2,1,0:T(8,128)(2,1)} custom-call(s32[32]{0:T(128)} %get-tuple-element.21.mine_hbm.mine_ref, bf16[32,136,128]{2,1,0:T(8,128)(2,1)S(1)} %all-to-all-done.1.in_ref, bf16[16,3,32,256]{3,2,1,0:T(8,128)(2,1)} %shard_map.66.part_ref), custom_call_target="tpu_custom_call", output_to_operand_aliasing={{}: (2, {})} | custom-call | tf_op jit(solution)/shard_map/pallas_call | solution.py:307
  61.4 0.0 copy-start.1
  61.4 11.5 %all-to-all-start.2 = ((bf16[16,3,32,256]{3,2,1,0:T(8,128)(2,1)}), bf16[16,3,32,256]{3,2,1,0:T(8,128)(2,1)S(1)}, u32[]{:S(2)}, u32[]{:S(2)}) async-start(bf16[16,3,32,256]{3,2,1,0:T(8,128)(2,1)} %shard_map.67), calls=%async_computation.2 | async-start | bytes 1572864 | tf_op jit(solution)/shard_map/all_to_all | solution.py:208
  72.9 0.7 dynamic_slice.4
  74.3 38.5 %all-to-all-done.2 = bf16[16,3,32,256]{3,2,1,0:T(8,128)(2,1)S(1)} async-done(((bf16[16,3,32,256]{3,2,1,0:T(8,128)(2,1)}), bf16[16,3,32,256]{3,2,1,0:T(8,128)(2,1)S(1)}, u32[]{:S(2)}, u32[]{:S(2)}) %all-to-all-start.2) | async-done | bytes 786464 | tf_op jit(solution)/shard_map/all_to_all | solution.py:208
  112.9 0.3 convolution_bitcast_fusion
  113.1 1.0 fusion.2
  (15 shorter events, 0.1 us)
Async XLA Ops:
  3.6 28.9 %copy-start = (bf16[16,256,256]{2,1,0:T(8,128)(2,1)S(1)}, bf16[16,256,256]{2,1,0:T(8,128)(2,1)}, u32[]{:S(2)}) copy-start(bf16[16,256,256]{2,1,0:T(8,128)(2,1)} %a_ref.1) | copy-start | bytes 6291460
  3.6 28.9 %copy-start.2 = (s32[32,16]{0,1:T(8,128)S(1)}, s32[32,16]{0,1:T(8,128)}, u32[]{:S(2)}) copy-start(s32[32,16]{0,1:T(8,128)} %param.11) | copy-start | bytes 6148
  3.6 28.9 %copy-start.4 = (s32[32]{0:T(128)S(1)}, s32[32]{0:T(128)}, u32[]{:S(2)}) copy-start(s32[32]{0:T(128)} %count_hbm.1) | copy-start | bytes 388
  3.6 28.8 %all-to-all-start = ((bf16[32,80,256]{2,1,0:T(8,128)(2,1)}), bf16[32,80,256]{2,1,0:T(8,128)(2,1)S(1)}, u32[]{:S(2)}, u32[]{:S(2)}) async-start(bf16[32,80,256]{2,1,0:T(8,128)(2,1)} %get-tuple-element.23), calls=%async_computation | async-start | bytes 2621440 | tf_op jit(solution)/shard_map/all_to_all | solution.py:208
  11.4 31.2 %collective-permute-start = (bf16[4,32,256]{2,1,0:T(8,128)(2,1)}, bf16[4,32,256]{2,1,0:T(8,128)(2,1)S(1)}, u32[]{:S(2)}, u32[]{:S(2)}) collective-permute-start(bf16[4,32,256]{2,1,0:T(8,128)(2,1)} %get-tuple-element.25), channel_id=1, source_target_pairs={{0,128},{32,160},{64,192},{96,224},{128,0},{160,32},{192,64},{224,... | collective-permute-start | bytes 196616 | tf_op jit(solution)/shard_map/ppermute | solution.py:215
  20.5 22.1 %collective-permute-start.1 = (bf16[4,32,256]{2,1,0:T(8,128)(2,1)}, bf16[4,32,256]{2,1,0:T(8,128)(2,1)S(1)}, u32[]{:S(2)}, u32[]{:S(2)}) collective-permute-start(bf16[4,32,256]{2,1,0:T(8,128)(2,1)} %get-tuple-element.26), channel_id=1, source_target_pairs={{0,256},{32,288},{64,320},{96,352},{128,384},{160,416},{192,448},{... | collective-permute-start | bytes 196616 | tf_op jit(solution)/shard_map/ppermute | solution.py:215
  30.5 12.3 %collective-permute-start.2 = (bf16[4,32,256]{2,1,0:T(8,128)(2,1)}, bf16[4,32,256]{2,1,0:T(8,128)(2,1)}, u32[]{:S(2)}, u32[]{:S(2)}) collective-permute-start(bf16[4,32,256]{2,1,0:T(8,128)(2,1)} %get-tuple-element.27), channel_id=1, source_target_pairs={{0,384},{32,416},{64,448},{96,480},{128,256},{160,288},{192,320},{... | collective-permute-start | bytes 196616 | tf_op jit(solution)/shard_map/ppermute | solution.py:215
  35.1 7.8 %copy-start.5 = (bf16[4,32,256]{2,1,0:T(8,128)(2,1)S(1)}, bf16[4,32,256]{2,1,0:T(8,128)(2,1)}, u32[]{:S(2)}) copy-start(bf16[4,32,256]{2,1,0:T(8,128)(2,1)} %get-tuple-element.24.in0_ref) | copy-start | bytes 196612
  35.1 24.3 %all-to-all-start.1 = ((bf16[32,136,128]{2,1,0:T(8,128)(2,1)}), bf16[32,136,128]{2,1,0:T(8,128)(2,1)S(1)}, u32[]{:S(2)}, u32[]{:S(2)}) async-start(bf16[32,136,128]{2,1,0:T(8,128)(2,1)} %shard_map.65), calls=%async_computation.1 | async-start | bytes 2228224 | tf_op jit(solution)/shard_map/all_to_all | solution.py:208
  42.8 10.9 %copy-start.3 = (s32[32]{0:T(128)S(1)}, s32[32]{0:T(128)}, u32[]{:S(2)}) copy-start(s32[32]{0:T(128)} %get-tuple-element.21.mine_hbm.mine_ref) | copy-start | bytes 388
  44.4 17.0 %collective-permute-start.3 = (bf16[4,32,256]{2,1,0:T(8,128)(2,1)}, bf16[4,32,256]{2,1,0:T(8,128)(2,1)S(1)}, u32[]{:S(2)}, u32[]{:S(2)}) collective-permute-start(bf16[4,32,256]{2,1,0:T(8,128)(2,1)} %get-tuple-element.29), channel_id=1, source_target_pairs={{0,32},{32,0},{64,96},{96,64},{128,160},{160,128},{192,224},{224,1... | collective-permute-start | bytes 196616 | tf_op jit(solution)/shard_map/ppermute | solution.py:215
  47.1 14.3 %collective-permute-start.4 = (bf16[4,32,256]{2,1,0:T(8,128)(2,1)}, bf16[4,32,256]{2,1,0:T(8,128)(2,1)S(1)}, u32[]{:S(2)}, u32[]{:S(2)}) collective-permute-start(bf16[4,32,256]{2,1,0:T(8,128)(2,1)} %get-tuple-element.30), channel_id=1, source_target_pairs={{0,64},{32,96},{64,0},{96,32},{128,192},{160,224},{192,128},{224,1... | collective-permute-start | bytes 196616 | tf_op jit(solution)/shard_map/ppermute | solution.py:215
  51.3 10.2 %collective-permute-start.5 = (bf16[4,32,256]{2,1,0:T(8,128)(2,1)}, bf16[4,32,256]{2,1,0:T(8,128)(2,1)S(1)}, u32[]{:S(2)}, u32[]{:S(2)}) collective-permute-start(bf16[4,32,256]{2,1,0:T(8,128)(2,1)} %get-tuple-element.31), channel_id=1, source_target_pairs={{0,96},{32,64},{64,32},{96,0},{128,224},{160,192},{192,160},{224,1... | collective-permute-start | bytes 196616 | tf_op jit(solution)/shard_map/ppermute | solution.py:215
  61.4 12.9 %copy-start.1 = (bf16[4,32,256]{2,1,0:T(8,128)(2,1)S(1)}, bf16[4,32,256]{2,1,0:T(8,128)(2,1)}, u32[]{:S(2)}) copy-start(bf16[4,32,256]{2,1,0:T(8,128)(2,1)} %get-tuple-element.32.in0_ref) | copy-start | bytes 196612
  61.4 51.4 %all-to-all-start.2 = ((bf16[16,3,32,256]{3,2,1,0:T(8,128)(2,1)}), bf16[16,3,32,256]{3,2,1,0:T(8,128)(2,1)S(1)}, u32[]{:S(2)}, u32[]{:S(2)}) async-start(bf16[16,3,32,256]{3,2,1,0:T(8,128)(2,1)} %shard_map.67), calls=%async_computation.2 | async-start | bytes 1572864 | tf_op jit(solution)/shard_map/all_to_all | solution.py:208
